TPU v7x, 256 devices: a whole 4x4x8 slice. The times are simulated.
256 devices in a mesh: chain: 32 (over x, y, core), col: 8 (over z).
Axes of the slice: x: 4, y: 4, z: 8, core: 2. Of those that a mesh axis runs over, the one named last changes fastest.
Arguments:
- rhs: bfloat16 [64, 64, 2560], P('chain', None, 'col'), may hold values from -6 to 6
- block_inverse: bfloat16 [64, 2560, 2560], P('chain', 'col'), as said below
- entry_factor: bfloat16 [64, 2560, 128], P('chain', 'col'), as said below
- exit_factor: bfloat16 [64, 2560, 128], P('chain', 'col'), as said below
- previous: bfloat16 [64, 2560], P(None, 'col'), may hold values from -6 to 6
Outputs:
- solution: float32 [64, 64, 2560], P('chain', None, 'col')
Inputs may be any that keep to these rules, and one draw needn't show every extreme that they name: Every block of block_inverse equals its own transpose. `entry_factor`: entries are independent, of mean zero. `exit_factor`: entries are independent, of mean zero.
All inputs are finite; a program needn't handle non-finite values.
Results may differ from a plain program's by a relative error of at most 0.0003.
Values may be sent and summed in bfloat16 or wider, within the bound.
No kernel may reach another device: no remote copies, remote signals or barrier semaphores. Data moves between devices by JAX's collectives and lax.ppermute only.
A program may use at most 64 MiB of HBM per device.

v0:
```python
import jax
import jax.numpy as jnp
from jax import lax
from jax.sharding import Mesh
from jax.sharding import PartitionSpec as P

CHAIN = ("chain_0", "chain_1", "chain_2")


def from_behind(block, axis, distance):
    devices = range(lax.axis_size(axis))
    route = [(i - distance, i) for i in devices if i - distance in devices]
    return lax.ppermute(block, axis, route)


def from_everyone(value, axis):
    copies = jnp.broadcast_to(value, (lax.axis_size(axis), *value.shape))
    return lax.all_to_all(copies, axis, split_axis=0, concat_axis=0, tiled=True)


def of_everyone(value, axis):
    return from_everyone(value, axis).sum(axis=0)


def in_one(arrays, axis):
    ends = [0]
    for a in arrays:
        ends.append(ends[-1] + a.size)
    total = of_everyone(jnp.concatenate([a.ravel() for a in arrays]), axis)
    return tuple((total[b:e].reshape(a.shape) for a, b, e in zip(arrays, ends, ends[1:])))


def neutral_like(value, identity):
    return jax.tree.map(
        lambda a, e: jnp.broadcast_to(jnp.asarray(e, a.dtype), a.shape), value, identity
    )


def prefix_by_axis(value, axes, combine, identity, reverse):
    before = start = neutral_like(value, identity)
    total = value
    for axis in reversed(axes):
        devices, position = (lax.axis_size(axis), lax.axis_index(axis))
        pieces = jax.tree.map(lambda part: lax.all_gather(part, axis), total)
        inside, total = (start, start)
        for k in reversed(range(devices)) if reverse else range(devices):
            passed = k > position if reverse else k < position
            total = combine(total, jax.tree.map(lambda part: part[k], pieces))
            inside = jax.tree.map(lambda new, old: jnp.where(passed, new, old), total, inside)
        before = combine(inside, before)
    return before


def joined_along(parts, dim):
    lengths = list(parts.shape[1:])
    lengths[dim] *= parts.shape[0]
    return jnp.moveaxis(parts, 0, dim).reshape(lengths)


def gather_directly(value, axis, dim):
    parts = from_everyone(value, axis)
    return joined_along(parts, dim)


def compose(earlier, later):
    exact = lax.Precision.HIGHEST
    first_map, first_shift = earlier
    second_map, second_shift = later
    return (
        jnp.dot(first_map, second_map, precision=exact),
        jnp.dot(first_shift, second_map, precision=exact) + second_shift,
    )


def shards(rhs, block_inverse, entry_factor, exit_factor, previous):
    exact = lax.Precision.HIGHEST
    intervals_here = rhs.shape[0]
    column_count = rhs.shape[1]
    state_width = entry_factor.shape[2]
    arriving = from_behind(exit_factor[:1], CHAIN, -1)
    following = jnp.concatenate([exit_factor[1:], arriving], axis=0)
    couple_part = -jnp.einsum(
        "irn,irm->inm", entry_factor, following, preferred_element_type=jnp.float32
    )
    source_part = jnp.einsum("icr,irm->icm", rhs, following, preferred_element_type=jnp.float32)
    opening_part = jnp.dot(previous, exit_factor[0], preferred_element_type=jnp.float32)
    couple, source, opening = in_one((couple_part, source_part, opening_part), "col")
    identity = jnp.eye(state_width, dtype=jnp.float32)
    empty_shift = jnp.zeros((column_count, state_width), jnp.float32)
    first_chain = lax.axis_index(CHAIN) == 0
    matrix = identity
    offset = empty_shift
    for position in range(intervals_here):
        matrix = jnp.dot(matrix, couple[position], precision=exact)
        offset = jnp.dot(offset, couple[position], precision=exact) + source[position]
    folded = jnp.dot(opening, matrix, precision=exact) + offset
    offset = jnp.where(first_chain, folded, offset)
    matrix = jnp.where(first_chain, jnp.zeros_like(matrix), matrix)
    _, incoming = prefix_by_axis((matrix, offset), CHAIN, compose, (identity, empty_shift), False)
    carry_state = jnp.where(first_chain, opening, incoming)
    solved_list = []
    for position in range(intervals_here):
        solved_list.append(
            rhs[position].astype(jnp.float32)
            - jnp.dot(carry_state, entry_factor[position].astype(jnp.float32).T, precision=exact)
        )
        carry_state = jnp.dot(carry_state, couple[position], precision=exact) + source[position]
    forward = jnp.stack(solved_list).astype(jnp.bfloat16)
    applied = jnp.einsum(
        "icb,irb->icr",
        gather_directly(forward, "col", 2),
        block_inverse,
        preferred_element_type=jnp.float32,
    )
    carried_part = jnp.einsum(
        "icr,irn->icn",
        applied.astype(jnp.bfloat16),
        entry_factor,
        preferred_element_type=jnp.float32,
    )
    carried = of_everyone(carried_part, "col")
    last_chain = lax.axis_index(CHAIN) == lax.axis_size(CHAIN) - 1
    matrix = identity
    offset = empty_shift
    for position in reversed(range(intervals_here)):
        turned = couple[position].T
        matrix = jnp.dot(matrix, turned, precision=exact)
        offset = jnp.dot(offset, turned, precision=exact) + carried[position]
    matrix = jnp.where(last_chain, jnp.zeros_like(matrix), matrix)
    _, behind = prefix_by_axis((matrix, offset), CHAIN, compose, (identity, empty_shift), True)
    results = [None] * intervals_here
    for position in reversed(range(intervals_here)):
        results[position] = applied[position] - jnp.dot(
            behind, following[position].astype(jnp.float32).T, precision=exact
        )
        behind = jnp.dot(behind, couple[position].T, precision=exact) + carried[position]
    return jnp.stack(results)


def solution(mesh):
    torus = Mesh(
        mesh.devices.reshape(4, 4, 2, mesh.shape["col"]), ("chain_0", "chain_1", "chain_2", "col")
    )
    return jax.shard_map(
        shards,
        mesh=torus,
        in_specs=(
            P(CHAIN, None, "col"),
            P(CHAIN, "col", None),
            P(CHAIN, "col", None),
            P(CHAIN, "col", None),
            P(None, "col"),
        ),
        out_specs=P(CHAIN, None, "col"),
        check_vma=False,
    )
```

profile of v0, /device:TPU:32, one launch (start us, length us, event | category | flops | bytes accessed | tf_op | source)
XLA Modules:
  0.0 234.8 jit_solution(9002553044777800805)
XLA Ops:
  0.0 1.1 fusion.152
  1.1 1.3 collective-permute-start
  2.4 1.1 convolution_bitcast_fusion
  4.9 1.2 fusion
  6.8 1.1 fusion.13
  8.9 2.2 broadcast_in_dim.12
  11.0 8.6 %all-to-all-start = ((f32[8,1,57344]{2,1,0:T(1,128)}), f32[8,1,57344]{2,1,0:T(1,128)}, u32[]{:S(2)}, u32[]{:S(2)}) async-start(f32[8,1,57344]{2,1,0:T(1,128)} %broadcast_in_dim.12), calls=%async_computation | async-start | bytes 3670016 | tf_op jit(solution)/shard_map/all_to_all | solution.py:18
  19.6 44.3 %all-to-all-done = f32[8,1,57344]{2,1,0:T(1,128)} async-done(((f32[8,1,57344]{2,1,0:T(1,128)}), f32[8,1,57344]{2,1,0:T(1,128)}, u32[]{:S(2)}, u32[]{:S(2)}) %all-to-all-start) | async-done | bytes 1835040 | tf_op jit(solution)/shard_map/all_to_all | solution.py:18
  63.9 2.8 %reduce_sum.18 = f32[57344]{0:T(1024)S(1)} reduce(f32[8,1,57344]{2,1,0:T(1,128)} %all-to-all-done, f32[]{:T(128)} %constant.10.clone.1), dimensions={0,1}, to_apply=%region_0.0 | reduce | flops 401408 | bytes 2064388 | tf_op jit(solution)/shard_map/reduce_sum | solution.py:22
  68.2 2.7 %all-gather = f32[256,128]{1,0:T(8,128)S(1)} all-gather(f32[128,128]{1,0:T(8,128)S(1)} %get-tuple-element.7), channel_id=2, replica_groups=mesh['chain_0'=4,'chain_1'=4,'chain_2'=2,'col'=8] {'chain_2'}, dimensions={0}, use_global_device_ids=true | all-gather | bytes 196608 | tf_op jit(solution)/shard_map/all_gather | solution.py:44
  71.3 13.8 %all-gather.1 = f32[512,128]{1,0:T(8,128)S(1)} all-gather(f32[128,128]{1,0:T(8,128)S(1)} %fusion.80), channel_id=3, replica_groups=mesh['chain_0'=4,'chain_1'=4,'chain_2'=2,'col'=8] {'chain_1'}, dimensions={0}, use_global_device_ids=true | all-gather | bytes 327680 | tf_op jit(solution)/shard_map/all_gather | solution.py:44
  85.9 12.9 %all-gather.2 = f32[512,128]{1,0:T(8,128)S(1)} all-gather(f32[128,128]{1,0:T(8,128)S(1)} %fusion.69), channel_id=4, replica_groups=mesh['chain_0'=4,'chain_1'=4,'chain_2'=2,'col'=8] {'chain_0'}, dimensions={0}, use_global_device_ids=true | all-gather | bytes 327680 | tf_op jit(solution)/shard_map/all_gather | solution.py:44
  99.2 1.9 all-gather.3
  101.5 12.0 %all-gather.4 = f32[256,128]{1,0:T(8,128)S(1)} all-gather(f32[64,128]{1,0:T(8,128)S(1)} %convolution_add_fusion.22), channel_id=6, replica_groups=mesh['chain_0'=4,'chain_1'=4,'chain_2'=2,'col'=8] {'chain_1'}, dimensions={0}, use_global_device_ids=true | all-gather | bytes 163840 | tf_op jit(solution)/shard_map/all_gather | solution.py:44
  114.2 12.0 %all-gather.5 = f32[256,128]{1,0:T(8,128)S(1)} all-gather(f32[64,128]{1,0:T(8,128)S(1)} %convolution_add_fusion.19), channel_id=7, replica_groups=mesh['chain_0'=4,'chain_1'=4,'chain_2'=2,'col'=8] {'chain_0'}, dimensions={0}, use_global_device_ids=true | all-gather | bytes 163840 | tf_op jit(solution)/shard_map/all_gather | solution.py:44
  129.7 5.7 %all-to-all-start.1 = ((bf16[8,2,64,320]{3,2,1,0:T(8,128)(2,1)}), bf16[8,2,64,320]{3,2,1,0:T(8,128)(2,1)}, u32[]{:S(2)}, u32[]{:S(2)}) async-start(bf16[8,2,64,320]{3,2,1,0:T(8,128)(2,1)} %broadcast_in_dim.14), calls=%async_computation.1 | async-start | bytes 1572864 | tf_op jit(solution)/shard_map/all_to_all | solution.py:18
  135.3 1.1 convolution_select_fusion
  136.4 1.9 all-gather.6
  140.4 12.2 %all-gather.7 = f32[512,128]{1,0:T(8,128)S(1)} all-gather(f32[128,128]{1,0:T(8,128)S(1)} %fusion.64), channel_id=9, replica_groups=mesh['chain_0'=4,'chain_1'=4,'chain_2'=2,'col'=8] {'chain_1'}, dimensions={0}, use_global_device_ids=true | all-gather | bytes 327680 | tf_op jit(solution)/shard_map/all_gather | solution.py:44
  154.8 2.5 %copy.13 = bf16[2,64,8,320]{3,2,1,0:T(8,128)(2,1)} copy(bf16[2,64,8,320]{3,1,0,2:T(8,128)(2,1)} %bitcast.17) | data formatting | bytes 1310720 | tf_op jit(solution)/shard_map/transpose | solution.py:57
  157.3 2.3 reshape.76
  159.7 2.1 fusion.154
  163.5 7.2 %all-to-all-start.2 = ((f32[8,2,64,128]{3,2,1,0:T(8,128)}), f32[8,2,64,128]{3,2,1,0:T(8,128)}, u32[]{:S(2)}, u32[]{:S(2)}) async-start(f32[8,2,64,128]{3,2,1,0:T(8,128)} %broadcast_in_dim.15), calls=%async_computation.2 | async-start | bytes 1048576 | tf_op jit(solution)/shard_map/all_to_all | solution.py:18
  170.7 1.1 fusion.56
  171.8 1.0 fusion.53
  172.9 13.3 %all-gather.8 = f32[512,128]{1,0:T(8,128)} all-gather(f32[128,128]{1,0:T(8,128)S(1)} %fusion.53), channel_id=10, replica_groups=mesh['chain_0'=4,'chain_1'=4,'chain_2'=2,'col'=8] {'chain_0'}, dimensions={0}, use_global_device_ids=true | all-gather | bytes 327680 | tf_op jit(solution)/shard_map/all_gather | solution.py:44
  187.8 1.7 fusion.34
  189.5 1.7 reduce_sum.19
  193.3 1.9 all-gather.9
  197.2 12.0 %all-gather.10 = f32[256,128]{1,0:T(8,128)S(1)} all-gather(f32[64,128]{1,0:T(8,128)S(1)} %convolution_add_fusion.8), channel_id=12, replica_groups=mesh['chain_0'=4,'chain_1'=4,'chain_2'=2,'col'=8] {'chain_1'}, dimensions={0}, use_global_device_ids=true | all-gather | bytes 163840 | tf_op jit(solution)/shard_map/all_gather | solution.py:44
  213.3 12.0 %all-gather.11 = f32[256,128]{1,0:T(8,128)S(1)} all-gather(f32[64,128]{1,0:T(8,128)S(1)} %convolution_add_fusion.5), channel_id=13, replica_groups=mesh['chain_0'=4,'chain_1'=4,'chain_2'=2,'col'=8] {'chain_0'}, dimensions={0}, use_global_device_ids=true | all-gather | bytes 163840 | tf_op jit(solution)/shard_map/all_gather | solution.py:44
  232.7 1.2 fusion.2
  (90 shorter events, 34.5 us)
Async XLA Ops:
  0.0 159.7 %copy-start = (bf16[2,320,2560]{2,1,0:T(8,128)(2,1)S(1)}, bf16[2,320,2560]{2,1,0:T(8,128)(2,1)}, u32[]{:S(2)}) copy-start(bf16[2,320,2560]{2,1,0:T(8,128)(2,1)} %param.6) | copy-start | bytes 9830404
  1.1 3.2 %collective-permute-start = (bf16[1,320,128]{2,1,0:T(8,128)(2,1)S(1)}, bf16[1,320,128]{2,1,0:T(8,128)(2,1)S(1)}, u32[]{:S(2)}, u32[]{:S(2)}) collective-permute-start(bf16[1,320,128]{2,1,0:T(8,128)(2,1)S(1)} %get-tuple-element.6), channel_id=1, source_target_pairs={{8,0},{16,8},{24,16},{32,24},{40,32},{48,40},{56,48},{64,56},{72,6... | collective-permute-start | bytes 245768 | tf_op jit(solution)/shard_map/ppermute | solution.py:13
  4.3 0.6 copy-start.11
  11.0 52.9 %all-to-all-start = ((f32[8,1,57344]{2,1,0:T(1,128)}), f32[8,1,57344]{2,1,0:T(1,128)}, u32[]{:S(2)}, u32[]{:S(2)}) async-start(f32[8,1,57344]{2,1,0:T(1,128)} %broadcast_in_dim.12), calls=%async_computation | async-start | bytes 3670016 | tf_op jit(solution)/shard_map/all_to_all | solution.py:18
  66.8 61.4 %copy-start.4 = (bf16[2,320,128]{2,1,0:T(8,128)(2,1)S(1)}, bf16[2,320,128]{2,1,0:T(8,128)(2,1)}, u32[]{:S(2)}) copy-start(bf16[2,320,128]{2,1,0:T(8,128)(2,1)} %param.7) | copy-start | bytes 491524
  66.8 61.4 %copy-start.13 = (bf16[2,64,320]{2,1,0:T(8,128)(2,1)S(1)}, bf16[2,64,320]{2,1,0:T(8,128)(2,1)}, u32[]{:S(2)}) copy-start(bf16[2,64,320]{2,1,0:T(8,128)(2,1)} %param.5) | copy-start | bytes 245764
  129.7 25.2 %all-to-all-start.1 = ((bf16[8,2,64,320]{3,2,1,0:T(8,128)(2,1)}), bf16[8,2,64,320]{3,2,1,0:T(8,128)(2,1)}, u32[]{:S(2)}, u32[]{:S(2)}) async-start(bf16[8,2,64,320]{3,2,1,0:T(8,128)(2,1)} %broadcast_in_dim.14), calls=%async_computation.1 | async-start | bytes 1572864 | tf_op jit(solution)/shard_map/all_to_all | solution.py:18
  138.3 0.7 copy-start.6
  139.0 0.6 copy-start.8
  139.8 0.6 copy-start.7
  152.7 0.7 copy-start.1
  153.4 0.6 copy-start.10
  159.7 2.8 %copy-start.5 = (bf16[2,320,128]{2,1,0:T(8,128)(2,1)S(1)}, bf16[2,320,128]{2,1,0:T(8,128)(2,1)}, u32[]{:S(2)}) copy-start(bf16[2,320,128]{2,1,0:T(8,128)(2,1)} %param.7) | copy-start | bytes 491524
  161.8 0.7 copy-start.2
  163.5 26.0 %all-to-all-start.2 = ((f32[8,2,64,128]{3,2,1,0:T(8,128)}), f32[8,2,64,128]{3,2,1,0:T(8,128)}, u32[]{:S(2)}, u32[]{:S(2)}) async-start(f32[8,2,64,128]{3,2,1,0:T(8,128)} %broadcast_in_dim.15), calls=%async_computation.2 | async-start | bytes 1048576 | tf_op jit(solution)/shard_map/all_to_all | solution.py:18
  187.2 0.6 copy-start.9
  191.2 42.6 %copy-start.3 = (f32[2,64,320]{2,1,0:T(8,128)S(1)}, f32[2,64,320]{2,1,0:T(8,128)}, u32[]{:S(2)}) copy-start(f32[2,64,320]{2,1,0:T(8,128)} %copy-done.2) | copy-start | bytes 491524
  191.2 42.6 %copy-start.12 = (bf16[1,320,128]{2,1,0:T(8,128)(2,1)S(1)}, bf16[1,320,128]{2,1,0:T(8,128)(2,1)}, u32[]{:S(2)}) copy-start(bf16[1,320,128]{2,1,0:T(8,128)(2,1)} %copy-done.11) | copy-start | bytes 245764
where the time goes:
time: 236 us; the launch traced here: 235 us
  blocking collectives  109 us (46%)
  waiting for transfers between devices  45.1 us (19%)
  matrix products  36.2 us (15%)
  starting transfers between devices  22.7 us (10%)
  local copies, waits for them, and re-layouts  15.5 us (7%)
  other arithmetic  6.17 us (3%)
    all_gather x12, blocking collectives, prefix_by_axis(): pieces = jax.tree.map(lambda part: lax.all_gather(part, axis), total)  109 us
    all_to_all x3, waiting for transfers between devices, from_everyone(): return lax.all_to_all(copies, axis, split_axis=0, concat_axis=0, tiled=True)  44.3 us
    all_to_all x3, starting transfers between devices, from_everyone(): return lax.all_to_all(copies, axis, split_axis=0, concat_axis=0, tiled=True)  21.4 us
    dot_general x26, matrix products, compose(): jnp.dot(first_shift, second_map, precision=exact) + second_shift  14.9 us
    dot_general x16, matrix products, compose(): jnp.dot(first_map, second_map, precision=exact)  7.78 us
    unnamed x28, local copies, waits for them, and re-layouts  4.78 us
  transfers between devices with their start and end apart: 4, of which 2 were waited for; matrix products, arithmetic and copies ran while one was open for 4% of the time, Pallas kernels for 0%

commit v1 on v0

v1 whole, which is shorter than its diff:
```python
import jax
import jax.numpy as jnp
from jax import lax
from jax.experimental import pallas as pl
from jax.experimental.pallas import tpu as pltpu
from jax.sharding import Mesh
from jax.sharding import PartitionSpec as P

X, Y, CORE, COL = "chain_0", "chain_1", "chain_2", "col"
CHAIN = (X, Y, CORE)
F32 = jnp.float32
BF16 = jnp.bfloat16

NN = (((1,), (0,)), ((), ()))
NT = (((1,), (1,)), ((), ()))
TN = (((0,), (0,)), ((), ()))


def dot16(a, b, dims):
    return lax.dot_general(a, b, dims, preferred_element_type=F32)


def dot32(a, b, dims):
    return lax.dot_general(a, b, dims, precision=lax.Precision.HIGHEST, preferred_element_type=F32)


def dot32_16(a, b, dims):
    high = a.astype(BF16)
    rest = a - high.astype(F32)
    middle = rest.astype(BF16)
    low = (rest - middle.astype(F32)).astype(BF16)
    rows = a.shape[0]
    out = dot16(jnp.concatenate([high, middle, low], axis=0), b, dims)
    return (out[2 * rows :] + out[rows : 2 * rows]) + out[:rows]


def vmem():
    return pl.BlockSpec(memory_space=pltpu.VMEM)


def smem():
    return pl.BlockSpec(memory_space=pltpu.SMEM)


def call(kernel, place, arrays, outs, scratch=()):
    return pl.pallas_call(
        kernel,
        out_shape=outs,
        in_specs=[smem()] + [vmem()] * len(arrays),
        out_specs=jax.tree.map(lambda _: vmem(), outs),
        scratch_shapes=list(scratch),
        compiler_params=pltpu.CompilerParams(vmem_limit_bytes=40 * 1024 * 1024),
    )(place, *arrays)


def of(shape, dtype=F32):
    return jax.ShapeDtypeStruct(shape, dtype)


def partial_kernel(place, entry, exit_, arriving, rhs, previous, out):
    groups = out.shape[0]

    def put(start, rows, value):
        out[:, start : start + rows, :] = value.reshape(groups, rows, value.shape[1])

    n = entry.shape[2] // groups
    c = rhs.shape[1] // groups
    put(0, n, -dot16(entry[0], exit_[1], TN))
    put(n, n, -dot16(entry[1], arriving[0], TN))
    put(2 * n, c, dot16(rhs[0], exit_[1], NN))
    put(2 * n + c, c, dot16(rhs[1], arriving[0], NN))
    put(2 * n + 2 * c, c, dot16(previous[...], exit_[0], NN))


def sum_kernel(place, parts, out):
    total = parts[0]
    for k in range(1, parts.shape[0]):
        total = total + parts[k]
    for k in range(parts.shape[0]):
        out[k] = total


def pieces(whole):
    groups, rows, width = whole.shape
    n = width // groups
    c = (rows - 2 * n) // 3

    def take(start, count):
        return whole[:, start : start + count, :].reshape(groups * count, width)

    return take(0, n), take(n, n), take(2 * n, c), take(2 * n + c, c), take(2 * n + 2 * c, c)


def is_first(place):
    return (place[0] == 0) & (place[1] == 0) & (place[2] == 0)


def after(earlier, later, n):
    out = dot32(earlier, later[:n], NN)
    return out[:n], out[n:] + later[n:]


def local_kernel(place, whole, out):
    couple0, couple1, source0, source1, opening = pieces(whole)
    n = couple0.shape[0]
    folded = dot32(opening, couple0, NN) + source0
    source0 = jnp.where(is_first(place), folded, source0)
    out[:n] = dot32(couple0, couple1, NN)
    out[n:] = dot32(source0, couple1, NN) + source1


def pair_kernel(place, mine, other, out, before):
    n = mine.shape[1]
    upper = place[2] == 1
    first = jnp.where(upper, other[...], mine[...])
    second = jnp.where(upper, mine[...], other[...])
    out[:n], out[n:] = after(first, second, n)
    before[...] = other[...]


def group_kernel(place, mine, one, two, three, total, before, slots):
    n = mine.shape[1]
    y = place[1]
    for d, ref in enumerate((mine, one, two, three)):
        slots[lax.rem(y - d + 4, 4)] = ref[...]
    rows = lax.broadcasted_iota(jnp.int32, mine.shape, 0)
    lanes = lax.broadcasted_iota(jnp.int32, mine.shape, 1)
    before[...] = jnp.where(rows == lanes, 1.0, 0.0).astype(F32)
    total[...] = slots[0]
    for q in range(1, 4):

        @pl.when(y == q)
        def _():
            before[...] = total[...]

        top, bottom = after(total[...], slots[q], n)
        total[:n] = top
        total[n:] = bottom


def forward_kernel(place, whole, core_other, before, one, two, three, entry, rhs, out):
    couple0, _, source0, _, opening = pieces(whole)
    n = couple0.shape[0]
    x = place[0]
    state = jnp.zeros(opening.shape, F32)
    for d, ref in ((3, three), (2, two), (1, one)):
        state = jnp.where(d <= x, dot32(state, ref[:n], NN) + ref[n:], state)
    state = dot32(state, before[:n], NN) + before[n:]
    state = jnp.where(place[2] == 1, dot32(state, core_other[:n], NN) + core_other[n:], state)
    state = jnp.where(is_first(place), opening, state)
    out[0] = (rhs[0].astype(F32) - dot32_16(state, entry[0], NT)).astype(BF16)
    state = dot32(state, couple0, NN) + source0
    out[1] = (rhs[1].astype(F32) - dot32_16(state, entry[1], NT)).astype(BF16)


def apply_kernel(place, forward, inverse, entry, applied, carried):
    groups = forward.shape[0]
    for i in range(forward.shape[1]):
        whole = jnp.concatenate([forward[g, i] for g in range(groups)], axis=1)
        value = dot16(whole, inverse[i], NT)
        applied[i] = value
        part = dot16(value.astype(BF16), entry[i], NN)
        c = part.shape[0] // groups
        carried[:, i * c : (i + 1) * c, :] = part.reshape(groups, c, part.shape[1])


def back_kernel(place, parts, whole, core_other, before, carried, send):
    couple0 = pieces(whole)[0]
    n = couple0.shape[0]
    c = parts.shape[1] // 2
    total = parts[0]
    for k in range(1, parts.shape[0]):
        total = total + parts[k]
    carried[...] = total
    x, y, core = place[0], place[1], place[2]
    own = dot32(total[c:], couple0, NT) + total[:c]
    chip = jnp.where(core == 1, dot32(own, core_other[:n], NT), own)
    group = dot32(chip, before[:n], NT)
    for k in range(send.shape[0]):
        same_x = x == k // 8
        same_y = y == (k // 2) % 4
        value = jnp.where(same_x, jnp.where(same_y, own, chip), group)
        send[k] = value


def behind_kernel(place, got, carried, whole, core_other, y1, y2, y3, x1, x2, x3, out):
    _, couple1, _, _, _ = pieces(whole)
    n = couple1.shape[0]
    c = carried.shape[0] // 2
    x, y, core = place[0], place[1], place[2]
    state = jnp.zeros((c, n), F32)
    for e, ref in ((3, x1), (2, x2), (1, x3)):
        base = lax.rem(x + e, 4) * 8
        extra = got[base]
        for k in range(1, 8):
            extra = extra + got[base + k]
        state = jnp.where(x + e <= 3, dot32(state, ref[:n], NT) + extra, state)
    for e, ref in ((3, y1), (2, y2), (1, y3)):
        base = x * 8 + lax.rem(y + e, 4) * 2
        extra = got[base] + got[base + 1]
        state = jnp.where(y + e <= 3, dot32(state, ref[:n], NT) + extra, state)
    extra = got[x * 8 + y * 2 + 1]
    state = jnp.where(core == 0, dot32(state, core_other[:n], NT) + extra, state)
    inner = dot32(state, couple1, NT) + carried[c:]
    for k in range(out.shape[0]):
        out[k, :c] = inner
        out[k, c:] = state


def final_kernel(place, got, applied, exit_, arriving, out):
    groups, rows, width = got.shape
    c = rows // 2
    inner = got[:, :c, :].reshape(groups * c, width)
    outer = got[:, c:, :].reshape(groups * c, width)
    out[0] = applied[0] - dot32_16(inner, exit_[1], NT)
    out[1] = applied[1] - dot32_16(outer, arriving[0], NT)


def exchange(value, axes):
    return lax.all_to_all(value, axes, split_axis=0, concat_axis=0, tiled=True)


def ring(value, axis):
    size = lax.axis_size(axis)
    return [
        lax.ppermute(value, axis, [(i, (i + d) % size) for i in range(size)])
        for d in range(1, size)
    ]


def shards(rhs, block_inverse, entry, exit_, previous):
    z = lax.axis_size(COL)
    here, cols, local = rhs.shape
    n = entry.shape[2]
    place = jnp.stack([lax.axis_index(X), lax.axis_index(Y), lax.axis_index(CORE)]).astype(jnp.int32)
    chain = lax.axis_size(CHAIN)
    arriving = lax.ppermute(exit_[:1], CHAIN, [(i, i - 1) for i in range(1, chain)])
    rows = (2 * n + 3 * cols) // z
    parts = call(partial_kernel, place, (entry, exit_, arriving, rhs, previous), of((z, rows, n)))
    summed = call(sum_kernel, place, (exchange(parts, COL),), of((z, rows, n)))
    whole = exchange(summed, COL)
    maps = of((n + cols, n))
    mine = call(local_kernel, place, (whole,), maps)
    other = lax.ppermute(mine, CORE, [(0, 1), (1, 0)])
    chip, core_other = call(pair_kernel, place, (mine, other), (maps, maps))
    y1, y2, y3 = ring(chip, Y)
    group, before = call(
        group_kernel, place, (chip, y1, y2, y3), (maps, maps), [pltpu.VMEM((4, n + cols, n), F32)]
    )
    x1, x2, x3 = ring(group, X)
    forward = call(
        forward_kernel,
        place,
        (whole, core_other, before, x1, x2, x3, entry, rhs),
        of((here, cols, local), BF16),
    )
    gathered = exchange(jnp.broadcast_to(forward, (z, *forward.shape)), COL)
    c = cols // z
    applied, carried_parts = call(
        apply_kernel,
        place,
        (gathered, block_inverse, entry),
        (of((here, cols, local)), of((z, 2 * c, n))),
    )
    carried, send = call(
        back_kernel,
        place,
        (exchange(carried_parts, COL), whole, core_other, before),
        (of((2 * c, n)), of((chain, c, n))),
    )
    behind = call(
        behind_kernel,
        place,
        (exchange(send, CHAIN), carried, whole, core_other, y1, y2, y3, x1, x2, x3),
        of((z, 2 * c, n)),
    )
    return call(
        final_kernel,
        place,
        (exchange(behind, COL), applied, exit_, arriving),
        of((here, cols, local)),
    )


def solution(mesh):
    torus = Mesh(mesh.devices.reshape(4, 4, 2, mesh.shape["col"]), (X, Y, CORE, COL))
    return jax.shard_map(
        shards,
        mesh=torus,
        in_specs=(
            P(CHAIN, None, COL),
            P(CHAIN, COL, None),
            P(CHAIN, COL, None),
            P(CHAIN, COL, None),
            P(None, COL),
        ),
        out_specs=P(CHAIN, None, COL),
        check_vma=False,
    )
```

time: 236 us -> 139 us (0.59)
  matrix products: 36.2 us -> 0 us
  waiting for transfers between devices: 45.1 us -> 13.2 us
  blocking collectives: 109 us -> 92.4 us
  Pallas kernels: 0 us -> 14.5 us
  starting transfers between devices: 22.7 us -> 11.8 us
  local copies, waits for them, and re-layouts: 15.5 us -> 5.45 us
  other arithmetic: 6.17 us -> 0.08 us
    all_gather x12 -> x0, blocking collectives: 109 us -> none  [prefix_by_axis(): pieces = jax.tree.map(lambda part: lax.all_gather(part, axis), total)]
    all_to_all x0 -> x6, blocking collectives: none -> 92.4 us  [exchange(): return lax.all_to_all(value, axes, split_axis=0, concat_axis=0, tiled=True)]
    all_to_all x3 -> x0, waiting for transfers between devices: 44.3 us -> none  [from_everyone(): return lax.all_to_all(copies, axis, split_axis=0, concat_axis=0, tiled=True)]
    dot_general x62 -> x0, matrix products: 36.2 us -> none  [the longest x26 14.9 us: compose(): jnp.dot(first_shift, second_map, precision=exact) + second_shift]
    all_to_all x3 -> x0, starting transfers between devices: 21.4 us -> none  [from_everyone(): return lax.all_to_all(copies, axis, split_axis=0, concat_axis=0, tiled=True)]
    pallas_call x0 -> x10, Pallas kernels: none -> 14.5 us  [call(): pl.pallas_call(kernel, out_shape=outs, in_specs=[smem()] + [vmem()] * len...]
    ppermute x1 -> x8, waiting for transfers between devices: 0.8 us -> 13.2 us  [the longest x6 10.2 us: ring(): lax.ppermute(value, axis, [(i, (i + d) % size) for i in range(size)])]
    ppermute x1 -> x8, starting transfers between devices: 1.29 us -> 11.8 us  [the longest x6 10.3 us: ring(): lax.ppermute(value, axis, [(i, (i + d) % size) for i in range(size)])]
  transfers between devices with their start and end apart: 4 -> 8, of which waited for: 2 -> 7; matrix products, arithmetic and copies ran while one was open for 4% -> 0% of each run, Pallas kernels for 0% -> 0%
where the time goes in v1:
time: 139 us; the launch traced here: 137 us
  blocking collectives  92.4 us (66%)
  Pallas kernels  14.5 us (10%)
  waiting for transfers between devices  13.2 us (9%)
  starting transfers between devices  11.8 us (8%)
  local copies, waits for them, and re-layouts  5.45 us (4%)
    all_to_all x6, blocking collectives, exchange(): return lax.all_to_all(value, axes, split_axis=0, concat_axis=0, tiled=True)  92.4 us
    pallas_call x10, Pallas kernels, call(): pl.pallas_call(kernel, out_shape=outs, in_specs=[smem()] + [vmem()] * len...  14.5 us
    ppermute x6, starting transfers between devices, ring(): lax.ppermute(value, axis, [(i, (i + d) % size) for i in range(size)])  10.3 us
    ppermute x6, waiting for transfers between devices, ring(): lax.ppermute(value, axis, [(i, (i + d) % size) for i in range(size)])  10.2 us
    unnamed x16, local copies, waits for them, and re-layouts  4.43 us
  transfers between devices with their start and end apart: 8, of which 7 were waited for; matrix products, arithmetic and copies ran while one was open for 0% of the time, Pallas kernels for 0%

profile of v1, /device:TPU:32, one launch (start us, length us, event | category | flops | bytes accessed | tf_op | source)
XLA Modules:
  0.0 137.4 jit_solution(4091482762449135656)
XLA Ops:
  0.0 0.9 slice.3
  0.9 1.3 collective-permute-start
  2.3 1.8 %collective-permute-done.arriving = bf16[1,320,128]{2,1,0:T(8,128)(2,1)S(1)} collective-permute-done((bf16[1,320,128]{2,1,0:T(8,128)(2,1)S(1)}, bf16[1,320,128]{2,1,0:T(8,128)(2,1)S(1)}, u32[]{:S(2)}, u32[]{:S(2)}) %collective-permute-start) | collective-permute-done | bytes 81952 | tf_op jit(solution)/shard_map/ppermute | solution.py:237
  4.1 0.9 copy-done.1
  5.0 0.9 copy-done.3
  5.9 0.9 copy-done.5
  8.5 17.0 %all_to_all.30.parts = f32[8,56,128]{2,1,0:T(8,128)S(1)} all-to-all(f32[8,56,128]{2,1,0:T(8,128)S(1)} %shard_map.55), channel_id=1, replica_groups=mesh['chain_0'=4,'chain_1'=4,'chain_2'=2,'col'=8] {'col'}, dimensions={0} | all-to-all | bytes 458752 | tf_op jit(solution)/shard_map/all_to_all | solution.py:220
  26.0 16.3 %all_to_all.31.whole = f32[8,56,128]{2,1,0:T(8,128)S(1)} all-to-all(f32[8,56,128]{2,1,0:T(8,128)S(1)} %shard_map.56), channel_id=1, replica_groups=mesh['chain_0'=4,'chain_1'=4,'chain_2'=2,'col'=8] {'col'}, dimensions={0} | all-to-all | bytes 458752 | tf_op jit(solution)/shard_map/all_to_all | solution.py:220
  42.3 0.9 shard_map.57.mine
  43.4 1.2 collective-permute-done.1.other
  45.4 2.6 %collective-permute-start.4 = (f32[192,128]{1,0:T(8,128)S(1)}, f32[192,128]{1,0:T(8,128)S(1)}, u32[]{:S(2)}, u32[]{:S(2)}) collective-permute-start(f32[192,128]{1,0:T(8,128)S(1)} %get-tuple-element.14.mine), channel_id=1, source_target_pairs={{0,48},{16,0},{32,16},{48,32},{1,49},{17,1},{33,17},{49,33},{2,50}... | collective-permute-start | bytes 294920 | tf_op jit(solution)/shard_map/ppermute | solution.py:226
  48.0 2.1 %collective-permute-start.3 = (f32[192,128]{1,0:T(8,128)S(1)}, f32[192,128]{1,0:T(8,128)S(1)}, u32[]{:S(2)}, u32[]{:S(2)}) collective-permute-start(f32[192,128]{1,0:T(8,128)S(1)} %get-tuple-element.14.mine), channel_id=1, source_target_pairs={{0,32},{16,48},{32,0},{48,16},{1,33},{17,49},{33,1},{49,17},{2,34}... | collective-permute-start | bytes 294920 | tf_op jit(solution)/shard_map/ppermute | solution.py:226
  50.0 1.1 collective-permute-start.2
  51.1 4.0 %collective-permute-done.3.two.y2 = f32[192,128]{1,0:T(8,128)S(1)} collective-permute-done((f32[192,128]{1,0:T(8,128)S(1)}, f32[192,128]{1,0:T(8,128)S(1)}, u32[]{:S(2)}, u32[]{:S(2)}) %collective-permute-start.3) | collective-permute-done | bytes 98336 | tf_op jit(solution)/shard_map/ppermute | solution.py:226
  55.1 1.3 collective-permute-done.2.one.y1
  56.4 1.4 %shard_map.59 = (f32[192,128]{1,0:T(8,128)S(1)}, f32[192,128]{1,0:T(8,128)S(1)}) custom-call(s32[3]{0:T(128)S(1)} %pad_add_fusion.place, f32[192,128]{1,0:T(8,128)S(1)} %get-tuple-element.14.mine, f32[192,128]{1,0:T(8,128)S(1)} %collective-permute-done.2.one.y1, f32[192,128]{1,0:T(8,128)S(1)} %collective-permute-done.3.two.y2, ...), custom_call_target="tpu_custom_call" | custom-call | tf_op jit(solution)/shard_map/pallas_call | solution.py:46
  57.8 2.3 %collective-permute-start.7 = (f32[192,128]{1,0:T(8,128)S(1)}, f32[192,128]{1,0:T(8,128)S(1)}, u32[]{:S(2)}, u32[]{:S(2)}) collective-permute-start(f32[192,128]{1,0:T(8,128)S(1)} %get-tuple-element.16), channel_id=1, source_target_pairs={{0,192},{64,0},{128,64},{192,128},{1,193},{65,1},{129,65},{193,129... | collective-permute-start | bytes 294920 | tf_op jit(solution)/shard_map/ppermute | solution.py:226
  60.1 1.3 collective-permute-start.6
  61.5 0.9 collective-permute-start.5
  62.3 1.9 %collective-permute-done.7.three.x3 = f32[192,128]{1,0:T(8,128)S(1)} collective-permute-done((f32[192,128]{1,0:T(8,128)S(1)}, f32[192,128]{1,0:T(8,128)S(1)}, u32[]{:S(2)}, u32[]{:S(2)}) %collective-permute-start.7) | collective-permute-done | bytes 98336 | tf_op jit(solution)/shard_map/ppermute | solution.py:226
  64.3 2.0 %collective-permute-done.6.two.x2 = f32[192,128]{1,0:T(8,128)S(1)} collective-permute-done((f32[192,128]{1,0:T(8,128)S(1)}, f32[192,128]{1,0:T(8,128)S(1)}, u32[]{:S(2)}, u32[]{:S(2)}) %collective-permute-start.6) | collective-permute-done | bytes 98336 | tf_op jit(solution)/shard_map/ppermute | solution.py:226
  66.2 1.1 collective-permute-done.5.one.x1
  67.3 0.9 copy-done.6
  68.2 2.0 %shard_map.60 = bf16[2,64,320]{2,1,0:T(8,128)(2,1)S(1)} custom-call(s32[3]{0:T(128)S(1)} %pad_add_fusion.place, f32[8,56,128]{2,1,0:T(8,128)S(1)} %all_to_all.31.whole, f32[192,128]{1,0:T(8,128)S(1)} %get-tuple-element.13.core_other, f32[192,128]{1,0:T(8,128)S(1)} %get-tuple-element.15.before, f32[192,128]{1,0:T(8,128)S(1)} %collective-permute-done.5.one.x1, ...), custom_call_target="tpu_custom_call" | custom-call | tf_op jit(solution)/shard_map/pallas_call | solution.py:46
  70.3 24.0 %all_to_all.32.forward = bf16[8,2,64,320]{3,2,1,0:T(8,128)(2,1)S(1)} all-to-all(bf16[8,2,64,320]{3,2,1,0:T(8,128)(2,1)S(1)} %broadcast_in_dim.3), channel_id=1, replica_groups=mesh['chain_0'=4,'chain_1'=4,'chain_2'=2,'col'=8] {'col'}, dimensions={0} | all-to-all | bytes 1310720 | tf_op jit(solution)/shard_map/all_to_all | solution.py:220
  94.3 2.3 %shard_map.61 = (f32[2,64,320]{2,1,0:T(8,128)S(1)}, f32[8,16,128]{2,1,0:T(8,128)S(1)}) custom-call(s32[3]{0:T(128)S(1)} %pad_add_fusion.place, bf16[8,2,64,320]{3,2,1,0:T(8,128)(2,1)S(1)} %all_to_all.32.forward, bf16[2,320,2560]{2,1,0:T(8,128)(2,1)S(1)} %copy-done, bf16[2,320,128]{2,1,0:T(8,128)(2,1)S(1)} %copy-done.2), custom_call_target="tpu_custom_call" | custom-call | tf_op jit(solution)/shard_map/pallas_call | solution.py:46
  96.7 10.8 %all_to_all.33.parts = f32[8,16,128]{2,1,0:T(8,128)S(1)} all-to-all(f32[8,16,128]{2,1,0:T(8,128)S(1)} %get-tuple-element.17), channel_id=1, replica_groups=mesh['chain_0'=4,'chain_1'=4,'chain_2'=2,'col'=8] {'col'}, dimensions={0} | all-to-all | bytes 131072 | tf_op jit(solution)/shard_map/all_to_all | solution.py:220
  107.4 1.3 shard_map.62
  108.8 13.6 %all_to_all.34.got = f32[32,8,128]{2,1,0:T(8,128)S(1)} all-to-all(f32[32,8,128]{2,1,0:T(8,128)S(1)} %get-tuple-element.18), channel_id=1, replica_groups=mesh['chain_0'=4,'chain_1'=4,'chain_2'=2,'col'=8] {'chain_0','chain_1','..., dimensions={0} | all-to-all | bytes 262144 | tf_op jit(solution)/shard_map/all_to_all | solution.py:220
  122.4 2.8 %shard_map.63 = f32[8,16,128]{2,1,0:T(8,128)S(1)} custom-call(s32[3]{0:T(128)S(1)} %pad_add_fusion.place, f32[32,8,128]{2,1,0:T(8,128)S(1)} %all_to_all.34.got, f32[16,128]{1,0:T(8,128)S(1)} %get-tuple-element.19.carried, f32[8,56,128]{2,1,0:T(8,128)S(1)} %all_to_all.31.whole, f32[192,128]{1,0:T(8,128)S(1)} %get-tuple-element.13.core_other, ...), custom_call_target="tpu_custom_call" | custom-call | tf_op jit(solution)/shard_map/pallas_call | solution.py:46
  125.2 10.8 %all_to_all.35.got = f32[8,16,128]{2,1,0:T(8,128)S(1)} all-to-all(f32[8,16,128]{2,1,0:T(8,128)S(1)} %shard_map.63), channel_id=1, replica_groups=mesh['chain_0'=4,'chain_1'=4,'chain_2'=2,'col'=8] {'col'}, dimensions={0} | all-to-all | bytes 131072 | tf_op jit(solution)/shard_map/all_to_all | solution.py:220
  136.0 1.5 %shard_map.64 = f32[2,64,320]{2,1,0:T(8,128)} custom-call(s32[3]{0:T(128)S(1)} %pad_add_fusion.place, f32[8,16,128]{2,1,0:T(8,128)S(1)} %all_to_all.35.got, f32[2,64,320]{2,1,0:T(8,128)S(1)} %get-tuple-element.20.applied, bf16[2,320,128]{2,1,0:T(8,128)(2,1)S(1)} %copy-done.4, bf16[1,320,128]{2,1,0:T(8,128)(2,1)S(1)} %collective-permute-done.arriving), custom_call_target="tpu_custom_call" | custom-call | tf_op jit(solution)/shard_map/pallas_call | solution.py:46
  (19 shorter events, 3.4 us)
Async XLA Ops:
  0.0 67.3 %copy-start.2 = (bf16[2,320,128]{2,1,0:T(8,128)(2,1)S(1)}, bf16[2,320,128]{2,1,0:T(8,128)(2,1)}, u32[]{:S(2)}) copy-start(bf16[2,320,128]{2,1,0:T(8,128)(2,1)} %entry.5) | copy-start | bytes 491524
  0.9 3.2 %collective-permute-start = (bf16[1,320,128]{2,1,0:T(8,128)(2,1)S(1)}, bf16[1,320,128]{2,1,0:T(8,128)(2,1)S(1)}, u32[]{:S(2)}, u32[]{:S(2)}) collective-permute-start(bf16[1,320,128]{2,1,0:T(8,128)(2,1)S(1)} %slice.3), channel_id=1, source_target_pairs={{8,0},{16,8},{24,16},{32,24},{40,32},{48,40},{56,48},{64,56},{72,6... | collective-permute-start | bytes 245768 | tf_op jit(solution)/shard_map/ppermute | solution.py:237
  2.3 92.0 %copy-start = (bf16[2,320,2560]{2,1,0:T(8,128)(2,1)S(1)}, bf16[2,320,2560]{2,1,0:T(8,128)(2,1)}, u32[]{:S(2)}) copy-start(bf16[2,320,2560]{2,1,0:T(8,128)(2,1)} %inverse.1) | copy-start | bytes 9830404
  4.1 0.9 copy-start.1
  5.0 0.9 copy-start.3
  5.9 0.9 copy-start.5
  6.8 0.8 copy-start.7
  43.2 1.4 %collective-permute-start.1 = (f32[192,128]{1,0:T(8,128)S(1)}, f32[192,128]{1,0:T(8,128)S(1)}, u32[]{:S(2)}, u32[]{:S(2)}) collective-permute-start(f32[192,128]{1,0:T(8,128)S(1)} %shard_map.57.mine), channel_id=1, source_target_pairs={{0,8},{8,0},{1,9},{9,1},{2,10},{10,2},{3,11},{11,3},{4,12},{12,4},... | collective-permute-start | bytes 294920 | tf_op jit(solution)/shard_map/ppermute | solution.py:244
  45.4 5.8 %collective-permute-start.4 = (f32[192,128]{1,0:T(8,128)S(1)}, f32[192,128]{1,0:T(8,128)S(1)}, u32[]{:S(2)}, u32[]{:S(2)}) collective-permute-start(f32[192,128]{1,0:T(8,128)S(1)} %get-tuple-element.14.mine), channel_id=1, source_target_pairs={{0,48},{16,0},{32,16},{48,32},{1,49},{17,1},{33,17},{49,33},{2,50}... | collective-permute-start | bytes 294920 | tf_op jit(solution)/shard_map/ppermute | solution.py:226
  48.0 7.2 %collective-permute-start.3 = (f32[192,128]{1,0:T(8,128)S(1)}, f32[192,128]{1,0:T(8,128)S(1)}, u32[]{:S(2)}, u32[]{:S(2)}) collective-permute-start(f32[192,128]{1,0:T(8,128)S(1)} %get-tuple-element.14.mine), channel_id=1, source_target_pairs={{0,32},{16,48},{32,0},{48,16},{1,33},{17,49},{33,1},{49,17},{2,34}... | collective-permute-start | bytes 294920 | tf_op jit(solution)/shard_map/ppermute | solution.py:226
  50.0 6.4 %collective-permute-start.2 = (f32[192,128]{1,0:T(8,128)S(1)}, f32[192,128]{1,0:T(8,128)S(1)}, u32[]{:S(2)}, u32[]{:S(2)}) collective-permute-start(f32[192,128]{1,0:T(8,128)S(1)} %get-tuple-element.14.mine), channel_id=1, source_target_pairs={{0,16},{16,32},{32,48},{48,0},{1,17},{17,33},{33,49},{49,1},{2,18}... | collective-permute-start | bytes 294920 | tf_op jit(solution)/shard_map/ppermute | solution.py:226
  57.8 6.4 %collective-permute-start.7 = (f32[192,128]{1,0:T(8,128)S(1)}, f32[192,128]{1,0:T(8,128)S(1)}, u32[]{:S(2)}, u32[]{:S(2)}) collective-permute-start(f32[192,128]{1,0:T(8,128)S(1)} %get-tuple-element.16), channel_id=1, source_target_pairs={{0,192},{64,0},{128,64},{192,128},{1,193},{65,1},{129,65},{193,129... | collective-permute-start | bytes 294920 | tf_op jit(solution)/shard_map/ppermute | solution.py:226
  60.1 6.1 %collective-permute-start.6 = (f32[192,128]{1,0:T(8,128)S(1)}, f32[192,128]{1,0:T(8,128)S(1)}, u32[]{:S(2)}, u32[]{:S(2)}) collective-permute-start(f32[192,128]{1,0:T(8,128)S(1)} %get-tuple-element.16), channel_id=1, source_target_pairs={{0,128},{64,192},{128,0},{192,64},{1,129},{65,193},{129,1},{193,65... | collective-permute-start | bytes 294920 | tf_op jit(solution)/shard_map/ppermute | solution.py:226
  61.5 5.8 %collective-permute-start.5 = (f32[192,128]{1,0:T(8,128)S(1)}, f32[192,128]{1,0:T(8,128)S(1)}, u32[]{:S(2)}, u32[]{:S(2)}) collective-permute-start(f32[192,128]{1,0:T(8,128)S(1)} %get-tuple-element.16), channel_id=1, source_target_pairs={{0,64},{64,128},{128,192},{192,0},{1,65},{65,129},{129,193},{193,1... | collective-permute-start | bytes 294920 | tf_op jit(solution)/shard_map/ppermute | solution.py:226
  67.3 0.9 copy-start.6
  94.3 41.6 %copy-start.4 = (bf16[2,320,128]{2,1,0:T(8,128)(2,1)S(1)}, bf16[2,320,128]{2,1,0:T(8,128)(2,1)}, u32[]{:S(2)}) copy-start(bf16[2,320,128]{2,1,0:T(8,128)(2,1)} %exit_.3) | copy-start | bytes 491524

commit v2 on v1

v2 whole, which is shorter than its diff:
```python
import jax
import jax.numpy as jnp
from jax import lax
from jax.experimental import pallas as pl
from jax.experimental.pallas import tpu as pltpu
from jax.sharding import Mesh
from jax.sharding import PartitionSpec as P

X, Y, CORE, COL = "chain_0", "chain_1", "chain_2", "col"
CHAIN = (X, Y, CORE)
F32 = jnp.float32
BF16 = jnp.bfloat16

NN = (((1,), (0,)), ((), ()))
NT = (((1,), (1,)), ((), ()))
TN = (((0,), (0,)), ((), ()))


def dot16(a, b, dims):
    return lax.dot_general(a, b, dims, preferred_element_type=F32)


def dot32(a, b, dims):
    return lax.dot_general(a, b, dims, precision=lax.Precision.HIGHEST, preferred_element_type=F32)


def dot32_16(a, b, dims):
    high = a.astype(BF16)
    rest = a - high.astype(F32)
    middle = rest.astype(BF16)
    low = (rest - middle.astype(F32)).astype(BF16)
    rows = a.shape[0]
    out = dot16(jnp.concatenate([high, middle, low], axis=0), b, dims)
    return (out[2 * rows :] + out[rows : 2 * rows]) + out[:rows]


def vmem():
    return pl.BlockSpec(memory_space=pltpu.VMEM)


def smem():
    return pl.BlockSpec(memory_space=pltpu.SMEM)


def hbm():
    return pl.BlockSpec(memory_space=pltpu.HBM)


def call(kernel, place, arrays, outs, scratch=(), specs=None, cost=None, room=40):
    return pl.pallas_call(
        kernel,
        out_shape=outs,
        in_specs=[smem()] + (specs or [vmem()] * len(arrays)),
        out_specs=jax.tree.map(lambda _: vmem(), outs),
        scratch_shapes=list(scratch),
        cost_estimate=cost and pl.CostEstimate(flops=cost, bytes_accessed=cost // 100, transcendentals=0),
        compiler_params=pltpu.CompilerParams(vmem_limit_bytes=room * 1024 * 1024),
    )(place, *arrays)


def of(shape, dtype=F32):
    return jax.ShapeDtypeStruct(shape, dtype)


def put(out, start, rows, value):
    groups = out.shape[0]
    out[:, start : start + rows, :] = value.reshape(groups, rows, value.shape[1])


def load_kernel(place, entry, exit_, rhs, previous, entry_v, exit_v, rhs_v, turned, out, previous_v, sems):
    copies = [
        pltpu.make_async_copy(source, target, sems.at[i])
        for i, (source, target) in enumerate(
            ((entry, entry_v), (exit_, exit_v), (rhs, rhs_v), (previous, previous_v))
        )
    ]
    for copy in copies:
        copy.start()
    for copy in copies:
        copy.wait()
    groups = out.shape[0]
    n = entry_v.shape[2] // groups
    c = rhs_v.shape[1] // groups
    put(out, 0, n, -dot16(entry_v[0], exit_v[1], TN))
    put(out, n, c, dot16(rhs_v[0], exit_v[1], NN))
    put(out, n + c, c, dot16(previous_v[...], exit_v[0], NN))
    both = jnp.concatenate([rhs_v[0], rhs_v[1]], axis=0).astype(F32)
    turned[...] = both.T


def partial_kernel(place, entry, arriving, rhs, early, out):
    groups = out.shape[0]
    n = entry.shape[2] // groups
    c = rhs.shape[1] // groups
    out[:, 0:n, :] = early[:, 0:n, :]
    put(out, n, n, -dot16(entry[1], arriving[0], TN))
    out[:, 2 * n : 2 * n + c, :] = early[:, n : n + c, :]
    put(out, 2 * n + c, c, dot16(rhs[1], arriving[0], NN))
    out[:, 2 * n + 2 * c :, :] = early[:, n + c :, :]


def sum_kernel(place, parts, out):
    total = parts[0]
    for k in range(1, parts.shape[0]):
        total = total + parts[k]
    for k in range(parts.shape[0]):
        out[k] = total


def pieces(whole):
    groups, rows, width = whole.shape
    n = width // groups
    c = (rows - 2 * n) // 3

    def take(start, count):
        return whole[:, start : start + count, :].reshape(groups * count, width)

    return take(0, n), take(n, n), take(2 * n, c), take(2 * n + c, c), take(2 * n + 2 * c, c)


def is_first(place):
    return (place[0] == 0) & (place[1] == 0) & (place[2] == 0)


def after(earlier, later, n):
    out = dot32(earlier, later[:n], NN)
    return out[:n], out[n:] + later[n:]


def local_kernel(place, whole, out):
    couple0, couple1, source0, source1, opening = pieces(whole)
    n = couple0.shape[0]
    folded = dot32(opening, couple0, NN) + source0
    source0 = jnp.where(is_first(place), folded, source0)
    out[:n] = dot32(couple0, couple1, NN)
    out[n:] = dot32(source0, couple1, NN) + source1


def pair_kernel(place, mine, other, out):
    n = mine.shape[1]
    upper = place[2] == 1
    first = jnp.where(upper, other[...], mine[...])
    second = jnp.where(upper, mine[...], other[...])
    out[:n], out[n:] = after(first, second, n)


def group_kernel(place, mine, one, two, three, total, before, slots):
    n = mine.shape[1]
    y = place[1]
    for d, ref in enumerate((mine, one, two, three)):
        slots[lax.rem(y - d + 4, 4)] = ref[...]

    low_top, low_bottom = after(slots[0], slots[1], n)
    high_top, high_bottom = after(slots[2], slots[3], n)
    low = jnp.concatenate([low_top, low_bottom], axis=0)
    out = dot32(low, high_top, NN)
    total[:n] = out[:n]
    total[n:] = out[n:] + high_bottom
    rows = lax.broadcasted_iota(jnp.int32, mine.shape, 0)
    lanes = lax.broadcasted_iota(jnp.int32, mine.shape, 1)

    @pl.when(y == 0)
    def _():
        before[...] = jnp.where(rows == lanes, 1.0, 0.0).astype(F32)

    @pl.when(y == 1)
    def _():
        before[...] = slots[0]

    @pl.when(y == 2)
    def _():
        before[...] = low

    @pl.when(y == 3)
    def _():
        out = dot32(low, slots[2, :n], NN)
        before[:n] = out[:n]
        before[n:] = out[n:] + slots[2, n:]


def tail_kernel(place, whole, other, before, maps, shifts):
    couple0, _, source0, _, opening = pieces(whole)
    n = couple0.shape[0]
    reach, shift = after(before[...], other[...], n)
    upper = place[2] == 1
    reach = jnp.where(upper, reach, before[:n])
    shift = jnp.where(upper, shift, before[n:])
    shift = jnp.where(is_first(place), opening, shift)
    out = dot32(jnp.concatenate([reach, shift], axis=0), couple0, NN)
    maps[:, :n] = reach
    maps[:, n:] = out[:n]
    shifts[:, :n] = shift
    shifts[:, n:] = out[n:] + source0


def forward_kernel(place, maps, shifts, one, two, three, entry, turned, out):
    n = one.shape[1]
    x = place[0]
    state = jnp.where(3 <= x, three[n:], 0.0)
    state = jnp.where(2 <= x, dot32(state, two[:n], NN) + two[n:], state)
    state = jnp.where(1 <= x, dot32(state, one[:n], NN) + one[n:], state)
    both = dot32(state, maps[...], NN) + shifts[...]
    states = jnp.concatenate([both[:, :n], both[:, n:]], axis=0)
    high = states.astype(BF16)
    rest = states - high.astype(F32)
    middle = rest.astype(BF16)
    low = (rest - middle.astype(F32)).astype(BF16)
    lanes = lax.broadcasted_iota(jnp.int32, out.shape, 1)

    def through(i):
        return (dot16(entry[i], low, NT) + dot16(entry[i], middle, NT)) + dot16(entry[i], high, NT)

    product = jnp.where(lanes < both.shape[0], through(0), through(1))
    out[...] = (turned[...] - product).astype(BF16)


def apply_kernel(place, forward, inverse, entry, applied, carried):
    groups, local, both = forward.shape
    whole = forward[...].reshape(groups * local, both)
    lanes = lax.broadcasted_iota(jnp.int32, applied.shape, 1)
    half = both // 2
    value = jnp.where(lanes < half, dot16(inverse[0], whole, NN), dot16(inverse[1], whole, NN))
    applied[...] = value
    low = value.astype(BF16)
    c = half // groups
    put(carried, 0, c, dot16(low, entry[0], TN)[:half])
    put(carried, c, c, dot16(low, entry[1], TN)[half:])


def routes_kernel(place, whole, other, before, y1, y2, y3, x1, x2, x3, leave, reach):
    couple0, couple1, _, _, _ = pieces(whole)
    n = couple0.shape[0]
    rows = lax.broadcasted_iota(jnp.int32, (n, n), 0)
    lanes = lax.broadcasted_iota(jnp.int32, (n, n), 1)
    identity = jnp.where(rows == lanes, 1.0, 0.0).astype(F32)
    x, y, core = place[0], place[1], place[2]
    lower = jnp.where(core == 1, other[:n], identity)
    out = dot32(lower, couple0, NN)
    chip = jnp.concatenate([lower, out], axis=1)
    leave[0:n, :n] = identity
    leave[0:n, n:] = couple0
    leave[n : 2 * n, :] = chip
    leave[2 * n : 3 * n, :] = dot32(before[:n], chip, NN)
    here = jnp.where(core == 0, other[:n], identity)
    blocks = [identity]
    for e, ref in ((1, y3), (2, y2), (3, y1)):
        blocks.append(here)
        here = jnp.where(y + e <= 3, dot32(here, ref[:n], NN), here)
    for e, ref in ((1, x3), (2, x2), (3, x1)):
        blocks.append(here)
        if e < 3:
            here = dot32(here, ref[:n], NN)
    stacked = jnp.concatenate(blocks, axis=1)
    reach[:n, :] = stacked
    reach[n:, :] = dot32(couple1, stacked, NN)


def back_kernel(place, parts, leave, carried, send):
    c = parts.shape[1] // 2
    total = parts[0]
    for k in range(1, parts.shape[0]):
        total = total + parts[k]
    carried[...] = total
    n = total.shape[1]
    x, y = place[0], place[1]
    values = dot32(jnp.concatenate([total[:c], total[c:]], axis=1), leave[...], NT)
    own, chip, group = values[:, :n], values[:, n : 2 * n], values[:, 2 * n :]
    for k in range(send.shape[0]):
        same_x = x == k // 8
        same_y = y == (k // 2) % 4
        send[k] = jnp.where(same_x, jnp.where(same_y, own, chip), group)


def behind_kernel(place, got, carried, reach, out):
    n = carried.shape[1]
    c = carried.shape[0] // 2
    x, y, core = place[0], place[1], place[2]
    terms = [jnp.where(core == 0, got[x * 8 + y * 2 + 1], 0.0)]
    for e in (1, 2, 3):
        base = x * 8 + lax.rem(y + e, 4) * 2
        terms.append(jnp.where(y + e <= 3, got[base] + got[base + 1], 0.0))
    for e in (1, 2, 3):
        base = lax.rem(x + e, 4) * 8
        extra = got[base]
        for k in range(1, 8):
            extra = extra + got[base + k]
        terms.append(jnp.where(x + e <= 3, extra, 0.0))
    values = dot32(jnp.concatenate(terms, axis=1), reach[...], NT)
    state = values[:, :n]
    inner = values[:, n:] + carried[c:]
    for k in range(out.shape[0]):
        out[k, :c] = inner
        out[k, c:] = state


def final_kernel(place, got, applied, exit_, arriving, out):
    groups, rows, width = got.shape
    c = rows // 2
    inner = got[:, :c, :].reshape(groups * c, width)
    outer = got[:, c:, :].reshape(groups * c, width)
    turned = applied[...].T
    out[0] = turned[: groups * c] - dot32_16(inner, exit_[1], NT)
    out[1] = turned[groups * c :] - dot32_16(outer, arriving[0], NT)


def exchange(value, axes):
    return lax.all_to_all(value, axes, split_axis=0, concat_axis=0, tiled=True)


def ring(value, axis):
    size = lax.axis_size(axis)
    return [
        lax.ppermute(value, axis, [(i, (i + d) % size) for i in range(size)])
        for d in range(1, size)
    ]


def shards(rhs, block_inverse, entry, exit_, previous):
    z = lax.axis_size(COL)
    here, cols, local = rhs.shape
    n = entry.shape[2]
    place = jnp.stack([lax.axis_index(X), lax.axis_index(Y), lax.axis_index(CORE)]).astype(jnp.int32)
    chain = lax.axis_size(CHAIN)
    arriving = lax.ppermute(exit_[:1], CHAIN, [(i, i - 1) for i in range(1, chain)])
    rows = (2 * n + 3 * cols) // z
    entry_v, exit_v, rhs_v, turned, early = call(
        load_kernel,
        place,
        [pltpu.with_memory_space_constraint(a, pltpu.HBM) for a in (entry, exit_, rhs, previous)],
        (
            of(entry.shape, BF16),
            of(exit_.shape, BF16),
            of(rhs.shape, BF16),
            of((local, 2 * cols)),
            of((z, (n + 2 * cols) // z, n)),
        ),
        [pltpu.VMEM(previous.shape, BF16), pltpu.SemaphoreType.DMA((4,))],
        [hbm()] * 4,
        cost=1 << 28,
    )
    parts = call(partial_kernel, place, (entry_v, arriving, rhs_v, early), of((z, rows, n)))
    summed = call(sum_kernel, place, (exchange(parts, COL),), of((z, rows, n)))
    whole = exchange(summed, COL)
    maps = of((n + cols, n))
    mine = call(local_kernel, place, (whole,), maps)
    other = lax.ppermute(mine, CORE, [(0, 1), (1, 0)])
    chip = call(pair_kernel, place, (mine, other), maps)
    y1, y2, y3 = ring(chip, Y)
    group, before = call(
        group_kernel, place, (chip, y1, y2, y3), (maps, maps), [pltpu.VMEM((4, n + cols, n), F32)]
    )
    x1, x2, x3 = ring(group, X)
    ahead, shifts = call(
        tail_kernel, place, (whole, other, before), (of((n, 2 * n)), of((cols, 2 * n))), cost=1 << 27
    )
    forward = call(
        forward_kernel,
        place,
        (ahead, shifts, x1, x2, x3, entry_v, turned),
        of((local, 2 * cols), BF16),
    )
    leave, reach = call(
        routes_kernel,
        place,
        (whole, other, before, y1, y2, y3, x1, x2, x3),
        (of((3 * n, 2 * n)), of((2 * n, 7 * n))),
        cost=1 << 29,
    )
    gathered = exchange(jnp.broadcast_to(forward, (z, *forward.shape)), COL)
    c = cols // z
    applied, carried_parts = call(
        apply_kernel,
        place,
        (gathered, block_inverse, entry_v),
        (of((local, 2 * cols)), of((z, 2 * c, n))),
    )
    carried, send = call(
        back_kernel,
        place,
        (exchange(carried_parts, COL), leave),
        (of((2 * c, n)), of((chain, c, n))),
    )
    behind = call(
        behind_kernel, place, (exchange(send, CHAIN), carried, reach), of((z, 2 * c, n))
    )
    return call(
        final_kernel,
        place,
        (exchange(behind, COL), applied, exit_v, arriving),
        of((here, cols, local)),
    )


def solution(mesh):
    torus = Mesh(mesh.devices.reshape(4, 4, 2, mesh.shape["col"]), (X, Y, CORE, COL))
    return jax.shard_map(
        shards,
        mesh=torus,
        in_specs=(
            P(CHAIN, None, COL),
            P(CHAIN, COL, None),
            P(CHAIN, COL, None),
            P(CHAIN, COL, None),
            P(None, COL),
        ),
        out_specs=P(CHAIN, None, COL),
        check_vma=False,
    )
```

time: 139 us -> 129 us (0.928)
  blocking collectives: 92.4 us -> 80 us
  starting transfers between devices: 11.8 us -> 18.8 us
  local copies, waits for them, and re-layouts: 5.45 us -> 0.98 us
  Pallas kernels: 14.5 us -> 17 us
  waiting for transfers between devices: 13.2 us -> 10.8 us
    all_to_all x6 -> x5, blocking collectives: 92.4 us -> 80 us  [exchange(): return lax.all_to_all(value, axes, split_axis=0, concat_axis=0, tiled=True)]
    ppermute x6, waiting for transfers between devices: 10.2 us -> 4.69 us  [ring(): lax.ppermute(value, axis, [(i, (i + d) % size) for i in range(size)])]
    all_to_all x0 -> x1, waiting for transfers between devices: none -> 4.9 us  [exchange(): return lax.all_to_all(value, axes, split_axis=0, concat_axis=0, tiled=True)]
    all_to_all x0 -> x1, starting transfers between devices: none -> 4.71 us  [exchange(): return lax.all_to_all(value, axes, split_axis=0, concat_axis=0, tiled=True)]
    unnamed x16 -> x2, local copies, waits for them, and re-layouts: 4.43 us -> 0.01 us
    pallas_call x10 -> x13, Pallas kernels: 14.5 us -> 17 us  [call(): pl.pallas_call(kernel, out_shape=outs, in_specs=[smem()] + (specs or [vme...]
    ppermute x6, starting transfers between devices: 10.3 us -> 12.6 us  [ring(): lax.ppermute(value, axis, [(i, (i + d) % size) for i in range(size)])]
    ppermute x1, waiting for transfers between devices: 1.79 us -> 0.01 us  [shards(): lax.ppermute(exit_[:1], CHAIN, [(i, i - 1) for i in range(1, chain)])]
  transfers between devices with their start and end apart: 8 -> 9, of which waited for: 7 -> 5; matrix products, arithmetic and copies ran while one was open for 0% -> 0% of each run, Pallas kernels for 0% -> 4%
where the time goes in v2:
time: 129 us; the launch traced here: 128 us
  blocking collectives  80 us (62%)
  starting transfers between devices  18.8 us (15%)
  Pallas kernels  17 us (13%)
  waiting for transfers between devices  10.8 us (8%)
    all_to_all x5, blocking collectives, exchange(): return lax.all_to_all(value, axes, split_axis=0, concat_axis=0, tiled=True)  80 us
    pallas_call x13, Pallas kernels, call(): pl.pallas_call(kernel, out_shape=outs, in_specs=[smem()] + (specs or [vme...  17 us
    ppermute x6, starting transfers between devices, ring(): lax.ppermute(value, axis, [(i, (i + d) % size) for i in range(size)])  12.6 us
    all_to_all x1, waiting for transfers between devices, exchange(): return lax.all_to_all(value, axes, split_axis=0, concat_axis=0, tiled=True)  4.9 us
    all_to_all x1, starting transfers between devices, exchange(): return lax.all_to_all(value, axes, split_axis=0, concat_axis=0, tiled=True)  4.71 us
    ppermute x6, waiting for transfers between devices, ring(): lax.ppermute(value, axis, [(i, (i + d) % size) for i in range(size)])  4.69 us
  transfers between devices with their start and end apart: 9, of which 5 were waited for; matrix products, arithmetic and copies ran while one was open for 0% of the time, Pallas kernels for 4%

profile of v2, /device:TPU:32, one launch (start us, length us, event | category | flops | bytes accessed | tf_op | source)
XLA Modules:
  0.0 127.8 jit_solution(10528706377175954055)
XLA Ops:
  0.0 0.9 slice.3
  0.9 1.3 %collective-permute-start = (bf16[1,320,128]{2,1,0:T(8,128)(2,1)S(1)}, bf16[1,320,128]{2,1,0:T(8,128)(2,1)S(1)}, u32[]{:S(2)}, u32[]{:S(2)}) collective-permute-start(bf16[1,320,128]{2,1,0:T(8,128)(2,1)S(1)} %slice.3), channel_id=1, source_target_pairs={{8,0},{16,8},{24,16},{32,24},{40,32},{48,40},{56,48},{64,56},{72,6... | collective-permute-start | bytes 245768 | tf_op jit(solution)/shard_map/ppermute | solution.py:324
  2.3 1.9 %shard_map.55 = (bf16[2,320,128]{2,1,0:T(8,128)(2,1)S(1)}, bf16[2,320,128]{2,1,0:T(8,128)(2,1)S(1)}, bf16[2,64,320]{2,1,0:T(8,128)(2,1)S(1)}, f32[320,128]{1,0:T(8,128)S(1)}, f32[8,32,128]{2,1,0:T(8,128)S(1)}) custom-call(s32[3]{0:T(128)S(1)} %pad_add_fusion.place, bf16[2,320,128]{2,1,0:T(8,128)(2,1)} %entry.1, bf16[2,320,128]{2,1,0:T(8,128)(2,1)} %exit_.1, ...), custom_call_target="tpu_custom_call" | custom-call | flops 268435456 | bytes 2684354 | tf_op jit(solution)/shard_map/pallas_call | solution.py:50
  4.2 0.8 shard_map.56
  4.9 17.1 %all_to_all.30.parts = f32[8,56,128]{2,1,0:T(8,128)S(1)} all-to-all(f32[8,56,128]{2,1,0:T(8,128)S(1)} %shard_map.56), channel_id=1, replica_groups=mesh['chain_0'=4,'chain_1'=4,'chain_2'=2,'col'=8] {'col'}, dimensions={0} | all-to-all | bytes 458752 | tf_op jit(solution)/shard_map/all_to_all | solution.py:307
  22.0 0.6 shard_map.57
  22.6 16.3 %all_to_all.31.whole = f32[8,56,128]{2,1,0:T(8,128)S(1)} all-to-all(f32[8,56,128]{2,1,0:T(8,128)S(1)} %shard_map.57), channel_id=1, replica_groups=mesh['chain_0'=4,'chain_1'=4,'chain_2'=2,'col'=8] {'col'}, dimensions={0} | all-to-all | bytes 458752 | tf_op jit(solution)/shard_map/all_to_all | solution.py:307
  38.9 0.9 shard_map.58.mine
  39.8 0.2 collective-permute-start.1
  40.0 1.2 collective-permute-done.1.other
  41.2 0.8 shard_map.59.mine
  42.0 2.5 %collective-permute-start.2 = (f32[192,128]{1,0:T(8,128)S(1)}, f32[192,128]{1,0:T(8,128)S(1)}, u32[]{:S(2)}, u32[]{:S(2)}) collective-permute-start(f32[192,128]{1,0:T(8,128)S(1)} %shard_map.59.mine), channel_id=1, source_target_pairs={{0,16},{16,32},{32,48},{48,0},{1,17},{17,33},{33,49},{49,1},{2,18}... | collective-permute-start | bytes 294920 | tf_op jit(solution)/shard_map/ppermute | solution.py:313
  44.5 1.9 %collective-permute-start.3 = (f32[192,128]{1,0:T(8,128)S(1)}, f32[192,128]{1,0:T(8,128)S(1)}, u32[]{:S(2)}, u32[]{:S(2)}) collective-permute-start(f32[192,128]{1,0:T(8,128)S(1)} %shard_map.59.mine), channel_id=1, source_target_pairs={{0,32},{16,48},{32,0},{48,16},{1,33},{17,49},{33,1},{49,17},{2,34}... | collective-permute-start | bytes 294920 | tf_op jit(solution)/shard_map/ppermute | solution.py:313
  46.3 2.5 %collective-permute-start.4 = (f32[192,128]{1,0:T(8,128)S(1)}, f32[192,128]{1,0:T(8,128)S(1)}, u32[]{:S(2)}, u32[]{:S(2)}) collective-permute-start(f32[192,128]{1,0:T(8,128)S(1)} %shard_map.59.mine), channel_id=1, source_target_pairs={{0,48},{16,0},{32,16},{48,32},{1,49},{17,1},{33,17},{49,33},{2,50}... | collective-permute-start | bytes 294920 | tf_op jit(solution)/shard_map/ppermute | solution.py:313
  48.9 2.6 %collective-permute-done.3.two.y2 = f32[192,128]{1,0:T(8,128)S(1)} collective-permute-done((f32[192,128]{1,0:T(8,128)S(1)}, f32[192,128]{1,0:T(8,128)S(1)}, u32[]{:S(2)}, u32[]{:S(2)}) %collective-permute-start.3) | collective-permute-done | bytes 98336 | tf_op jit(solution)/shard_map/ppermute | solution.py:313
  51.5 1.2 shard_map.60
  52.7 1.6 %collective-permute-start.5 = (f32[192,128]{1,0:T(8,128)S(1)}, f32[192,128]{1,0:T(8,128)S(1)}, u32[]{:S(2)}, u32[]{:S(2)}) collective-permute-start(f32[192,128]{1,0:T(8,128)S(1)} %get-tuple-element.26), channel_id=1, source_target_pairs={{0,64},{64,128},{128,192},{192,0},{1,65},{65,129},{129,193},{193,1... | collective-permute-start | bytes 294920 | tf_op jit(solution)/shard_map/ppermute | solution.py:313
  54.2 2.7 %collective-permute-start.6 = (f32[192,128]{1,0:T(8,128)S(1)}, f32[192,128]{1,0:T(8,128)S(1)}, u32[]{:S(2)}, u32[]{:S(2)}) collective-permute-start(f32[192,128]{1,0:T(8,128)S(1)} %get-tuple-element.26), channel_id=1, source_target_pairs={{0,128},{64,192},{128,0},{192,64},{1,129},{65,193},{129,1},{193,65... | collective-permute-start | bytes 294920 | tf_op jit(solution)/shard_map/ppermute | solution.py:313
  57.0 1.4 %collective-permute-start.7 = (f32[192,128]{1,0:T(8,128)S(1)}, f32[192,128]{1,0:T(8,128)S(1)}, u32[]{:S(2)}, u32[]{:S(2)}) collective-permute-start(f32[192,128]{1,0:T(8,128)S(1)} %get-tuple-element.26), channel_id=1, source_target_pairs={{0,192},{64,0},{128,64},{192,128},{1,193},{65,1},{129,65},{193,129... | collective-permute-start | bytes 294920 | tf_op jit(solution)/shard_map/ppermute | solution.py:313
  58.4 1.1 shard_map.61
  59.5 1.9 %collective-permute-done.6.two.x2 = f32[192,128]{1,0:T(8,128)S(1)} collective-permute-done((f32[192,128]{1,0:T(8,128)S(1)}, f32[192,128]{1,0:T(8,128)S(1)}, u32[]{:S(2)}, u32[]{:S(2)}) %collective-permute-start.6) | collective-permute-done | bytes 98336 | tf_op jit(solution)/shard_map/ppermute | solution.py:313
  61.6 1.5 %shard_map.62 = bf16[320,128]{1,0:T(8,128)(2,1)S(1)} custom-call(s32[3]{0:T(128)S(1)} %pad_add_fusion.place, f32[128,256]{1,0:T(8,128)S(1)} %get-tuple-element.24.maps, f32[64,256]{1,0:T(8,128)S(1)} %get-tuple-element.25.shifts, f32[192,128]{1,0:T(8,128)S(1)} %collective-permute-done.5.one.x1, f32[192,128]{1,0:T(8,128)S(1)} %collective-permute-done.6.two.x2, ...), custom_call_target="tpu_custom_call" | custom-call | tf_op jit(solution)/shard_map/pallas_call | solution.py:50
  63.2 22.2 %all_to_all.32.forward = bf16[8,320,128]{2,1,0:T(8,128)(2,1)S(1)} all-to-all(bf16[8,320,128]{2,1,0:T(8,128)(2,1)S(1)} %broadcast_in_dim.3), channel_id=1, replica_groups=mesh['chain_0'=4,'chain_1'=4,'chain_2'=2,'col'=8] {'col'}, dimensions={0} | all-to-all | bytes 1310720 | tf_op jit(solution)/shard_map/all_to_all | solution.py:307
  85.4 2.4 %shard_map.63 = (f32[320,128]{1,0:T(8,128)S(1)}, f32[8,16,128]{2,1,0:T(8,128)}) custom-call(s32[3]{0:T(128)S(1)} %pad_add_fusion.place, bf16[8,320,128]{2,1,0:T(8,128)(2,1)S(1)} %all_to_all.32.forward, bf16[2,320,2560]{2,1,0:T(8,128)(2,1)S(1)} %copy-done, bf16[2,320,128]{2,1,0:T(8,128)(2,1)S(1)} %get-tuple-element.20.entry), custom_call_target="tpu_custom_call" | custom-call | tf_op jit(solution)/shard_map/pallas_call | solution.py:50
  87.8 4.7 %all-to-all-start.3 = ((f32[8,16,128]{2,1,0:T(8,128)}), f32[8,16,128]{2,1,0:T(8,128)S(1)}, u32[]{:S(2)}, u32[]{:S(2)}) async-start(f32[8,16,128]{2,1,0:T(8,128)} %get-tuple-element.28), calls=%async_computation.3 | async-start | bytes 131072 | tf_op jit(solution)/shard_map/all_to_all | solution.py:307
  92.5 2.0 %shard_map.64 = (f32[384,256]{1,0:T(8,128)S(1)}, f32[256,896]{1,0:T(8,128)S(1)}) custom-call(s32[3]{0:T(128)S(1)} %pad_add_fusion.place, f32[8,56,128]{2,1,0:T(8,128)S(1)} %all_to_all.31.whole, f32[192,128]{1,0:T(8,128)S(1)} %collective-permute-done.1.other, f32[192,128]{1,0:T(8,128)S(1)} %get-tuple-element.23.before, ...), custom_call_target="tpu_custom_call" | custom-call | flops 536870912 | bytes 5368709 | tf_op jit(solution)/shard_map/pallas_call | solution.py:50
  94.5 4.9 %all-to-all-done.3.parts = f32[8,16,128]{2,1,0:T(8,128)S(1)} async-done(((f32[8,16,128]{2,1,0:T(8,128)}), f32[8,16,128]{2,1,0:T(8,128)S(1)}, u32[]{:S(2)}, u32[]{:S(2)}) %all-to-all-start.3) | async-done | bytes 65568 | tf_op jit(solution)/shard_map/all_to_all | solution.py:307
  99.4 1.0 shard_map.65
  100.4 13.8 %all_to_all.33.got = f32[32,8,128]{2,1,0:T(8,128)S(1)} all-to-all(f32[32,8,128]{2,1,0:T(8,128)S(1)} %get-tuple-element.30), channel_id=1, replica_groups=mesh['chain_0'=4,'chain_1'=4,'chain_2'=2,'col'=8] {'chain_0','chain_1','..., dimensions={0} | all-to-all | bytes 262144 | tf_op jit(solution)/shard_map/all_to_all | solution.py:307
  114.2 1.4 %shard_map.66 = f32[8,16,128]{2,1,0:T(8,128)S(1)} custom-call(s32[3]{0:T(128)S(1)} %pad_add_fusion.place, f32[32,8,128]{2,1,0:T(8,128)S(1)} %all_to_all.33.got, f32[16,128]{1,0:T(8,128)S(1)} %get-tuple-element.31.carried, f32[256,896]{1,0:T(8,128)S(1)} %get-tuple-element.32.reach), custom_call_target="tpu_custom_call" | custom-call | tf_op jit(solution)/shard_map/pallas_call | solution.py:50
  115.6 10.8 %all_to_all.34.got = f32[8,16,128]{2,1,0:T(8,128)S(1)} all-to-all(f32[8,16,128]{2,1,0:T(8,128)S(1)} %shard_map.66), channel_id=1, replica_groups=mesh['chain_0'=4,'chain_1'=4,'chain_2'=2,'col'=8] {'col'}, dimensions={0} | all-to-all | bytes 131072 | tf_op jit(solution)/shard_map/all_to_all | solution.py:307
  126.3 1.5 %shard_map.67 = f32[2,64,320]{2,1,0:T(8,128)} custom-call(s32[3]{0:T(128)S(1)} %pad_add_fusion.place, f32[8,16,128]{2,1,0:T(8,128)S(1)} %all_to_all.34.got, f32[320,128]{1,0:T(8,128)S(1)} %get-tuple-element.33.applied, bf16[2,320,128]{2,1,0:T(8,128)(2,1)S(1)} %get-tuple-element.34.exit_, bf16[1,320,128]{2,1,0:T(8,128)(2,1)S(1)} %collective-permute-done.arriving), custom_call_target="tpu_custom_call" | custom-call | tf_op jit(solution)/shard_map/pallas_call | solution.py:50
  (9 shorter events, 0.4 us)
Async XLA Ops:
  0.9 3.3 %collective-permute-start = (bf16[1,320,128]{2,1,0:T(8,128)(2,1)S(1)}, bf16[1,320,128]{2,1,0:T(8,128)(2,1)S(1)}, u32[]{:S(2)}, u32[]{:S(2)}) collective-permute-start(bf16[1,320,128]{2,1,0:T(8,128)(2,1)S(1)} %slice.3), channel_id=1, source_target_pairs={{8,0},{16,8},{24,16},{32,24},{40,32},{48,40},{56,48},{64,56},{72,6... | collective-permute-start | bytes 245768 | tf_op jit(solution)/shard_map/ppermute | solution.py:324
  4.2 81.2 %copy-start = (bf16[2,320,2560]{2,1,0:T(8,128)(2,1)S(1)}, bf16[2,320,2560]{2,1,0:T(8,128)(2,1)}, u32[]{:S(2)}) copy-start(bf16[2,320,2560]{2,1,0:T(8,128)(2,1)} %inverse.1) | copy-start | bytes 9830404
  39.8 1.4 %collective-permute-start.1 = (f32[192,128]{1,0:T(8,128)S(1)}, f32[192,128]{1,0:T(8,128)S(1)}, u32[]{:S(2)}, u32[]{:S(2)}) collective-permute-start(f32[192,128]{1,0:T(8,128)S(1)} %shard_map.58.mine), channel_id=1, source_target_pairs={{0,8},{8,0},{1,9},{9,1},{2,10},{10,2},{3,11},{11,3},{4,12},{12,4},... | collective-permute-start | bytes 294920 | tf_op jit(solution)/shard_map/ppermute | solution.py:346
  42.0 6.9 %collective-permute-start.2 = (f32[192,128]{1,0:T(8,128)S(1)}, f32[192,128]{1,0:T(8,128)S(1)}, u32[]{:S(2)}, u32[]{:S(2)}) collective-permute-start(f32[192,128]{1,0:T(8,128)S(1)} %shard_map.59.mine), channel_id=1, source_target_pairs={{0,16},{16,32},{32,48},{48,0},{1,17},{17,33},{33,49},{49,1},{2,18}... | collective-permute-start | bytes 294920 | tf_op jit(solution)/shard_map/ppermute | solution.py:313
  44.5 7.0 %collective-permute-start.3 = (f32[192,128]{1,0:T(8,128)S(1)}, f32[192,128]{1,0:T(8,128)S(1)}, u32[]{:S(2)}, u32[]{:S(2)}) collective-permute-start(f32[192,128]{1,0:T(8,128)S(1)} %shard_map.59.mine), channel_id=1, source_target_pairs={{0,32},{16,48},{32,0},{48,16},{1,33},{17,49},{33,1},{49,17},{2,34}... | collective-permute-start | bytes 294920 | tf_op jit(solution)/shard_map/ppermute | solution.py:313
  46.3 5.1 %collective-permute-start.4 = (f32[192,128]{1,0:T(8,128)S(1)}, f32[192,128]{1,0:T(8,128)S(1)}, u32[]{:S(2)}, u32[]{:S(2)}) collective-permute-start(f32[192,128]{1,0:T(8,128)S(1)} %shard_map.59.mine), channel_id=1, source_target_pairs={{0,48},{16,0},{32,16},{48,32},{1,49},{17,1},{33,17},{49,33},{2,50}... | collective-permute-start | bytes 294920 | tf_op jit(solution)/shard_map/ppermute | solution.py:313
  52.7 6.8 %collective-permute-start.5 = (f32[192,128]{1,0:T(8,128)S(1)}, f32[192,128]{1,0:T(8,128)S(1)}, u32[]{:S(2)}, u32[]{:S(2)}) collective-permute-start(f32[192,128]{1,0:T(8,128)S(1)} %get-tuple-element.26), channel_id=1, source_target_pairs={{0,64},{64,128},{128,192},{192,0},{1,65},{65,129},{129,193},{193,1... | collective-permute-start | bytes 294920 | tf_op jit(solution)/shard_map/ppermute | solution.py:313
  54.2 7.2 %collective-permute-start.6 = (f32[192,128]{1,0:T(8,128)S(1)}, f32[192,128]{1,0:T(8,128)S(1)}, u32[]{:S(2)}, u32[]{:S(2)}) collective-permute-start(f32[192,128]{1,0:T(8,128)S(1)} %get-tuple-element.26), channel_id=1, source_target_pairs={{0,128},{64,192},{128,0},{192,64},{1,129},{65,193},{129,1},{193,65... | collective-permute-start | bytes 294920 | tf_op jit(solution)/shard_map/ppermute | solution.py:313
  57.0 4.6 %collective-permute-start.7 = (f32[192,128]{1,0:T(8,128)S(1)}, f32[192,128]{1,0:T(8,128)S(1)}, u32[]{:S(2)}, u32[]{:S(2)}) collective-permute-start(f32[192,128]{1,0:T(8,128)S(1)} %get-tuple-element.26), channel_id=1, source_target_pairs={{0,192},{64,0},{128,64},{192,128},{1,193},{65,1},{129,65},{193,129... | collective-permute-start | bytes 294920 | tf_op jit(solution)/shard_map/ppermute | solution.py:313
  87.8 11.7 %all-to-all-start.3 = ((f32[8,16,128]{2,1,0:T(8,128)}), f32[8,16,128]{2,1,0:T(8,128)S(1)}, u32[]{:S(2)}, u32[]{:S(2)}) async-start(f32[8,16,128]{2,1,0:T(8,128)} %get-tuple-element.28), calls=%async_computation.3 | async-start | bytes 131072 | tf_op jit(solution)/shard_map/all_to_all | solution.py:307

commit v3 on v2

--- a/solution.py
+++ b/solution.py
@@ -34,6 +34,27 @@
     return (out[2 * rows :] + out[rows : 2 * rows]) + out[:rows]
 
 
+def three_parts(a):
+    high = a.astype(BF16).astype(F32)
+    middle = (a - high).astype(BF16).astype(F32)
+    return high, middle, (a - high) - middle
+
+
+def store_parts(ref, value):
+    for k, part in enumerate(three_parts(value)):
+        ref[k] = part.astype(BF16)
+
+
+def dot_parts(a, b, dims):
+    rows = a.shape[0]
+    parts = jnp.concatenate(three_parts(a), axis=0)
+    by_high = dot16(parts.astype(BF16), b[0], dims)
+    by_middle = dot16(parts[: 2 * rows].astype(BF16), b[1], dims)
+    by_low = dot16(parts[:rows].astype(BF16), b[2], dims)
+    small = (by_low + by_middle[rows:]) + by_high[2 * rows :]
+    return (small + (by_middle[:rows] + by_high[rows : 2 * rows])) + by_high[:rows]
+
+
 def vmem():
     return pl.BlockSpec(memory_space=pltpu.VMEM)
 
@@ -46,7 +67,7 @@
     return pl.BlockSpec(memory_space=pltpu.HBM)
 
 
-def call(kernel, place, arrays, outs, scratch=(), specs=None, cost=None, room=40):
+def call(kernel, place, arrays, outs, scratch=(), specs=None, cost=None, room=24):
     return pl.pallas_call(
         kernel,
         out_shape=outs,
@@ -67,7 +88,7 @@
     out[:, start : start + rows, :] = value.reshape(groups, rows, value.shape[1])
 
 
-def load_kernel(place, entry, exit_, rhs, previous, entry_v, exit_v, rhs_v, turned, out, previous_v, sems):
+def load_kernel(place, entry, exit_, rhs, previous, entry_v, exit_v, second, turned, out, rhs_v, previous_v, sems):
     copies = [
         pltpu.make_async_copy(source, target, sems.at[i])
         for i, (source, target) in enumerate(
@@ -83,20 +104,20 @@
     c = rhs_v.shape[1] // groups
     put(out, 0, n, -dot16(entry_v[0], exit_v[1], TN))
     put(out, n, c, dot16(rhs_v[0], exit_v[1], NN))
-    put(out, n + c, c, dot16(previous_v[...], exit_v[0], NN))
+    last = is_last(place)
+    second[...] = jnp.where(last, previous_v[...].astype(F32), rhs_v[1].astype(F32)).astype(BF16)
     both = jnp.concatenate([rhs_v[0], rhs_v[1]], axis=0).astype(F32)
     turned[...] = both.T
 
 
-def partial_kernel(place, entry, arriving, rhs, early, out):
+def partial_kernel(place, entry, arriving, second, early, out):
     groups = out.shape[0]
     n = entry.shape[2] // groups
-    c = rhs.shape[1] // groups
+    c = second.shape[0] // groups
     out[:, 0:n, :] = early[:, 0:n, :]
-    put(out, n, n, -dot16(entry[1], arriving[0], TN))
+    put(out, n, n, jnp.where(is_last(place), 0.0, -dot16(entry[1], arriving[0], TN)))
     out[:, 2 * n : 2 * n + c, :] = early[:, n : n + c, :]
-    put(out, 2 * n + c, c, dot16(rhs[1], arriving[0], NN))
-    out[:, 2 * n + 2 * c :, :] = early[:, n + c :, :]
+    put(out, 2 * n + c, c, dot16(second[...], arriving[0], NN))
 
 
 def sum_kernel(place, parts, out):
@@ -110,16 +131,16 @@
 def pieces(whole):
     groups, rows, width = whole.shape
     n = width // groups
-    c = (rows - 2 * n) // 3
+    c = (rows - 2 * n) // 2
 
     def take(start, count):
         return whole[:, start : start + count, :].reshape(groups * count, width)
 
-    return take(0, n), take(n, n), take(2 * n, c), take(2 * n + c, c), take(2 * n + 2 * c, c)
-
-
-def is_first(place):
-    return (place[0] == 0) & (place[1] == 0) & (place[2] == 0)
+    return take(0, n), take(n, n), take(2 * n, c), take(2 * n + c, c)
+
+
+def is_last(place):
+    return (place[0] == 3) & (place[1] == 3) & (place[2] == 1)
 
 
 def after(earlier, later, n):
@@ -127,21 +148,23 @@
     return out[:n], out[n:] + later[n:]
 
 
-def local_kernel(place, whole, out):
-    couple0, couple1, source0, source1, opening = pieces(whole)
-    n = couple0.shape[0]
-    folded = dot32(opening, couple0, NN) + source0
-    source0 = jnp.where(is_first(place), folded, source0)
-    out[:n] = dot32(couple0, couple1, NN)
-    out[n:] = dot32(source0, couple1, NN) + source1
-
-
-def pair_kernel(place, mine, other, out):
-    n = mine.shape[1]
+def pair_kernel(place, mine, other, out, beside):
+    def own(whole):
+        couple0, couple1, source0, source1 = pieces(whole)
+        top, bottom = after(
+            jnp.concatenate([couple0, source0], axis=0),
+            jnp.concatenate([couple1, source1], axis=0),
+            couple0.shape[0],
+        )
+        return jnp.concatenate([top, bottom], axis=0)
+
+    here, there = own(mine), own(other)
+    n = here.shape[1]
     upper = place[2] == 1
-    first = jnp.where(upper, other[...], mine[...])
-    second = jnp.where(upper, mine[...], other[...])
+    first = jnp.where(upper, there, here)
+    second = jnp.where(upper, here, there)
     out[:n], out[n:] = after(first, second, n)
+    beside[...] = there
 
 
 def group_kernel(place, mine, one, two, three, total, before, slots):
@@ -179,13 +202,12 @@
 
 
 def tail_kernel(place, whole, other, before, maps, shifts):
-    couple0, _, source0, _, opening = pieces(whole)
+    couple0, _, source0, _ = pieces(whole)
     n = couple0.shape[0]
     reach, shift = after(before[...], other[...], n)
     upper = place[2] == 1
     reach = jnp.where(upper, reach, before[:n])
     shift = jnp.where(upper, shift, before[n:])
-    shift = jnp.where(is_first(place), opening, shift)
     out = dot32(jnp.concatenate([reach, shift], axis=0), couple0, NN)
     maps[:, :n] = reach
     maps[:, n:] = out[:n]
@@ -193,24 +215,30 @@
     shifts[:, n:] = out[n:] + source0
 
 
-def forward_kernel(place, maps, shifts, one, two, three, entry, turned, out):
+def forward_kernel(place, maps, shifts, own, one, two, three, entry, turned, out):
     n = one.shape[1]
     x = place[0]
-    state = jnp.where(3 <= x, three[n:], 0.0)
-    state = jnp.where(2 <= x, dot32(state, two[:n], NN) + two[n:], state)
-    state = jnp.where(1 <= x, dot32(state, one[:n], NN) + one[n:], state)
+    state = jnp.where(x == 3, own[n:], 0.0)
+    for d, ref in ((3, three), (2, two), (1, one)):
+        state = jnp.where(d <= x + 1, dot32(state, ref[:n], NN) + ref[n:], state)
     both = dot32(state, maps[...], NN) + shifts[...]
     states = jnp.concatenate([both[:, :n], both[:, n:]], axis=0)
-    high = states.astype(BF16)
-    rest = states - high.astype(F32)
-    middle = rest.astype(BF16)
-    low = (rest - middle.astype(F32)).astype(BF16)
+    high, middle, low = (part.astype(BF16) for part in three_parts(states))
+    factor = jnp.concatenate(
+        [
+            jnp.concatenate([high, low], axis=1),
+            jnp.concatenate([middle, jnp.zeros_like(middle)], axis=1),
+        ],
+        axis=0,
+    )
     lanes = lax.broadcasted_iota(jnp.int32, out.shape, 1)
+    width = states.shape[0]
 
     def through(i):
-        return (dot16(entry[i], low, NT) + dot16(entry[i], middle, NT)) + dot16(entry[i], high, NT)
-
-    product = jnp.where(lanes < both.shape[0], through(0), through(1))
+        product = dot16(jnp.concatenate([entry[i], entry[i]], axis=1), factor, NT)
+        return product[:, width:] + product[:, :width]
+
+    product = jnp.where(lanes < width // 2, through(0), through(1))
     out[...] = (turned[...] - product).astype(BF16)
 
 
@@ -227,8 +255,9 @@
     put(carried, c, c, dot16(low, entry[1], TN)[half:])
 
 
-def routes_kernel(place, whole, other, before, y1, y2, y3, x1, x2, x3, leave, reach):
-    couple0, couple1, _, _, _ = pieces(whole)
+def routes_kernel(place, whole, other, before, y1, y2, y3, x1, x2, x3, applied, leave, reach, turned):
+    couple0, couple1, _, _ = pieces(whole)
+    turned[...] = applied[...].T
     n = couple0.shape[0]
     rows = lax.broadcasted_iota(jnp.int32, (n, n), 0)
     lanes = lax.broadcasted_iota(jnp.int32, (n, n), 1)
@@ -237,10 +266,8 @@
     lower = jnp.where(core == 1, other[:n], identity)
     out = dot32(lower, couple0, NN)
     chip = jnp.concatenate([lower, out], axis=1)
-    leave[0:n, :n] = identity
-    leave[0:n, n:] = couple0
-    leave[n : 2 * n, :] = chip
-    leave[2 * n : 3 * n, :] = dot32(before[:n], chip, NN)
+    top = jnp.concatenate([identity, couple0], axis=1)
+    store_parts(leave, jnp.concatenate([top, chip, dot32(before[:n], chip, NN)], axis=0))
     here = jnp.where(core == 0, other[:n], identity)
     blocks = [identity]
     for e, ref in ((1, y3), (2, y2), (3, y1)):
@@ -251,8 +278,7 @@
         if e < 3:
             here = dot32(here, ref[:n], NN)
     stacked = jnp.concatenate(blocks, axis=1)
-    reach[:n, :] = stacked
-    reach[n:, :] = dot32(couple1, stacked, NN)
+    store_parts(reach, jnp.concatenate([stacked, dot32(couple1, stacked, NN)], axis=0))
 
 
 def back_kernel(place, parts, leave, carried, send):
@@ -263,7 +289,7 @@
     carried[...] = total
     n = total.shape[1]
     x, y = place[0], place[1]
-    values = dot32(jnp.concatenate([total[:c], total[c:]], axis=1), leave[...], NT)
+    values = dot_parts(jnp.concatenate([total[:c], total[c:]], axis=1), leave, NT)
     own, chip, group = values[:, :n], values[:, n : 2 * n], values[:, 2 * n :]
     for k in range(send.shape[0]):
         same_x = x == k // 8
@@ -285,7 +311,7 @@
         for k in range(1, 8):
             extra = extra + got[base + k]
         terms.append(jnp.where(x + e <= 3, extra, 0.0))
-    values = dot32(jnp.concatenate(terms, axis=1), reach[...], NT)
+    values = dot_parts(jnp.concatenate(terms, axis=1), reach, NT)
     state = values[:, :n]
     inner = values[:, n:] + carried[c:]
     for k in range(out.shape[0]):
@@ -293,12 +319,11 @@
         out[k, c:] = state
 
 
-def final_kernel(place, got, applied, exit_, arriving, out):
+def final_kernel(place, got, turned, exit_, arriving, out):
     groups, rows, width = got.shape
     c = rows // 2
     inner = got[:, :c, :].reshape(groups * c, width)
     outer = got[:, c:, :].reshape(groups * c, width)
-    turned = applied[...].T
     out[0] = turned[: groups * c] - dot32_16(inner, exit_[1], NT)
     out[1] = turned[groups * c :] - dot32_16(outer, arriving[0], NT)
 
@@ -321,30 +346,33 @@
     n = entry.shape[2]
     place = jnp.stack([lax.axis_index(X), lax.axis_index(Y), lax.axis_index(CORE)]).astype(jnp.int32)
     chain = lax.axis_size(CHAIN)
-    arriving = lax.ppermute(exit_[:1], CHAIN, [(i, i - 1) for i in range(1, chain)])
-    rows = (2 * n + 3 * cols) // z
-    entry_v, exit_v, rhs_v, turned, early = call(
+    arriving = lax.ppermute(exit_[:1], CHAIN, [(i, (i - 1) % chain) for i in range(chain)])
+    rows = (2 * n + 2 * cols) // z
+    entry_v, exit_v, second, turned, early = call(
         load_kernel,
         place,
         [pltpu.with_memory_space_constraint(a, pltpu.HBM) for a in (entry, exit_, rhs, previous)],
         (
             of(entry.shape, BF16),
             of(exit_.shape, BF16),
-            of(rhs.shape, BF16),
+            of(previous.shape, BF16),
             of((local, 2 * cols)),
-            of((z, (n + 2 * cols) // z, n)),
+            of((z, (n + cols) // z, n)),
         ),
-        [pltpu.VMEM(previous.shape, BF16), pltpu.SemaphoreType.DMA((4,))],
+        [
+            pltpu.VMEM(rhs.shape, BF16),
+            pltpu.VMEM(previous.shape, BF16),
+            pltpu.SemaphoreType.DMA((4,)),
+        ],
         [hbm()] * 4,
         cost=1 << 28,
     )
-    parts = call(partial_kernel, place, (entry_v, arriving, rhs_v, early), of((z, rows, n)))
+    parts = call(partial_kernel, place, (entry_v, arriving, second, early), of((z, rows, n)))
     summed = call(sum_kernel, place, (exchange(parts, COL),), of((z, rows, n)))
     whole = exchange(summed, COL)
     maps = of((n + cols, n))
-    mine = call(local_kernel, place, (whole,), maps)
-    other = lax.ppermute(mine, CORE, [(0, 1), (1, 0)])
-    chip = call(pair_kernel, place, (mine, other), maps)
+    whole_other = lax.ppermute(whole, CORE, [(0, 1), (1, 0)])
+    chip, other = call(pair_kernel, place, (whole, whole_other), (maps, maps))
     y1, y2, y3 = ring(chip, Y)
     group, before = call(
         group_kernel, place, (chip, y1, y2, y3), (maps, maps), [pltpu.VMEM((4, n + cols, n), F32)]
@@ -356,15 +384,8 @@
     forward = call(
         forward_kernel,
         place,
-        (ahead, shifts, x1, x2, x3, entry_v, turned),
+        (ahead, shifts, group, x1, x2, x3, entry_v, turned),
         of((local, 2 * cols), BF16),
-    )
-    leave, reach = call(
-        routes_kernel,
-        place,
-        (whole, other, before, y1, y2, y3, x1, x2, x3),
-        (of((3 * n, 2 * n)), of((2 * n, 7 * n))),
-        cost=1 << 29,
     )
     gathered = exchange(jnp.broadcast_to(forward, (z, *forward.shape)), COL)
     c = cols // z
@@ -374,6 +395,13 @@
         (gathered, block_inverse, entry_v),
         (of((local, 2 * cols)), of((z, 2 * c, n))),
     )
+    leave, reach, applied_turned = call(
+        routes_kernel,
+        place,
+        (whole, other, before, y1, y2, y3, x1, x2, x3, applied),
+        (of((3, 3 * n, 2 * n), BF16), of((3, 2 * n, 7 * n), BF16), of((2 * cols, local))),
+        cost=1 << 29,
+    )
     carried, send = call(
         back_kernel,
         place,
@@ -386,7 +414,7 @@
     return call(
         final_kernel,
         place,
-        (exchange(behind, COL), applied, exit_v, arriving),
+        (exchange(behind, COL), applied_turned, exit_v, arriving),
         of((here, cols, local)),
     )
 

time: 129 us -> 127 us (0.984)
  blocking collectives: 80 us -> 74.1 us
  waiting for transfers between devices: 10.8 us -> 15.6 us
  starting transfers between devices: 18.8 us -> 17.2 us
    all_to_all x5, blocking collectives: 80 us -> 74.1 us  [exchange(): return lax.all_to_all(value, axes, split_axis=0, concat_axis=0, tiled=True)]
    ppermute x6, waiting for transfers between devices: 4.69 us -> 10.1 us  [ring(): lax.ppermute(value, axis, [(i, (i + d) % size) for i in range(size)])]
    ppermute x6, starting transfers between devices: 12.6 us -> 7.83 us  [ring(): lax.ppermute(value, axis, [(i, (i + d) % size) for i in range(size)])]
    ppermute x2, starting transfers between devices: 1.48 us -> 4.65 us  [the longest x1 4.65 us: shards(): lax.ppermute(exit_[:1], CHAIN, [(i, (i - 1) % chain) for i in range(chain)])]
    pallas_call x13 -> x12, Pallas kernels: 17 us -> 16.2 us  [call(): pl.pallas_call(kernel, out_shape=outs, in_specs=[smem()] + (specs or [vme...]
  transfers between devices with their start and end apart: 9 -> 9, of which waited for: 5 -> 9; matrix products, arithmetic and copies ran while one was open for 0% -> 0% of each run, Pallas kernels for 4% -> 4%
where the time goes in v3:
time: 127 us; the launch traced here: 125 us
  blocking collectives  74.1 us (58%)
  starting transfers between devices  17.2 us (14%)
  Pallas kernels  16.2 us (13%)
  waiting for transfers between devices  15.6 us (12%)
  local copies, waits for them, and re-layouts  1.88 us (1%)
    all_to_all x5, blocking collectives, exchange(): return lax.all_to_all(value, axes, split_axis=0, concat_axis=0, tiled=True)  74.1 us
    pallas_call x12, Pallas kernels, call(): pl.pallas_call(kernel, out_shape=outs, in_specs=[smem()] + (specs or [vme...  16.2 us
    ppermute x6, waiting for transfers between devices, ring(): lax.ppermute(value, axis, [(i, (i + d) % size) for i in range(size)])  10.1 us
    ppermute x6, starting transfers between devices, ring(): lax.ppermute(value, axis, [(i, (i + d) % size) for i in range(size)])  7.83 us
    all_to_all x1, starting transfers between devices, exchange(): return lax.all_to_all(value, axes, split_axis=0, concat_axis=0, tiled=True)  4.71 us
    ppermute x1, starting transfers between devices, shards(): lax.ppermute(exit_[:1], CHAIN, [(i, (i - 1) % chain) for i in range(chain)])  4.65 us
    all_to_all x1, waiting for transfers between devices, exchange(): return lax.all_to_all(value, axes, split_axis=0, concat_axis=0, tiled=True)  3.94 us
  transfers between devices with their start and end apart: 9, of which 9 were waited for; matrix products, arithmetic and copies ran while one was open for 0% of the time, Pallas kernels for 4%

profile of v3, /device:TPU:32, one launch (start us, length us, event | category | flops | bytes accessed | tf_op | source)
XLA Modules:
  0.0 125.1 jit_solution(10912772146932747225)
XLA Ops:
  0.0 0.9 slice.3
  0.9 4.6 %collective-permute-start = (bf16[1,320,128]{2,1,0:T(8,128)(2,1)S(1)}, bf16[1,320,128]{2,1,0:T(8,128)(2,1)S(1)}, u32[]{:S(2)}, u32[]{:S(2)}) collective-permute-start(bf16[1,320,128]{2,1,0:T(8,128)(2,1)S(1)} %slice.3), channel_id=1, source_target_pairs={{0,248},{8,0},{16,8},{24,16},{32,24},{40,32},{48,40},{56,48},{64,5... | collective-permute-start | bytes 245768 | tf_op jit(solution)/shard_map/ppermute | solution.py:349
  5.6 1.9 %shard_map.55 = (bf16[2,320,128]{2,1,0:T(8,128)(2,1)S(1)}, bf16[2,320,128]{2,1,0:T(8,128)(2,1)S(1)}, bf16[64,320]{1,0:T(8,128)(2,1)S(1)}, f32[320,128]{1,0:T(8,128)S(1)}, f32[8,24,128]{2,1,0:T(8,128)S(1)}) custom-call(s32[3]{0:T(128)S(1)} %pad_add_fusion.place, bf16[2,320,128]{2,1,0:T(8,128)(2,1)} %entry.1, bf16[2,320,128]{2,1,0:T(8,128)(2,1)} %exit_.1, ...), custom_call_target="tpu_custom_call" | custom-call | flops 268435456 | bytes 2684354 | tf_op jit(solution)/shard_map/pallas_call | solution.py:71
  7.6 0.8 shard_map.56
  8.4 16.7 %all_to_all.30.parts = f32[8,48,128]{2,1,0:T(8,128)S(1)} all-to-all(f32[8,48,128]{2,1,0:T(8,128)S(1)} %shard_map.56), channel_id=1, replica_groups=mesh['chain_0'=4,'chain_1'=4,'chain_2'=2,'col'=8] {'col'}, dimensions={0} | all-to-all | bytes 393216 | tf_op jit(solution)/shard_map/all_to_all | solution.py:332
  25.6 12.3 %all_to_all.31.mine.whole = f32[8,48,128]{2,1,0:T(8,128)S(1)} all-to-all(f32[8,48,128]{2,1,0:T(8,128)S(1)} %shard_map.57), channel_id=1, replica_groups=mesh['chain_0'=4,'chain_1'=4,'chain_2'=2,'col'=8] {'col'}, dimensions={0} | all-to-all | bytes 393216 | tf_op jit(solution)/shard_map/all_to_all | solution.py:332
  37.9 1.4 %collective-permute-done.1.other = f32[8,48,128]{2,1,0:T(8,128)S(1)} collective-permute-done((f32[8,48,128]{2,1,0:T(8,128)S(1)}, f32[8,48,128]{2,1,0:T(8,128)S(1)}, u32[]{:S(2)}, u32[]{:S(2)}) %collective-permute-start.1) | collective-permute-done | bytes 196640 | tf_op jit(solution)/shard_map/ppermute | solution.py:374
  39.4 1.2 shard_map.58
  40.9 1.9 %collective-permute-start.3 = (f32[192,128]{1,0:T(8,128)S(1)}, f32[192,128]{1,0:T(8,128)S(1)}, u32[]{:S(2)}, u32[]{:S(2)}) collective-permute-start(f32[192,128]{1,0:T(8,128)S(1)} %get-tuple-element.27.mine), channel_id=1, source_target_pairs={{0,32},{16,48},{32,0},{48,16},{1,33},{17,49},{33,1},{49,17},{2,34}... | collective-permute-start | bytes 294920 | tf_op jit(solution)/shard_map/ppermute | solution.py:338
  42.8 1.1 collective-permute-start.2
  43.9 2.4 %collective-permute-done.4.three.y3 = f32[192,128]{1,0:T(8,128)S(1)} collective-permute-done((f32[192,128]{1,0:T(8,128)S(1)}, f32[192,128]{1,0:T(8,128)S(1)}, u32[]{:S(2)}, u32[]{:S(2)}) %collective-permute-start.4) | collective-permute-done | bytes 98336 | tf_op jit(solution)/shard_map/ppermute | solution.py:338
  46.3 1.1 collective-permute-done.3.two.y2
  47.4 1.9 %collective-permute-done.2.one.y1 = f32[192,128]{1,0:T(8,128)S(1)} collective-permute-done((f32[192,128]{1,0:T(8,128)S(1)}, f32[192,128]{1,0:T(8,128)S(1)}, u32[]{:S(2)}, u32[]{:S(2)}) %collective-permute-start.2) | collective-permute-done | bytes 98336 | tf_op jit(solution)/shard_map/ppermute | solution.py:338
  49.3 1.2 shard_map.59
  50.5 2.9 %collective-permute-start.7 = (f32[192,128]{1,0:T(8,128)S(1)}, f32[192,128]{1,0:T(8,128)S(1)}, u32[]{:S(2)}, u32[]{:S(2)}) collective-permute-start(f32[192,128]{1,0:T(8,128)S(1)} %get-tuple-element.31.own), channel_id=1, source_target_pairs={{0,192},{64,0},{128,64},{192,128},{1,193},{65,1},{129,65},{193,129... | collective-permute-start | bytes 294920 | tf_op jit(solution)/shard_map/ppermute | solution.py:338
  54.1 0.9 collective-permute-start.5
  55.0 1.1 shard_map.60
  56.1 1.1 collective-permute-done.7.three.x3
  57.2 2.6 %collective-permute-done.6.two.x2 = f32[192,128]{1,0:T(8,128)S(1)} collective-permute-done((f32[192,128]{1,0:T(8,128)S(1)}, f32[192,128]{1,0:T(8,128)S(1)}, u32[]{:S(2)}, u32[]{:S(2)}) %collective-permute-start.6) | collective-permute-done | bytes 98336 | tf_op jit(solution)/shard_map/ppermute | solution.py:338
  59.9 1.0 collective-permute-done.5.one.x1
  60.9 1.7 %shard_map.61 = bf16[320,128]{1,0:T(8,128)(2,1)S(1)} custom-call(s32[3]{0:T(128)S(1)} %pad_add_fusion.place, f32[128,256]{1,0:T(8,128)S(1)} %get-tuple-element.29.maps, f32[64,256]{1,0:T(8,128)S(1)} %get-tuple-element.30.shifts, f32[192,128]{1,0:T(8,128)S(1)} %get-tuple-element.31.own, f32[192,128]{1,0:T(8,128)S(1)} %collective-permute-done.5.one.x1, ...), custom_call_target="tpu_custom_call" | custom-call | tf_op jit(solution)/shard_map/pallas_call | solution.py:71
  62.6 21.4 %all_to_all.32.forward = bf16[8,320,128]{2,1,0:T(8,128)(2,1)S(1)} all-to-all(bf16[8,320,128]{2,1,0:T(8,128)(2,1)S(1)} %broadcast_in_dim.3), channel_id=1, replica_groups=mesh['chain_0'=4,'chain_1'=4,'chain_2'=2,'col'=8] {'col'}, dimensions={0} | all-to-all | bytes 1310720 | tf_op jit(solution)/shard_map/all_to_all | solution.py:332
  84.0 2.4 %shard_map.62 = (f32[320,128]{1,0:T(8,128)S(1)}, f32[8,16,128]{2,1,0:T(8,128)}) custom-call(s32[3]{0:T(128)S(1)} %pad_add_fusion.place, bf16[8,320,128]{2,1,0:T(8,128)(2,1)S(1)} %all_to_all.32.forward, bf16[2,320,2560]{2,1,0:T(8,128)(2,1)S(1)} %copy-done, bf16[2,320,128]{2,1,0:T(8,128)(2,1)S(1)} %get-tuple-element.23.entry), custom_call_target="tpu_custom_call" | custom-call | tf_op jit(solution)/shard_map/pallas_call | solution.py:71
  86.4 4.7 %all-to-all-start.3 = ((f32[8,16,128]{2,1,0:T(8,128)}), f32[8,16,128]{2,1,0:T(8,128)S(1)}, u32[]{:S(2)}, u32[]{:S(2)}) async-start(f32[8,16,128]{2,1,0:T(8,128)} %get-tuple-element.33), calls=%async_computation.3 | async-start | bytes 131072 | tf_op jit(solution)/shard_map/all_to_all | solution.py:332
  91.2 0.9 copy-done.2
  92.1 2.1 %shard_map.63 = (bf16[3,384,256]{2,1,0:T(8,128)(2,1)S(1)}, bf16[3,256,896]{2,1,0:T(8,128)(2,1)S(1)}, f32[128,320]{1,0:T(8,128)S(1)}) custom-call(s32[3]{0:T(128)S(1)} %pad_add_fusion.place, f32[8,48,128]{2,1,0:T(8,128)S(1)} %all_to_all.31.mine.whole, f32[192,128]{1,0:T(8,128)S(1)} %get-tuple-element.26.other, f32[192,128]{1,0:T(8,128)S(1)} %copy-done.2, ...), custom_call_target="tpu_custom_call" | custom-call | flops 536870912 | bytes 5368709 | tf_op jit(solution)/shard_map/pallas_call | solution.py:71
  94.2 3.9 %all-to-all-done.3.parts = f32[8,16,128]{2,1,0:T(8,128)S(1)} async-done(((f32[8,16,128]{2,1,0:T(8,128)}), f32[8,16,128]{2,1,0:T(8,128)S(1)}, u32[]{:S(2)}, u32[]{:S(2)}) %all-to-all-start.3) | async-done | bytes 65568 | tf_op jit(solution)/shard_map/all_to_all | solution.py:332
  98.1 0.8 shard_map.64
  98.9 12.9 %all_to_all.33.got = f32[32,8,128]{2,1,0:T(8,128)S(1)} all-to-all(f32[32,8,128]{2,1,0:T(8,128)S(1)} %get-tuple-element.36), channel_id=1, replica_groups=mesh['chain_0'=4,'chain_1'=4,'chain_2'=2,'col'=8] {'chain_0','chain_1','..., dimensions={0} | all-to-all | bytes 262144 | tf_op jit(solution)/shard_map/all_to_all | solution.py:332
  111.9 1.0 shard_map.65
  112.9 10.7 %all_to_all.34.got = f32[8,16,128]{2,1,0:T(8,128)S(1)} all-to-all(f32[8,16,128]{2,1,0:T(8,128)S(1)} %shard_map.65), channel_id=1, replica_groups=mesh['chain_0'=4,'chain_1'=4,'chain_2'=2,'col'=8] {'col'}, dimensions={0} | all-to-all | bytes 131072 | tf_op jit(solution)/shard_map/all_to_all | solution.py:332
  123.7 1.5 %shard_map.66 = f32[2,64,320]{2,1,0:T(8,128)} custom-call(s32[3]{0:T(128)S(1)} %pad_add_fusion.place, f32[8,16,128]{2,1,0:T(8,128)S(1)} %all_to_all.34.got, f32[128,320]{1,0:T(8,128)S(1)} %get-tuple-element.39.turned, bf16[2,320,128]{2,1,0:T(8,128)(2,1)S(1)} %get-tuple-element.40.exit_, bf16[1,320,128]{2,1,0:T(8,128)(2,1)S(1)} %collective-permute-done.arriving), custom_call_target="tpu_custom_call" | custom-call | tf_op jit(solution)/shard_map/pallas_call | solution.py:71
  (12 shorter events, 1.9 us)
Async XLA Ops:
  0.9 6.7 %collective-permute-start = (bf16[1,320,128]{2,1,0:T(8,128)(2,1)S(1)}, bf16[1,320,128]{2,1,0:T(8,128)(2,1)S(1)}, u32[]{:S(2)}, u32[]{:S(2)}) collective-permute-start(bf16[1,320,128]{2,1,0:T(8,128)(2,1)S(1)} %slice.3), channel_id=1, source_target_pairs={{0,248},{8,0},{16,8},{24,16},{32,24},{40,32},{48,40},{56,48},{64,5... | collective-permute-start | bytes 245768 | tf_op jit(solution)/shard_map/ppermute | solution.py:349
  7.5 76.5 %copy-start = (bf16[2,320,2560]{2,1,0:T(8,128)(2,1)S(1)}, bf16[2,320,2560]{2,1,0:T(8,128)(2,1)}, u32[]{:S(2)}) copy-start(bf16[2,320,2560]{2,1,0:T(8,128)(2,1)} %inverse.1) | copy-start | bytes 9830404
  37.9 1.4 %collective-permute-start.1 = (f32[8,48,128]{2,1,0:T(8,128)S(1)}, f32[8,48,128]{2,1,0:T(8,128)S(1)}, u32[]{:S(2)}, u32[]{:S(2)}) collective-permute-start(f32[8,48,128]{2,1,0:T(8,128)S(1)} %all_to_all.31.mine.whole), channel_id=1, source_target_pairs={{0,8},{8,0},{1,9},{9,1},{2,10},{10,2},{3,11},{11,3},{4,12},{12,4},... | collective-permute-start | bytes 589832 | tf_op jit(solution)/shard_map/ppermute | solution.py:374
  40.6 5.7 %collective-permute-start.4 = (f32[192,128]{1,0:T(8,128)S(1)}, f32[192,128]{1,0:T(8,128)S(1)}, u32[]{:S(2)}, u32[]{:S(2)}) collective-permute-start(f32[192,128]{1,0:T(8,128)S(1)} %get-tuple-element.27.mine), channel_id=1, source_target_pairs={{0,48},{16,0},{32,16},{48,32},{1,49},{17,1},{33,17},{49,33},{2,50}... | collective-permute-start | bytes 294920 | tf_op jit(solution)/shard_map/ppermute | solution.py:338
  40.9 6.5 %collective-permute-start.3 = (f32[192,128]{1,0:T(8,128)S(1)}, f32[192,128]{1,0:T(8,128)S(1)}, u32[]{:S(2)}, u32[]{:S(2)}) collective-permute-start(f32[192,128]{1,0:T(8,128)S(1)} %get-tuple-element.27.mine), channel_id=1, source_target_pairs={{0,32},{16,48},{32,0},{48,16},{1,33},{17,49},{33,1},{49,17},{2,34}... | collective-permute-start | bytes 294920 | tf_op jit(solution)/shard_map/ppermute | solution.py:338
  42.8 6.5 %collective-permute-start.2 = (f32[192,128]{1,0:T(8,128)S(1)}, f32[192,128]{1,0:T(8,128)S(1)}, u32[]{:S(2)}, u32[]{:S(2)}) collective-permute-start(f32[192,128]{1,0:T(8,128)S(1)} %get-tuple-element.27.mine), channel_id=1, source_target_pairs={{0,16},{16,32},{32,48},{48,0},{1,17},{17,33},{33,49},{49,1},{2,18}... | collective-permute-start | bytes 294920 | tf_op jit(solution)/shard_map/ppermute | solution.py:338
  50.5 12.1 %copy-start.1 = (f32[192,128]{1,0:T(8,128)}, f32[192,128]{1,0:T(8,128)S(1)}, u32[]{:S(2)}) copy-start(f32[192,128]{1,0:T(8,128)S(1)} %get-tuple-element.28.before) | copy-start | bytes 294916
  50.5 6.7 %collective-permute-start.7 = (f32[192,128]{1,0:T(8,128)S(1)}, f32[192,128]{1,0:T(8,128)S(1)}, u32[]{:S(2)}, u32[]{:S(2)}) collective-permute-start(f32[192,128]{1,0:T(8,128)S(1)} %get-tuple-element.31.own), channel_id=1, source_target_pairs={{0,192},{64,0},{128,64},{192,128},{1,193},{65,1},{129,65},{193,129... | collective-permute-start | bytes 294920 | tf_op jit(solution)/shard_map/ppermute | solution.py:338
  53.4 6.5 %collective-permute-start.6 = (f32[192,128]{1,0:T(8,128)S(1)}, f32[192,128]{1,0:T(8,128)S(1)}, u32[]{:S(2)}, u32[]{:S(2)}) collective-permute-start(f32[192,128]{1,0:T(8,128)S(1)} %get-tuple-element.31.own), channel_id=1, source_target_pairs={{0,128},{64,192},{128,0},{192,64},{1,129},{65,193},{129,1},{193,65... | collective-permute-start | bytes 294920 | tf_op jit(solution)/shard_map/ppermute | solution.py:338
  54.1 6.7 %collective-permute-start.5 = (f32[192,128]{1,0:T(8,128)S(1)}, f32[192,128]{1,0:T(8,128)S(1)}, u32[]{:S(2)}, u32[]{:S(2)}) collective-permute-start(f32[192,128]{1,0:T(8,128)S(1)} %get-tuple-element.31.own), channel_id=1, source_target_pairs={{0,64},{64,128},{128,192},{192,0},{1,65},{65,129},{129,193},{193,1... | collective-permute-start | bytes 294920 | tf_op jit(solution)/shard_map/ppermute | solution.py:338
  86.4 11.7 %all-to-all-start.3 = ((f32[8,16,128]{2,1,0:T(8,128)}), f32[8,16,128]{2,1,0:T(8,128)S(1)}, u32[]{:S(2)}, u32[]{:S(2)}) async-start(f32[8,16,128]{2,1,0:T(8,128)} %get-tuple-element.33), calls=%async_computation.3 | async-start | bytes 131072 | tf_op jit(solution)/shard_map/all_to_all | solution.py:332
  91.2 0.9 copy-start.2

commit v4 on v3

--- a/solution.py
+++ b/solution.py
@@ -242,22 +242,26 @@
     out[...] = (turned[...] - product).astype(BF16)
 
 
-def apply_kernel(place, forward, inverse, entry, applied, carried):
-    groups, local, both = forward.shape
-    whole = forward[...].reshape(groups * local, both)
-    lanes = lax.broadcasted_iota(jnp.int32, applied.shape, 1)
+def apply_kernel(place, *refs):
+    groups = len(refs) - 5
+    blocks = refs[:groups]
+    inverse, entry, turned, carried, slots = refs[groups:]
+    local, both = blocks[0].shape
+    for d, block in enumerate(blocks):
+        slots[lax.rem(place[3] - d + groups, groups)] = block[...]
+    whole = slots[...].reshape(groups * local, both)
+    lanes = lax.broadcasted_iota(jnp.int32, (local, both), 1)
     half = both // 2
     value = jnp.where(lanes < half, dot16(inverse[0], whole, NN), dot16(inverse[1], whole, NN))
-    applied[...] = value
+    turned[...] = value.T
     low = value.astype(BF16)
     c = half // groups
     put(carried, 0, c, dot16(low, entry[0], TN)[:half])
     put(carried, c, c, dot16(low, entry[1], TN)[half:])
 
 
-def routes_kernel(place, whole, other, before, y1, y2, y3, x1, x2, x3, applied, leave, reach, turned):
+def routes_kernel(place, whole, other, before, y1, y2, y3, x1, x2, x3, leave, reach):
     couple0, couple1, _, _ = pieces(whole)
-    turned[...] = applied[...].T
     n = couple0.shape[0]
     rows = lax.broadcasted_iota(jnp.int32, (n, n), 0)
     lanes = lax.broadcasted_iota(jnp.int32, (n, n), 1)
@@ -344,7 +348,7 @@
     z = lax.axis_size(COL)
     here, cols, local = rhs.shape
     n = entry.shape[2]
-    place = jnp.stack([lax.axis_index(X), lax.axis_index(Y), lax.axis_index(CORE)]).astype(jnp.int32)
+    place = jnp.stack([lax.axis_index(X), lax.axis_index(Y), lax.axis_index(CORE), lax.axis_index(COL)]).astype(jnp.int32)
     chain = lax.axis_size(CHAIN)
     arriving = lax.ppermute(exit_[:1], CHAIN, [(i, (i - 1) % chain) for i in range(chain)])
     rows = (2 * n + 2 * cols) // z
@@ -387,20 +391,32 @@
         (ahead, shifts, group, x1, x2, x3, entry_v, turned),
         of((local, 2 * cols), BF16),
     )
-    gathered = exchange(jnp.broadcast_to(forward, (z, *forward.shape)), COL)
+    up = [(i, (i + 1) % z) for i in range(z)]
+    down = [(i, (i - 1) % z) for i in range(z)]
+    far = [(i, (i + z // 2) % z) for i in range(z)]
+    blocks = [forward] + [None] * (z - 1)
+    blocks[1] = lax.ppermute(forward, COL, up)
+    blocks[7] = lax.ppermute(forward, COL, down)
+    blocks[4] = lax.ppermute(forward, COL, far)
+    blocks[2] = lax.ppermute(blocks[1], COL, up)
+    blocks[6] = lax.ppermute(blocks[7], COL, down)
+    leave, reach = call(
+        routes_kernel,
+        place,
+        (whole, other, before, y1, y2, y3, x1, x2, x3),
+        (of((3, 3 * n, 2 * n), BF16), of((3, 2 * n, 7 * n), BF16)),
+        cost=1 << 29,
+    )
+    blocks[2], blocks[6], leave, reach = lax.optimization_barrier((blocks[2], blocks[6], leave, reach))
+    blocks[3] = lax.ppermute(blocks[2], COL, up)
+    blocks[5] = lax.ppermute(blocks[6], COL, down)
     c = cols // z
-    applied, carried_parts = call(
+    turned_applied, carried_parts = call(
         apply_kernel,
         place,
-        (gathered, block_inverse, entry_v),
-        (of((local, 2 * cols)), of((z, 2 * c, n))),
-    )
-    leave, reach, applied_turned = call(
-        routes_kernel,
-        place,
-        (whole, other, before, y1, y2, y3, x1, x2, x3, applied),
-        (of((3, 3 * n, 2 * n), BF16), of((3, 2 * n, 7 * n), BF16), of((2 * cols, local))),
-        cost=1 << 29,
+        (*blocks, block_inverse, entry_v),
+        (of((2 * cols, local)), of((z, 2 * c, n))),
+        [pltpu.VMEM((z, local, 2 * cols), BF16)],
     )
     carried, send = call(
         back_kernel,
@@ -414,7 +430,7 @@
     return call(
         final_kernel,
         place,
-        (exchange(behind, COL), applied_turned, exit_v, arriving),
+        (exchange(behind, COL), turned_applied, exit_v, arriving),
         of((here, cols, local)),
     )
 

time: 127 us -> 124 us (0.976)
  blocking collectives: 74.1 us -> 68.2 us
  starting transfers between devices: 17.2 us -> 20.3 us
    ppermute x0 -> x7, waiting for transfers between devices: none -> 8.26 us  [the longest x1 3.11 us: shards(): blocks[7] = lax.ppermute(forward, COL, down)]
    ppermute x0 -> x7, starting transfers between devices: none -> 7.12 us  [the longest x1 1.53 us: shards(): blocks[7] = lax.ppermute(forward, COL, down)]
    all_to_all x5, blocking collectives: 74.1 us -> 68.2 us  [exchange(): return lax.all_to_all(value, axes, split_axis=0, concat_axis=0, tiled=True)]
    all_to_all x1 -> x0, starting transfers between devices: 4.71 us -> none  [exchange(): return lax.all_to_all(value, axes, split_axis=0, concat_axis=0, tiled=True)]
    all_to_all x1 -> x0, waiting for transfers between devices: 3.94 us -> none  [exchange(): return lax.all_to_all(value, axes, split_axis=0, concat_axis=0, tiled=True)]
    ppermute x6, waiting for transfers between devices: 10.1 us -> 6.99 us  [ring(): lax.ppermute(value, axis, [(i, (i + d) % size) for i in range(size)])]
  transfers between devices with their start and end apart: 9 -> 15, of which waited for: 9 -> 12; matrix products, arithmetic and copies ran while one was open for 0% -> 0% of each run, Pallas kernels for 4% -> 4%
where the time goes in v4:
time: 124 us; the launch traced here: 122 us
  blocking collectives  68.2 us (55%)
  starting transfers between devices  20.3 us (16%)
  waiting for transfers between devices  16.8 us (14%)
  Pallas kernels  15.6 us (13%)
    all_to_all x5, blocking collectives, exchange(): return lax.all_to_all(value, axes, split_axis=0, concat_axis=0, tiled=True)  68.2 us
    pallas_call x12, Pallas kernels, call(): pl.pallas_call(kernel, out_shape=outs, in_specs=[smem()] + (specs or [vme...  15.6 us
    ppermute x6, starting transfers between devices, ring(): lax.ppermute(value, axis, [(i, (i + d) % size) for i in range(size)])  8.55 us
    ppermute x6, waiting for transfers between devices, ring(): lax.ppermute(value, axis, [(i, (i + d) % size) for i in range(size)])  6.99 us
    ppermute x1, starting transfers between devices, shards(): lax.ppermute(exit_[:1], CHAIN, [(i, (i - 1) % chain) for i in range(chain)])  4.65 us
    ppermute x1, waiting for transfers between devices, shards(): blocks[7] = lax.ppermute(forward, COL, down)  3.11 us
  transfers between devices with their start and end apart: 15, of which 12 were waited for; matrix products, arithmetic and copies ran while one was open for 0% of the time, Pallas kernels for 4%

profile of v4, /device:TPU:32, one launch (start us, length us, event | category | flops | bytes accessed | tf_op | source)
XLA Modules:
  0.0 122.0 jit_solution(5366277372801151159)
XLA Ops:
  0.0 0.9 slice.3
  0.9 4.6 %collective-permute-start = (bf16[1,320,128]{2,1,0:T(8,128)(2,1)S(1)}, bf16[1,320,128]{2,1,0:T(8,128)(2,1)S(1)}, u32[]{:S(2)}, u32[]{:S(2)}) collective-permute-start(bf16[1,320,128]{2,1,0:T(8,128)(2,1)S(1)} %slice.3), channel_id=1, source_target_pairs={{0,248},{8,0},{16,8},{24,16},{32,24},{40,32},{48,40},{56,48},{64,5... | collective-permute-start | bytes 245768 | tf_op jit(solution)/shard_map/ppermute | solution.py:353
  5.6 1.9 %shard_map.55 = (bf16[2,320,128]{2,1,0:T(8,128)(2,1)S(1)}, bf16[2,320,128]{2,1,0:T(8,128)(2,1)S(1)}, bf16[64,320]{1,0:T(8,128)(2,1)S(1)}, f32[320,128]{1,0:T(8,128)S(1)}, f32[8,24,128]{2,1,0:T(8,128)S(1)}) custom-call(s32[4]{0:T(128)S(1)} %pad_add_fusion.place, bf16[2,320,128]{2,1,0:T(8,128)(2,1)} %entry.1, bf16[2,320,128]{2,1,0:T(8,128)(2,1)} %exit_.1, ...), custom_call_target="tpu_custom_call" | custom-call | flops 268435456 | bytes 2684354 | tf_op jit(solution)/shard_map/pallas_call | solution.py:71
  8.4 16.7 %all_to_all.25.parts = f32[8,48,128]{2,1,0:T(8,128)S(1)} all-to-all(f32[8,48,128]{2,1,0:T(8,128)S(1)} %shard_map.56), channel_id=1, replica_groups=mesh['chain_0'=4,'chain_1'=4,'chain_2'=2,'col'=8] {'col'}, dimensions={0} | all-to-all | bytes 393216 | tf_op jit(solution)/shard_map/all_to_all | solution.py:336
  25.6 12.3 %all_to_all.26.mine.whole = f32[8,48,128]{2,1,0:T(8,128)S(1)} all-to-all(f32[8,48,128]{2,1,0:T(8,128)S(1)} %shard_map.57), channel_id=1, replica_groups=mesh['chain_0'=4,'chain_1'=4,'chain_2'=2,'col'=8] {'col'}, dimensions={0} | all-to-all | bytes 393216 | tf_op jit(solution)/shard_map/all_to_all | solution.py:336
  37.9 1.4 %collective-permute-done.1.other = f32[8,48,128]{2,1,0:T(8,128)S(1)} collective-permute-done((f32[8,48,128]{2,1,0:T(8,128)S(1)}, f32[8,48,128]{2,1,0:T(8,128)S(1)}, u32[]{:S(2)}, u32[]{:S(2)}) %collective-permute-start.1) | collective-permute-done | bytes 196640 | tf_op jit(solution)/shard_map/ppermute | solution.py:378
  39.4 1.2 shard_map.58
  40.8 1.8 %collective-permute-start.3 = (f32[192,128]{1,0:T(8,128)S(1)}, f32[192,128]{1,0:T(8,128)S(1)}, u32[]{:S(2)}, u32[]{:S(2)}) collective-permute-start(f32[192,128]{1,0:T(8,128)S(1)} %get-tuple-element.30.mine), channel_id=1, source_target_pairs={{0,32},{16,48},{32,0},{48,16},{1,33},{17,49},{33,1},{49,17},{2,34}... | collective-permute-start | bytes 294920 | tf_op jit(solution)/shard_map/ppermute | solution.py:342
  42.6 2.5 %collective-permute-start.4 = (f32[192,128]{1,0:T(8,128)S(1)}, f32[192,128]{1,0:T(8,128)S(1)}, u32[]{:S(2)}, u32[]{:S(2)}) collective-permute-start(f32[192,128]{1,0:T(8,128)S(1)} %get-tuple-element.30.mine), channel_id=1, source_target_pairs={{0,48},{16,0},{32,16},{48,32},{1,49},{17,1},{33,17},{49,33},{2,50}... | collective-permute-start | bytes 294920 | tf_op jit(solution)/shard_map/ppermute | solution.py:342
  45.1 3.7 %collective-permute-done.2.one.y1 = f32[192,128]{1,0:T(8,128)S(1)} collective-permute-done((f32[192,128]{1,0:T(8,128)S(1)}, f32[192,128]{1,0:T(8,128)S(1)}, u32[]{:S(2)}, u32[]{:S(2)}) %collective-permute-start.2) | collective-permute-done | bytes 98336 | tf_op jit(solution)/shard_map/ppermute | solution.py:342
  49.4 1.2 shard_map.59
  50.7 2.5 %collective-permute-start.6 = (f32[192,128]{1,0:T(8,128)S(1)}, f32[192,128]{1,0:T(8,128)S(1)}, u32[]{:S(2)}, u32[]{:S(2)}) collective-permute-start(f32[192,128]{1,0:T(8,128)S(1)} %get-tuple-element.34.own), channel_id=1, source_target_pairs={{0,128},{64,192},{128,0},{192,64},{1,129},{65,193},{129,1},{193,65... | collective-permute-start | bytes 294920 | tf_op jit(solution)/shard_map/ppermute | solution.py:342
  53.2 1.4 %collective-permute-start.7 = (f32[192,128]{1,0:T(8,128)S(1)}, f32[192,128]{1,0:T(8,128)S(1)}, u32[]{:S(2)}, u32[]{:S(2)}) collective-permute-start(f32[192,128]{1,0:T(8,128)S(1)} %get-tuple-element.34.own), channel_id=1, source_target_pairs={{0,192},{64,0},{128,64},{192,128},{1,193},{65,1},{129,65},{193,129... | collective-permute-start | bytes 294920 | tf_op jit(solution)/shard_map/ppermute | solution.py:342
  54.7 1.1 shard_map.60
  55.7 2.2 %collective-permute-done.5.one.x1 = f32[192,128]{1,0:T(8,128)S(1)} collective-permute-done((f32[192,128]{1,0:T(8,128)S(1)}, f32[192,128]{1,0:T(8,128)S(1)}, u32[]{:S(2)}, u32[]{:S(2)}) %collective-permute-start.5) | collective-permute-done | bytes 98336 | tf_op jit(solution)/shard_map/ppermute | solution.py:342
  58.4 1.7 %shard_map.61.refs_0_ = bf16[320,128]{1,0:T(8,128)(2,1)S(1)} custom-call(s32[4]{0:T(128)S(1)} %pad_add_fusion.place, f32[128,256]{1,0:T(8,128)S(1)} %get-tuple-element.32.maps, f32[64,256]{1,0:T(8,128)S(1)} %get-tuple-element.33.shifts, f32[192,128]{1,0:T(8,128)S(1)} %get-tuple-element.34.own, f32[192,128]{1,0:T(8,128)S(1)} %collective-permute-done.5.one.x1, ...), custom_call_target="tpu_custom_call" | custom-call | tf_op jit(solution)/shard_map/pallas_call | solution.py:71
  60.1 1.5 %collective-permute-start.10 = (bf16[320,128]{1,0:T(8,128)(2,1)S(1)}, bf16[320,128]{1,0:T(8,128)(2,1)S(1)}, u32[]{:S(2)}, u32[]{:S(2)}) collective-permute-start(bf16[320,128]{1,0:T(8,128)(2,1)S(1)} %shard_map.61.refs_0_), channel_id=1, source_target_pairs={{0,7},{1,0},{2,1},{3,2},{4,3},{5,4},{6,5},{7,6},{8,15},{9,8},{10,9... | collective-permute-start | bytes 245768 | tf_op jit(solution)/shard_map/ppermute | solution.py:399
  62.2 3.1 %collective-permute-done.10.refs_7_ = bf16[320,128]{1,0:T(8,128)(2,1)S(1)} collective-permute-done((bf16[320,128]{1,0:T(8,128)(2,1)S(1)}, bf16[320,128]{1,0:T(8,128)(2,1)S(1)}, u32[]{:S(2)}, u32[]{:S(2)}) %collective-permute-start.10) | collective-permute-done | bytes 81952 | tf_op jit(solution)/shard_map/ppermute | solution.py:399
  65.3 1.5 %collective-permute-start.11 = (bf16[320,128]{1,0:T(8,128)(2,1)S(1)}, bf16[320,128]{1,0:T(8,128)(2,1)S(1)}, u32[]{:S(2)}, u32[]{:S(2)}) collective-permute-start(bf16[320,128]{1,0:T(8,128)(2,1)S(1)} %collective-permute-done.10.refs_7_), channel_id=1, source_target_pairs={{0,7},{1,0},{2,1},{3,2},{4,3},{5,4},{6,5},{7,6},{8,15},{9,8},{10,9... | collective-permute-start | bytes 245768 | tf_op jit(solution)/shard_map/ppermute | solution.py:402
  67.4 1.0 collective-permute-start.13
  68.4 2.1 %shard_map.62 = (bf16[3,384,256]{2,1,0:T(8,128)(2,1)S(1)}, bf16[3,256,896]{2,1,0:T(8,128)(2,1)S(1)}) custom-call(s32[4]{0:T(128)S(1)} %pad_add_fusion.place, f32[8,48,128]{2,1,0:T(8,128)S(1)} %all_to_all.26.mine.whole, f32[192,128]{1,0:T(8,128)S(1)} %get-tuple-element.29.other, f32[192,128]{1,0:T(8,128)S(1)} %get-tuple-element.31.before, ...), custom_call_target="tpu_custom_call" | custom-call | flops 536870912 | bytes 5368709 | tf_op jit(solution)/shard_map/pallas_call | solution.py:71
  70.5 1.0 collective-permute-done.11.refs_6_
  71.5 1.1 collective-permute-start.12
  72.6 0.9 collective-permute-start.14
  73.5 2.3 %collective-permute-done.13.refs_4_ = bf16[320,128]{1,0:T(8,128)(2,1)S(1)} collective-permute-done((bf16[320,128]{1,0:T(8,128)(2,1)S(1)}, bf16[320,128]{1,0:T(8,128)(2,1)S(1)}, u32[]{:S(2)}, u32[]{:S(2)}) %collective-permute-start.13) | collective-permute-done | bytes 81952 | tf_op jit(solution)/shard_map/ppermute | solution.py:400
  76.0 1.6 %collective-permute-done.14.refs_5_ = bf16[320,128]{1,0:T(8,128)(2,1)S(1)} collective-permute-done((bf16[320,128]{1,0:T(8,128)(2,1)S(1)}, bf16[320,128]{1,0:T(8,128)(2,1)S(1)}, u32[]{:S(2)}, u32[]{:S(2)}) %collective-permute-start.14) | collective-permute-done | bytes 81952 | tf_op jit(solution)/shard_map/ppermute | solution.py:412
  77.6 1.8 %shard_map.63 = (f32[128,320]{1,0:T(8,128)S(1)}, f32[8,16,128]{2,1,0:T(8,128)S(1)}) custom-call(s32[4]{0:T(128)S(1)} %pad_add_fusion.place, bf16[320,128]{1,0:T(8,128)(2,1)S(1)} %shard_map.61.refs_0_, bf16[320,128]{1,0:T(8,128)(2,1)S(1)} %collective-permute-done.8.refs_1_, bf16[320,128]{1,0:T(8,128)(2,1)S(1)} %collective-permute-done.9.refs_2_, ...), custom_call_target="tpu_custom_call" | custom-call | tf_op jit(solution)/shard_map/pallas_call | solution.py:71
  79.4 14.0 %all_to_all.27.parts = f32[8,16,128]{2,1,0:T(8,128)S(1)} all-to-all(f32[8,16,128]{2,1,0:T(8,128)S(1)} %get-tuple-element.40), channel_id=1, replica_groups=mesh['chain_0'=4,'chain_1'=4,'chain_2'=2,'col'=8] {'col'}, dimensions={0} | all-to-all | bytes 131072 | tf_op jit(solution)/shard_map/all_to_all | solution.py:336
  94.2 14.5 %all_to_all.28.got = f32[32,8,128]{2,1,0:T(8,128)S(1)} all-to-all(f32[32,8,128]{2,1,0:T(8,128)S(1)} %get-tuple-element.42), channel_id=1, replica_groups=mesh['chain_0'=4,'chain_1'=4,'chain_2'=2,'col'=8] {'chain_0','chain_1','..., dimensions={0} | all-to-all | bytes 262144 | tf_op jit(solution)/shard_map/all_to_all | solution.py:336
  108.8 1.0 shard_map.65
  109.8 10.8 %all_to_all.29.got = f32[8,16,128]{2,1,0:T(8,128)S(1)} all-to-all(f32[8,16,128]{2,1,0:T(8,128)S(1)} %shard_map.65), channel_id=1, replica_groups=mesh['chain_0'=4,'chain_1'=4,'chain_2'=2,'col'=8] {'col'}, dimensions={0} | all-to-all | bytes 131072 | tf_op jit(solution)/shard_map/all_to_all | solution.py:336
  120.6 1.5 %shard_map.66 = f32[2,64,320]{2,1,0:T(8,128)} custom-call(s32[4]{0:T(128)S(1)} %pad_add_fusion.place, f32[8,16,128]{2,1,0:T(8,128)S(1)} %all_to_all.29.got, f32[128,320]{1,0:T(8,128)S(1)} %get-tuple-element.45.turned, bf16[2,320,128]{2,1,0:T(8,128)(2,1)S(1)} %get-tuple-element.46.exit_, bf16[1,320,128]{2,1,0:T(8,128)(2,1)S(1)} %collective-permute-done.arriving), custom_call_target="tpu_custom_call" | custom-call | tf_op jit(solution)/shard_map/pallas_call | solution.py:71
  (19 shorter events, 5.0 us)
Async XLA Ops:
  0.9 6.7 %collective-permute-start = (bf16[1,320,128]{2,1,0:T(8,128)(2,1)S(1)}, bf16[1,320,128]{2,1,0:T(8,128)(2,1)S(1)}, u32[]{:S(2)}, u32[]{:S(2)}) collective-permute-start(bf16[1,320,128]{2,1,0:T(8,128)(2,1)S(1)} %slice.3), channel_id=1, source_target_pairs={{0,248},{8,0},{16,8},{24,16},{32,24},{40,32},{48,40},{56,48},{64,5... | collective-permute-start | bytes 245768 | tf_op jit(solution)/shard_map/ppermute | solution.py:353
  7.5 70.1 %copy-start = (bf16[2,320,2560]{2,1,0:T(8,128)(2,1)S(1)}, bf16[2,320,2560]{2,1,0:T(8,128)(2,1)}, u32[]{:S(2)}) copy-start(bf16[2,320,2560]{2,1,0:T(8,128)(2,1)} %refs_8_.1) | copy-start | bytes 9830404
  37.9 1.4 %collective-permute-start.1 = (f32[8,48,128]{2,1,0:T(8,128)S(1)}, f32[8,48,128]{2,1,0:T(8,128)S(1)}, u32[]{:S(2)}, u32[]{:S(2)}) collective-permute-start(f32[8,48,128]{2,1,0:T(8,128)S(1)} %all_to_all.26.mine.whole), channel_id=1, source_target_pairs={{0,8},{8,0},{1,9},{9,1},{2,10},{10,2},{3,11},{11,3},{4,12},{12,4},... | collective-permute-start | bytes 589832 | tf_op jit(solution)/shard_map/ppermute | solution.py:378
  40.6 8.2 %collective-permute-start.2 = (f32[192,128]{1,0:T(8,128)S(1)}, f32[192,128]{1,0:T(8,128)S(1)}, u32[]{:S(2)}, u32[]{:S(2)}) collective-permute-start(f32[192,128]{1,0:T(8,128)S(1)} %get-tuple-element.30.mine), channel_id=1, source_target_pairs={{0,16},{16,32},{32,48},{48,0},{1,17},{17,33},{33,49},{49,1},{2,18}... | collective-permute-start | bytes 294920 | tf_op jit(solution)/shard_map/ppermute | solution.py:342
  40.8 8.1 %collective-permute-start.3 = (f32[192,128]{1,0:T(8,128)S(1)}, f32[192,128]{1,0:T(8,128)S(1)}, u32[]{:S(2)}, u32[]{:S(2)}) collective-permute-start(f32[192,128]{1,0:T(8,128)S(1)} %get-tuple-element.30.mine), channel_id=1, source_target_pairs={{0,32},{16,48},{32,0},{48,16},{1,33},{17,49},{33,1},{49,17},{2,34}... | collective-permute-start | bytes 294920 | tf_op jit(solution)/shard_map/ppermute | solution.py:342
  42.6 6.8 %collective-permute-start.4 = (f32[192,128]{1,0:T(8,128)S(1)}, f32[192,128]{1,0:T(8,128)S(1)}, u32[]{:S(2)}, u32[]{:S(2)}) collective-permute-start(f32[192,128]{1,0:T(8,128)S(1)} %get-tuple-element.30.mine), channel_id=1, source_target_pairs={{0,48},{16,0},{32,16},{48,32},{1,49},{17,1},{33,17},{49,33},{2,50}... | collective-permute-start | bytes 294920 | tf_op jit(solution)/shard_map/ppermute | solution.py:342
  50.6 7.3 %collective-permute-start.5 = (f32[192,128]{1,0:T(8,128)S(1)}, f32[192,128]{1,0:T(8,128)S(1)}, u32[]{:S(2)}, u32[]{:S(2)}) collective-permute-start(f32[192,128]{1,0:T(8,128)S(1)} %get-tuple-element.34.own), channel_id=1, source_target_pairs={{0,64},{64,128},{128,192},{192,0},{1,65},{65,129},{129,193},{193,1... | collective-permute-start | bytes 294920 | tf_op jit(solution)/shard_map/ppermute | solution.py:342
  50.7 7.2 %collective-permute-start.6 = (f32[192,128]{1,0:T(8,128)S(1)}, f32[192,128]{1,0:T(8,128)S(1)}, u32[]{:S(2)}, u32[]{:S(2)}) collective-permute-start(f32[192,128]{1,0:T(8,128)S(1)} %get-tuple-element.34.own), channel_id=1, source_target_pairs={{0,128},{64,192},{128,0},{192,64},{1,129},{65,193},{129,1},{193,65... | collective-permute-start | bytes 294920 | tf_op jit(solution)/shard_map/ppermute | solution.py:342
  53.2 5.2 %collective-permute-start.7 = (f32[192,128]{1,0:T(8,128)S(1)}, f32[192,128]{1,0:T(8,128)S(1)}, u32[]{:S(2)}, u32[]{:S(2)}) collective-permute-start(f32[192,128]{1,0:T(8,128)S(1)} %get-tuple-element.34.own), channel_id=1, source_target_pairs={{0,192},{64,0},{128,64},{192,128},{1,193},{65,1},{129,65},{193,129... | collective-permute-start | bytes 294920 | tf_op jit(solution)/shard_map/ppermute | solution.py:342
  60.1 5.2 %collective-permute-start.10 = (bf16[320,128]{1,0:T(8,128)(2,1)S(1)}, bf16[320,128]{1,0:T(8,128)(2,1)S(1)}, u32[]{:S(2)}, u32[]{:S(2)}) collective-permute-start(bf16[320,128]{1,0:T(8,128)(2,1)S(1)} %shard_map.61.refs_0_), channel_id=1, source_target_pairs={{0,7},{1,0},{2,1},{3,2},{4,3},{5,4},{6,5},{7,6},{8,15},{9,8},{10,9... | collective-permute-start | bytes 245768 | tf_op jit(solution)/shard_map/ppermute | solution.py:399
  61.6 5.2 %collective-permute-start.8 = (bf16[320,128]{1,0:T(8,128)(2,1)S(1)}, bf16[320,128]{1,0:T(8,128)(2,1)S(1)}, u32[]{:S(2)}, u32[]{:S(2)}) collective-permute-start(bf16[320,128]{1,0:T(8,128)(2,1)S(1)} %shard_map.61.refs_0_), channel_id=1, source_target_pairs={{0,1},{1,2},{2,3},{3,4},{4,5},{5,6},{6,7},{7,0},{8,9},{9,10},{10,1... | collective-permute-start | bytes 245768 | tf_op jit(solution)/shard_map/ppermute | solution.py:398
  65.3 6.2 %collective-permute-start.11 = (bf16[320,128]{1,0:T(8,128)(2,1)S(1)}, bf16[320,128]{1,0:T(8,128)(2,1)S(1)}, u32[]{:S(2)}, u32[]{:S(2)}) collective-permute-start(bf16[320,128]{1,0:T(8,128)(2,1)S(1)} %collective-permute-done.10.refs_7_), channel_id=1, source_target_pairs={{0,7},{1,0},{2,1},{3,2},{4,3},{5,4},{6,5},{7,6},{8,15},{9,8},{10,9... | collective-permute-start | bytes 245768 | tf_op jit(solution)/shard_map/ppermute | solution.py:402
  66.8 4.7 %collective-permute-start.9 = (bf16[320,128]{1,0:T(8,128)(2,1)S(1)}, bf16[320,128]{1,0:T(8,128)(2,1)S(1)}, u32[]{:S(2)}, u32[]{:S(2)}) collective-permute-start(bf16[320,128]{1,0:T(8,128)(2,1)S(1)} %collective-permute-done.8.refs_1_), channel_id=1, source_target_pairs={{0,1},{1,2},{2,3},{3,4},{4,5},{5,6},{6,7},{7,0},{8,9},{9,10},{10,1... | collective-permute-start | bytes 245768 | tf_op jit(solution)/shard_map/ppermute | solution.py:401
  67.4 8.5 %collective-permute-start.13 = (bf16[320,128]{1,0:T(8,128)(2,1)S(1)}, bf16[320,128]{1,0:T(8,128)(2,1)S(1)}, u32[]{:S(2)}, u32[]{:S(2)}) collective-permute-start(bf16[320,128]{1,0:T(8,128)(2,1)S(1)} %shard_map.61.refs_0_), channel_id=1, source_target_pairs={{0,4},{1,5},{2,6},{3,7},{4,0},{5,1},{6,2},{7,3},{8,12},{9,13},{10,... | collective-permute-start | bytes 245768 | tf_op jit(solution)/shard_map/ppermute | solution.py:400
  71.5 4.4 %collective-permute-start.12 = (bf16[320,128]{1,0:T(8,128)(2,1)S(1)}, bf16[320,128]{1,0:T(8,128)(2,1)S(1)}, u32[]{:S(2)}, u32[]{:S(2)}) collective-permute-start(bf16[320,128]{1,0:T(8,128)(2,1)S(1)} %collective-permute-done.9.refs_2_), channel_id=1, source_target_pairs={{0,1},{1,2},{2,3},{3,4},{4,5},{5,6},{6,7},{7,0},{8,9},{9,10},{10,1... | collective-permute-start | bytes 245768 | tf_op jit(solution)/shard_map/ppermute | solution.py:411
  72.6 5.0 %collective-permute-start.14 = (bf16[320,128]{1,0:T(8,128)(2,1)S(1)}, bf16[320,128]{1,0:T(8,128)(2,1)S(1)}, u32[]{:S(2)}, u32[]{:S(2)}) collective-permute-start(bf16[320,128]{1,0:T(8,128)(2,1)S(1)} %collective-permute-done.11.refs_6_), channel_id=1, source_target_pairs={{0,7},{1,0},{2,1},{3,2},{4,3},{5,4},{6,5},{7,6},{8,15},{9,8},{10,9... | collective-permute-start | bytes 245768 | tf_op jit(solution)/shard_map/ppermute | solution.py:412

commit v5 on v4

--- a/solution.py
+++ b/solution.py
@@ -21,7 +21,7 @@
 
 
 def dot32(a, b, dims):
-    return lax.dot_general(a, b, dims, precision=lax.Precision.HIGHEST, preferred_element_type=F32)
+    return dot_parts(a, [part.astype(BF16) for part in three_parts(b)], dims)
 
 
 def dot32_16(a, b, dims):
@@ -167,7 +167,7 @@
     beside[...] = there
 
 
-def group_kernel(place, mine, one, two, three, total, before, slots):
+def group_kernel(place, mine, one, two, three, total, low, slots):
     n = mine.shape[1]
     y = place[1]
     for d, ref in enumerate((mine, one, two, three)):
@@ -175,35 +175,25 @@
 
     low_top, low_bottom = after(slots[0], slots[1], n)
     high_top, high_bottom = after(slots[2], slots[3], n)
-    low = jnp.concatenate([low_top, low_bottom], axis=0)
-    out = dot32(low, high_top, NN)
+    low[:n] = low_top
+    low[n:] = low_bottom
+    out = dot32(low[...], high_top, NN)
     total[:n] = out[:n]
     total[n:] = out[n:] + high_bottom
-    rows = lax.broadcasted_iota(jnp.int32, mine.shape, 0)
-    lanes = lax.broadcasted_iota(jnp.int32, mine.shape, 1)
-
-    @pl.when(y == 0)
-    def _():
-        before[...] = jnp.where(rows == lanes, 1.0, 0.0).astype(F32)
-
-    @pl.when(y == 1)
-    def _():
-        before[...] = slots[0]
-
-    @pl.when(y == 2)
-    def _():
-        before[...] = low
-
-    @pl.when(y == 3)
-    def _():
-        out = dot32(low, slots[2, :n], NN)
-        before[:n] = out[:n]
-        before[n:] = out[n:] + slots[2, n:]
-
-
-def tail_kernel(place, whole, other, before, maps, shifts):
+
+
+def tail_kernel(place, whole, other, low, one, maps, shifts, before):
     couple0, _, source0, _ = pieces(whole)
     n = couple0.shape[0]
+    y = place[1]
+    top, bottom = after(low[...], one, n)
+    three = jnp.concatenate([top, bottom], axis=0)
+    rows = lax.broadcasted_iota(jnp.int32, low.shape, 0)
+    lanes = lax.broadcasted_iota(jnp.int32, low.shape, 1)
+    none = jnp.where(rows == lanes, 1.0, 0.0).astype(F32)
+    before[...] = jnp.where(
+        y == 3, three, jnp.where(y == 2, low[...], jnp.where(y == 1, one[...], none))
+    )
     reach, shift = after(before[...], other[...], n)
     upper = place[2] == 1
     reach = jnp.where(upper, reach, before[:n])
@@ -242,20 +232,46 @@
     out[...] = (turned[...] - product).astype(BF16)
 
 
+def windows(place, blocks, shifts, inverse, padded):
+    groups = 8
+    local, both = blocks[0].shape
+    room = padded.shape[1]
+    starts = []
+    for k, (block, d) in enumerate(zip(blocks, shifts)):
+        owner = lax.rem(place[3] - d + groups, groups)
+        odd = lax.rem(owner, 2)
+        offset = pl.multiple_of(odd * (room - local), room - local)
+        padded[k] = jnp.zeros(padded.shape[1:], BF16)
+        padded[k, pl.ds(offset, local), :] = block[...]
+        starts.append(pl.multiple_of(owner * local - odd * (room - local), 128))
+    whole = padded[...].reshape(len(blocks) * room, both)
+
+    def through(i):
+        rows = jnp.concatenate([inverse[i, :, pl.ds(start, room)] for start in starts], axis=1)
+        return dot16(rows, whole, NN)
+
+    lanes = lax.broadcasted_iota(jnp.int32, (local, both), 1)
+    return jnp.where(lanes < both // 2, through(0), through(1))
+
+
+EARLY = (0, 1, 2, 4, 6, 7)
+LATE = (3, 5)
+
+
+def early_kernel(place, *refs):
+    blocks = refs[: len(EARLY)]
+    inverse, out, padded = refs[len(EARLY) :]
+    out[...] = windows(place, blocks, EARLY, inverse, padded)
+
+
 def apply_kernel(place, *refs):
-    groups = len(refs) - 5
-    blocks = refs[:groups]
-    inverse, entry, turned, carried, slots = refs[groups:]
-    local, both = blocks[0].shape
-    for d, block in enumerate(blocks):
-        slots[lax.rem(place[3] - d + groups, groups)] = block[...]
-    whole = slots[...].reshape(groups * local, both)
-    lanes = lax.broadcasted_iota(jnp.int32, (local, both), 1)
-    half = both // 2
-    value = jnp.where(lanes < half, dot16(inverse[0], whole, NN), dot16(inverse[1], whole, NN))
+    blocks = refs[: len(LATE)]
+    early, inverse, entry, turned, carried, padded = refs[len(LATE) :]
+    value = early[...] + windows(place, blocks, LATE, inverse, padded)
     turned[...] = value.T
     low = value.astype(BF16)
-    c = half // groups
+    half = value.shape[1] // 2
+    c = half // carried.shape[0]
     put(carried, 0, c, dot16(low, entry[0], TN)[:half])
     put(carried, c, c, dot16(low, entry[1], TN)[half:])
 
@@ -352,7 +368,7 @@
     chain = lax.axis_size(CHAIN)
     arriving = lax.ppermute(exit_[:1], CHAIN, [(i, (i - 1) % chain) for i in range(chain)])
     rows = (2 * n + 2 * cols) // z
-    entry_v, exit_v, second, turned, early = call(
+    entry_v, exit_v, second, turned, begun = call(
         load_kernel,
         place,
         [pltpu.with_memory_space_constraint(a, pltpu.HBM) for a in (entry, exit_, rhs, previous)],
@@ -371,19 +387,23 @@
         [hbm()] * 4,
         cost=1 << 28,
     )
-    parts = call(partial_kernel, place, (entry_v, arriving, second, early), of((z, rows, n)))
+    parts = call(partial_kernel, place, (entry_v, arriving, second, begun), of((z, rows, n)))
     summed = call(sum_kernel, place, (exchange(parts, COL),), of((z, rows, n)))
     whole = exchange(summed, COL)
     maps = of((n + cols, n))
     whole_other = lax.ppermute(whole, CORE, [(0, 1), (1, 0)])
     chip, other = call(pair_kernel, place, (whole, whole_other), (maps, maps))
     y1, y2, y3 = ring(chip, Y)
-    group, before = call(
+    group, low = call(
         group_kernel, place, (chip, y1, y2, y3), (maps, maps), [pltpu.VMEM((4, n + cols, n), F32)]
     )
     x1, x2, x3 = ring(group, X)
-    ahead, shifts = call(
-        tail_kernel, place, (whole, other, before), (of((n, 2 * n)), of((cols, 2 * n))), cost=1 << 27
+    ahead, shifts, before = call(
+        tail_kernel,
+        place,
+        (whole, other, low, y1),
+        (of((n, 2 * n)), of((cols, 2 * n)), maps),
+        cost=1 << 27,
     )
     forward = call(
         forward_kernel,
@@ -407,16 +427,27 @@
         (of((3, 3 * n, 2 * n), BF16), of((3, 2 * n, 7 * n), BF16)),
         cost=1 << 29,
     )
-    blocks[2], blocks[6], leave, reach = lax.optimization_barrier((blocks[2], blocks[6], leave, reach))
+    blocks[2], blocks[4], blocks[6], leave, reach = lax.optimization_barrier(
+        (blocks[2], blocks[4], blocks[6], leave, reach)
+    )
     blocks[3] = lax.ppermute(blocks[2], COL, up)
     blocks[5] = lax.ppermute(blocks[6], COL, down)
     c = cols // z
+    room = -(-local // 128) * 128
+    early = call(
+        early_kernel,
+        place,
+        (*[blocks[d] for d in EARLY], block_inverse),
+        of((local, 2 * cols)),
+        [pltpu.VMEM((len(EARLY), room, 2 * cols), BF16)],
+        cost=1 << 29,
+    )
     turned_applied, carried_parts = call(
         apply_kernel,
         place,
-        (*blocks, block_inverse, entry_v),
+        (*[blocks[d] for d in LATE], early, block_inverse, entry_v),
         (of((2 * cols, local)), of((z, 2 * c, n))),
-        [pltpu.VMEM((z, local, 2 * cols), BF16)],
+        [pltpu.VMEM((len(LATE), room, 2 * cols), BF16)],
     )
     carried, send = call(
         back_kernel,

time: 124 us -> 122 us (0.984)
  waiting for transfers between devices: 16.8 us -> 15.5 us
    ppermute x1, waiting for transfers between devices: 2.34 us -> 0.01 us  [shards(): blocks[4] = lax.ppermute(forward, COL, far)]
    pallas_call x12 -> x13, Pallas kernels: 15.6 us -> 16.4 us  [call(): pl.pallas_call(kernel, out_shape=outs, in_specs=[smem()] + (specs or [vme...]
  transfers between devices with their start and end apart: 15 -> 15, of which waited for: 12 -> 11; matrix products, arithmetic and copies ran while one was open for 0% -> 0% of each run, Pallas kernels for 4% -> 6%
where the time goes in v5:
time: 122 us; the launch traced here: 121 us
  blocking collectives  67.2 us (55%)
  starting transfers between devices  20.4 us (17%)
  Pallas kernels  16.4 us (13%)
  waiting for transfers between devices  15.5 us (13%)
    all_to_all x5, blocking collectives, exchange(): return lax.all_to_all(value, axes, split_axis=0, concat_axis=0, tiled=True)  67.2 us
    pallas_call x13, Pallas kernels, call(): pl.pallas_call(kernel, out_shape=outs, in_specs=[smem()] + (specs or [vme...  16.4 us
    ppermute x6, starting transfers between devices, ring(): lax.ppermute(value, axis, [(i, (i + d) % size) for i in range(size)])  8.55 us
    ppermute x6, waiting for transfers between devices, ring(): lax.ppermute(value, axis, [(i, (i + d) % size) for i in range(size)])  6.8 us
    ppermute x1, starting transfers between devices, shards(): lax.ppermute(exit_[:1], CHAIN, [(i, (i - 1) % chain) for i in range(chain)])  4.65 us
    ppermute x1, waiting for transfers between devices, shards(): blocks[7] = lax.ppermute(forward, COL, down)  3.83 us
  transfers between devices with their start and end apart: 15, of which 11 were waited for; matrix products, arithmetic and copies ran while one was open for 0% of the time, Pallas kernels for 6%

profile of v5, /device:TPU:32, one launch (start us, length us, event | category | flops | bytes accessed | tf_op | source)
XLA Modules:
  0.0 120.5 jit_solution(652760715341977599)
XLA Ops:
  0.0 0.9 slice.3
  0.9 4.6 %collective-permute-start = (bf16[1,320,128]{2,1,0:T(8,128)(2,1)S(1)}, bf16[1,320,128]{2,1,0:T(8,128)(2,1)S(1)}, u32[]{:S(2)}, u32[]{:S(2)}) collective-permute-start(bf16[1,320,128]{2,1,0:T(8,128)(2,1)S(1)} %slice.3), channel_id=1, source_target_pairs={{0,248},{8,0},{16,8},{24,16},{32,24},{40,32},{48,40},{56,48},{64,5... | collective-permute-start | bytes 245768 | tf_op jit(solution)/shard_map/ppermute | solution.py:369
  5.6 1.9 %shard_map.55 = (bf16[2,320,128]{2,1,0:T(8,128)(2,1)S(1)}, bf16[2,320,128]{2,1,0:T(8,128)(2,1)S(1)}, bf16[64,320]{1,0:T(8,128)(2,1)S(1)}, f32[320,128]{1,0:T(8,128)S(1)}, f32[8,24,128]{2,1,0:T(8,128)S(1)}) custom-call(s32[4]{0:T(128)S(1)} %pad_add_fusion.place, bf16[2,320,128]{2,1,0:T(8,128)(2,1)} %entry.1, bf16[2,320,128]{2,1,0:T(8,128)(2,1)} %exit_.1, ...), custom_call_target="tpu_custom_call" | custom-call | flops 268435456 | bytes 2684354 | tf_op jit(solution)/shard_map/pallas_call | solution.py:71
  8.4 16.7 %all_to_all.25.parts = f32[8,48,128]{2,1,0:T(8,128)S(1)} all-to-all(f32[8,48,128]{2,1,0:T(8,128)S(1)} %shard_map.56), channel_id=1, replica_groups=mesh['chain_0'=4,'chain_1'=4,'chain_2'=2,'col'=8] {'col'}, dimensions={0} | all-to-all | bytes 393216 | tf_op jit(solution)/shard_map/all_to_all | solution.py:352
  25.6 12.3 %all_to_all.26.mine.whole = f32[8,48,128]{2,1,0:T(8,128)S(1)} all-to-all(f32[8,48,128]{2,1,0:T(8,128)S(1)} %shard_map.57), channel_id=1, replica_groups=mesh['chain_0'=4,'chain_1'=4,'chain_2'=2,'col'=8] {'col'}, dimensions={0} | all-to-all | bytes 393216 | tf_op jit(solution)/shard_map/all_to_all | solution.py:352
  37.9 1.4 %collective-permute-done.1.other = f32[8,48,128]{2,1,0:T(8,128)S(1)} collective-permute-done((f32[8,48,128]{2,1,0:T(8,128)S(1)}, f32[8,48,128]{2,1,0:T(8,128)S(1)}, u32[]{:S(2)}, u32[]{:S(2)}) %collective-permute-start.1) | collective-permute-done | bytes 196640 | tf_op jit(solution)/shard_map/ppermute | solution.py:394
  39.4 1.2 shard_map.58
  40.7 1.8 %collective-permute-start.3 = (f32[192,128]{1,0:T(8,128)S(1)}, f32[192,128]{1,0:T(8,128)S(1)}, u32[]{:S(2)}, u32[]{:S(2)}) collective-permute-start(f32[192,128]{1,0:T(8,128)S(1)} %get-tuple-element.32.mine), channel_id=1, source_target_pairs={{0,32},{16,48},{32,0},{48,16},{1,33},{17,49},{33,1},{49,17},{2,34}... | collective-permute-start | bytes 294920 | tf_op jit(solution)/shard_map/ppermute | solution.py:358
  42.6 2.5 %collective-permute-start.4 = (f32[192,128]{1,0:T(8,128)S(1)}, f32[192,128]{1,0:T(8,128)S(1)}, u32[]{:S(2)}, u32[]{:S(2)}) collective-permute-start(f32[192,128]{1,0:T(8,128)S(1)} %get-tuple-element.32.mine), channel_id=1, source_target_pairs={{0,48},{16,0},{32,16},{48,32},{1,49},{17,1},{33,17},{49,33},{2,50}... | collective-permute-start | bytes 294920 | tf_op jit(solution)/shard_map/ppermute | solution.py:358
  45.1 3.7 %collective-permute-done.2.one.y1 = f32[192,128]{1,0:T(8,128)S(1)} collective-permute-done((f32[192,128]{1,0:T(8,128)S(1)}, f32[192,128]{1,0:T(8,128)S(1)}, u32[]{:S(2)}, u32[]{:S(2)}) %collective-permute-start.2) | collective-permute-done | bytes 98336 | tf_op jit(solution)/shard_map/ppermute | solution.py:358
  49.4 1.2 shard_map.59
  50.7 2.5 %collective-permute-start.6 = (f32[192,128]{1,0:T(8,128)S(1)}, f32[192,128]{1,0:T(8,128)S(1)}, u32[]{:S(2)}, u32[]{:S(2)}) collective-permute-start(f32[192,128]{1,0:T(8,128)S(1)} %get-tuple-element.36.own), channel_id=1, source_target_pairs={{0,128},{64,192},{128,0},{192,64},{1,129},{65,193},{129,1},{193,65... | collective-permute-start | bytes 294920 | tf_op jit(solution)/shard_map/ppermute | solution.py:358
  53.2 1.4 %collective-permute-start.7 = (f32[192,128]{1,0:T(8,128)S(1)}, f32[192,128]{1,0:T(8,128)S(1)}, u32[]{:S(2)}, u32[]{:S(2)}) collective-permute-start(f32[192,128]{1,0:T(8,128)S(1)} %get-tuple-element.36.own), channel_id=1, source_target_pairs={{0,192},{64,0},{128,64},{192,128},{1,193},{65,1},{129,65},{193,129... | collective-permute-start | bytes 294920 | tf_op jit(solution)/shard_map/ppermute | solution.py:358
  54.6 1.3 %shard_map.60 = (f32[128,256]{1,0:T(8,128)S(1)}, f32[64,256]{1,0:T(8,128)S(1)}, f32[192,128]{1,0:T(8,128)S(1)}) custom-call(s32[4]{0:T(128)S(1)} %pad_add_fusion.place, f32[8,48,128]{2,1,0:T(8,128)S(1)} %all_to_all.26.mine.whole, f32[192,128]{1,0:T(8,128)S(1)} %get-tuple-element.31.other, f32[192,128]{1,0:T(8,128)S(1)} %get-tuple-element.33.low, ...), custom_call_target="tpu_custom_call" | custom-call | flops 134217728 | bytes 1342177 | tf_op jit(solution)/shard_map/pallas_call | solution.py:71
  55.9 2.0 %collective-permute-done.5.one.x1 = f32[192,128]{1,0:T(8,128)S(1)} collective-permute-done((f32[192,128]{1,0:T(8,128)S(1)}, f32[192,128]{1,0:T(8,128)S(1)}, u32[]{:S(2)}, u32[]{:S(2)}) %collective-permute-start.5) | collective-permute-done | bytes 98336 | tf_op jit(solution)/shard_map/ppermute | solution.py:358
  58.4 1.5 %shard_map.61.refs_0_ = bf16[320,128]{1,0:T(8,128)(2,1)S(1)} custom-call(s32[4]{0:T(128)S(1)} %pad_add_fusion.place, f32[128,256]{1,0:T(8,128)S(1)} %get-tuple-element.34.maps, f32[64,256]{1,0:T(8,128)S(1)} %get-tuple-element.35.shifts, f32[192,128]{1,0:T(8,128)S(1)} %get-tuple-element.36.own, f32[192,128]{1,0:T(8,128)S(1)} %collective-permute-done.5.one.x1, ...), custom_call_target="tpu_custom_call" | custom-call | tf_op jit(solution)/shard_map/pallas_call | solution.py:71
  59.9 1.5 %collective-permute-start.11 = (bf16[320,128]{1,0:T(8,128)(2,1)S(1)}, bf16[320,128]{1,0:T(8,128)(2,1)S(1)}, u32[]{:S(2)}, u32[]{:S(2)}) collective-permute-start(bf16[320,128]{1,0:T(8,128)(2,1)S(1)} %shard_map.61.refs_0_), channel_id=1, source_target_pairs={{0,7},{1,0},{2,1},{3,2},{4,3},{5,4},{6,5},{7,6},{8,15},{9,8},{10,9... | collective-permute-start | bytes 245768 | tf_op jit(solution)/shard_map/ppermute | solution.py:419
  62.0 1.0 collective-permute-start.10
  63.1 3.8 %collective-permute-done.11.refs_5_ = bf16[320,128]{1,0:T(8,128)(2,1)S(1)} collective-permute-done((bf16[320,128]{1,0:T(8,128)(2,1)S(1)}, bf16[320,128]{1,0:T(8,128)(2,1)S(1)}, u32[]{:S(2)}, u32[]{:S(2)}) %collective-permute-start.11) | collective-permute-done | bytes 81952 | tf_op jit(solution)/shard_map/ppermute | solution.py:419
  67.5 1.5 %collective-permute-start.9 = (bf16[320,128]{1,0:T(8,128)(2,1)S(1)}, bf16[320,128]{1,0:T(8,128)(2,1)S(1)}, u32[]{:S(2)}, u32[]{:S(2)}) collective-permute-start(bf16[320,128]{1,0:T(8,128)(2,1)S(1)} %collective-permute-done.8.refs_1_), channel_id=1, source_target_pairs={{0,1},{1,2},{2,3},{3,4},{4,5},{5,6},{6,7},{7,0},{8,9},{9,10},{10,1... | collective-permute-start | bytes 245768 | tf_op jit(solution)/shard_map/ppermute | solution.py:421
  68.9 2.0 %shard_map.62 = (bf16[3,384,256]{2,1,0:T(8,128)(2,1)S(1)}, bf16[3,256,896]{2,1,0:T(8,128)(2,1)S(1)}) custom-call(s32[4]{0:T(128)S(1)} %pad_add_fusion.place, f32[8,48,128]{2,1,0:T(8,128)S(1)} %all_to_all.26.mine.whole, f32[192,128]{1,0:T(8,128)S(1)} %get-tuple-element.31.other, f32[192,128]{1,0:T(8,128)S(1)} %get-tuple-element.38.before, ...), custom_call_target="tpu_custom_call" | custom-call | flops 536870912 | bytes 5368709 | tf_op jit(solution)/shard_map/pallas_call | solution.py:71
  70.9 1.3 %collective-permute-done.12.refs_4_ = bf16[320,128]{1,0:T(8,128)(2,1)S(1)} collective-permute-done((bf16[320,128]{1,0:T(8,128)(2,1)S(1)}, bf16[320,128]{1,0:T(8,128)(2,1)S(1)}, u32[]{:S(2)}, u32[]{:S(2)}) %collective-permute-start.12) | collective-permute-done | bytes 81952 | tf_op jit(solution)/shard_map/ppermute | solution.py:422
  72.5 0.9 collective-permute-start.13
  73.4 1.1 collective-permute-start.14
  74.5 1.5 %shard_map.63.refs_2_ = f32[320,128]{1,0:T(8,128)S(1)} custom-call(s32[4]{0:T(128)S(1)} %pad_add_fusion.place, bf16[320,128]{1,0:T(8,128)(2,1)S(1)} %shard_map.61.refs_0_, bf16[320,128]{1,0:T(8,128)(2,1)S(1)} %collective-permute-done.8.refs_1_, bf16[320,128]{1,0:T(8,128)(2,1)S(1)} %collective-permute-done.9.refs_2_, ...), custom_call_target="tpu_custom_call" | custom-call | flops 536870912 | bytes 5368709 | tf_op jit(solution)/shard_map/pallas_call | solution.py:71
  76.9 0.9 collective-permute-done.14.refs_1_
  77.8 1.2 %shard_map.64 = (f32[128,320]{1,0:T(8,128)S(1)}, f32[8,16,128]{2,1,0:T(8,128)S(1)}) custom-call(s32[4]{0:T(128)S(1)} %pad_add_fusion.place, bf16[320,128]{1,0:T(8,128)(2,1)S(1)} %collective-permute-done.13.refs_0_, bf16[320,128]{1,0:T(8,128)(2,1)S(1)} %collective-permute-done.14.refs_1_, f32[320,128]{1,0:T(8,128)S(1)} %shard_map.63.refs_2_, ...), custom_call_target="tpu_custom_call" | custom-call | tf_op jit(solution)/shard_map/pallas_call | solution.py:71
  79.0 12.8 %all_to_all.27.parts = f32[8,16,128]{2,1,0:T(8,128)S(1)} all-to-all(f32[8,16,128]{2,1,0:T(8,128)S(1)} %get-tuple-element.44), channel_id=1, replica_groups=mesh['chain_0'=4,'chain_1'=4,'chain_2'=2,'col'=8] {'col'}, dimensions={0} | all-to-all | bytes 131072 | tf_op jit(solution)/shard_map/all_to_all | solution.py:352
  92.6 14.6 %all_to_all.28.got = f32[32,8,128]{2,1,0:T(8,128)S(1)} all-to-all(f32[32,8,128]{2,1,0:T(8,128)S(1)} %get-tuple-element.46), channel_id=1, replica_groups=mesh['chain_0'=4,'chain_1'=4,'chain_2'=2,'col'=8] {'chain_0','chain_1','..., dimensions={0} | all-to-all | bytes 262144 | tf_op jit(solution)/shard_map/all_to_all | solution.py:352
  107.3 1.0 shard_map.66
  108.3 10.8 %all_to_all.29.got = f32[8,16,128]{2,1,0:T(8,128)S(1)} all-to-all(f32[8,16,128]{2,1,0:T(8,128)S(1)} %shard_map.66), channel_id=1, replica_groups=mesh['chain_0'=4,'chain_1'=4,'chain_2'=2,'col'=8] {'col'}, dimensions={0} | all-to-all | bytes 131072 | tf_op jit(solution)/shard_map/all_to_all | solution.py:352
  119.1 1.4 %shard_map.67 = f32[2,64,320]{2,1,0:T(8,128)} custom-call(s32[4]{0:T(128)S(1)} %pad_add_fusion.place, f32[8,16,128]{2,1,0:T(8,128)S(1)} %all_to_all.29.got, f32[128,320]{1,0:T(8,128)S(1)} %get-tuple-element.49.turned, bf16[2,320,128]{2,1,0:T(8,128)(2,1)S(1)} %get-tuple-element.50.exit_, bf16[1,320,128]{2,1,0:T(8,128)(2,1)S(1)} %collective-permute-done.arriving), custom_call_target="tpu_custom_call" | custom-call | tf_op jit(solution)/shard_map/pallas_call | solution.py:71
  (20 shorter events, 6.0 us)
Async XLA Ops:
  0.9 6.7 %collective-permute-start = (bf16[1,320,128]{2,1,0:T(8,128)(2,1)S(1)}, bf16[1,320,128]{2,1,0:T(8,128)(2,1)S(1)}, u32[]{:S(2)}, u32[]{:S(2)}) collective-permute-start(bf16[1,320,128]{2,1,0:T(8,128)(2,1)S(1)} %slice.3), channel_id=1, source_target_pairs={{0,248},{8,0},{16,8},{24,16},{32,24},{40,32},{48,40},{56,48},{64,5... | collective-permute-start | bytes 245768 | tf_op jit(solution)/shard_map/ppermute | solution.py:369
  7.5 67.0 %copy-start = (bf16[2,320,2560]{2,1,0:T(8,128)(2,1)S(1)}, bf16[2,320,2560]{2,1,0:T(8,128)(2,1)}, u32[]{:S(2)}) copy-start(bf16[2,320,2560]{2,1,0:T(8,128)(2,1)} %refs_3_.1) | copy-start | bytes 9830404
  37.9 1.4 %collective-permute-start.1 = (f32[8,48,128]{2,1,0:T(8,128)S(1)}, f32[8,48,128]{2,1,0:T(8,128)S(1)}, u32[]{:S(2)}, u32[]{:S(2)}) collective-permute-start(f32[8,48,128]{2,1,0:T(8,128)S(1)} %all_to_all.26.mine.whole), channel_id=1, source_target_pairs={{0,8},{8,0},{1,9},{9,1},{2,10},{10,2},{3,11},{11,3},{4,12},{12,4},... | collective-permute-start | bytes 589832 | tf_op jit(solution)/shard_map/ppermute | solution.py:394
  40.6 8.2 %collective-permute-start.2 = (f32[192,128]{1,0:T(8,128)S(1)}, f32[192,128]{1,0:T(8,128)S(1)}, u32[]{:S(2)}, u32[]{:S(2)}) collective-permute-start(f32[192,128]{1,0:T(8,128)S(1)} %get-tuple-element.32.mine), channel_id=1, source_target_pairs={{0,16},{16,32},{32,48},{48,0},{1,17},{17,33},{33,49},{49,1},{2,18}... | collective-permute-start | bytes 294920 | tf_op jit(solution)/shard_map/ppermute | solution.py:358
  40.7 8.1 %collective-permute-start.3 = (f32[192,128]{1,0:T(8,128)S(1)}, f32[192,128]{1,0:T(8,128)S(1)}, u32[]{:S(2)}, u32[]{:S(2)}) collective-permute-start(f32[192,128]{1,0:T(8,128)S(1)} %get-tuple-element.32.mine), channel_id=1, source_target_pairs={{0,32},{16,48},{32,0},{48,16},{1,33},{17,49},{33,1},{49,17},{2,34}... | collective-permute-start | bytes 294920 | tf_op jit(solution)/shard_map/ppermute | solution.py:358
  42.6 6.8 %collective-permute-start.4 = (f32[192,128]{1,0:T(8,128)S(1)}, f32[192,128]{1,0:T(8,128)S(1)}, u32[]{:S(2)}, u32[]{:S(2)}) collective-permute-start(f32[192,128]{1,0:T(8,128)S(1)} %get-tuple-element.32.mine), channel_id=1, source_target_pairs={{0,48},{16,0},{32,16},{48,32},{1,49},{17,1},{33,17},{49,33},{2,50}... | collective-permute-start | bytes 294920 | tf_op jit(solution)/shard_map/ppermute | solution.py:358
  50.6 7.3 %collective-permute-start.5 = (f32[192,128]{1,0:T(8,128)S(1)}, f32[192,128]{1,0:T(8,128)S(1)}, u32[]{:S(2)}, u32[]{:S(2)}) collective-permute-start(f32[192,128]{1,0:T(8,128)S(1)} %get-tuple-element.36.own), channel_id=1, source_target_pairs={{0,64},{64,128},{128,192},{192,0},{1,65},{65,129},{129,193},{193,1... | collective-permute-start | bytes 294920 | tf_op jit(solution)/shard_map/ppermute | solution.py:358
  50.7 7.2 %collective-permute-start.6 = (f32[192,128]{1,0:T(8,128)S(1)}, f32[192,128]{1,0:T(8,128)S(1)}, u32[]{:S(2)}, u32[]{:S(2)}) collective-permute-start(f32[192,128]{1,0:T(8,128)S(1)} %get-tuple-element.36.own), channel_id=1, source_target_pairs={{0,128},{64,192},{128,0},{192,64},{1,129},{65,193},{129,1},{193,65... | collective-permute-start | bytes 294920 | tf_op jit(solution)/shard_map/ppermute | solution.py:358
  53.2 5.2 %collective-permute-start.7 = (f32[192,128]{1,0:T(8,128)S(1)}, f32[192,128]{1,0:T(8,128)S(1)}, u32[]{:S(2)}, u32[]{:S(2)}) collective-permute-start(f32[192,128]{1,0:T(8,128)S(1)} %get-tuple-element.36.own), channel_id=1, source_target_pairs={{0,192},{64,0},{128,64},{192,128},{1,193},{65,1},{129,65},{193,129... | collective-permute-start | bytes 294920 | tf_op jit(solution)/shard_map/ppermute | solution.py:358
  59.9 7.0 %collective-permute-start.11 = (bf16[320,128]{1,0:T(8,128)(2,1)S(1)}, bf16[320,128]{1,0:T(8,128)(2,1)S(1)}, u32[]{:S(2)}, u32[]{:S(2)}) collective-permute-start(bf16[320,128]{1,0:T(8,128)(2,1)S(1)} %shard_map.61.refs_0_), channel_id=1, source_target_pairs={{0,7},{1,0},{2,1},{3,2},{4,3},{5,4},{6,5},{7,6},{8,15},{9,8},{10,9... | collective-permute-start | bytes 245768 | tf_op jit(solution)/shard_map/ppermute | solution.py:419
  61.4 6.0 %collective-permute-start.8 = (bf16[320,128]{1,0:T(8,128)(2,1)S(1)}, bf16[320,128]{1,0:T(8,128)(2,1)S(1)}, u32[]{:S(2)}, u32[]{:S(2)}) collective-permute-start(bf16[320,128]{1,0:T(8,128)(2,1)S(1)} %shard_map.61.refs_0_), channel_id=1, source_target_pairs={{0,1},{1,2},{2,3},{3,4},{4,5},{5,6},{6,7},{7,0},{8,9},{9,10},{10,1... | collective-permute-start | bytes 245768 | tf_op jit(solution)/shard_map/ppermute | solution.py:418
  62.0 8.9 %collective-permute-start.10 = (bf16[320,128]{1,0:T(8,128)(2,1)S(1)}, bf16[320,128]{1,0:T(8,128)(2,1)S(1)}, u32[]{:S(2)}, u32[]{:S(2)}) collective-permute-start(bf16[320,128]{1,0:T(8,128)(2,1)S(1)} %shard_map.61.refs_0_), channel_id=1, source_target_pairs={{0,4},{1,5},{2,6},{3,7},{4,0},{5,1},{6,2},{7,3},{8,12},{9,13},{10,... | collective-permute-start | bytes 245768 | tf_op jit(solution)/shard_map/ppermute | solution.py:420
  66.9 5.3 %collective-permute-start.12 = (bf16[320,128]{1,0:T(8,128)(2,1)S(1)}, bf16[320,128]{1,0:T(8,128)(2,1)S(1)}, u32[]{:S(2)}, u32[]{:S(2)}) collective-permute-start(bf16[320,128]{1,0:T(8,128)(2,1)S(1)} %collective-permute-done.11.refs_5_), channel_id=1, source_target_pairs={{0,7},{1,0},{2,1},{3,2},{4,3},{5,4},{6,5},{7,6},{8,15},{9,8},{10,9... | collective-permute-start | bytes 245768 | tf_op jit(solution)/shard_map/ppermute | solution.py:422
  67.5 5.0 %collective-permute-start.9 = (bf16[320,128]{1,0:T(8,128)(2,1)S(1)}, bf16[320,128]{1,0:T(8,128)(2,1)S(1)}, u32[]{:S(2)}, u32[]{:S(2)}) collective-permute-start(bf16[320,128]{1,0:T(8,128)(2,1)S(1)} %collective-permute-done.8.refs_1_), channel_id=1, source_target_pairs={{0,1},{1,2},{2,3},{3,4},{4,5},{5,6},{6,7},{7,0},{8,9},{9,10},{10,1... | collective-permute-start | bytes 245768 | tf_op jit(solution)/shard_map/ppermute | solution.py:421
  72.5 4.4 %collective-permute-start.13 = (bf16[320,128]{1,0:T(8,128)(2,1)S(1)}, bf16[320,128]{1,0:T(8,128)(2,1)S(1)}, u32[]{:S(2)}, u32[]{:S(2)}) collective-permute-start(bf16[320,128]{1,0:T(8,128)(2,1)S(1)} %collective-permute-done.9.refs_2_), channel_id=1, source_target_pairs={{0,1},{1,2},{2,3},{3,4},{4,5},{5,6},{6,7},{7,0},{8,9},{9,10},{10,1... | collective-permute-start | bytes 245768 | tf_op jit(solution)/shard_map/ppermute | solution.py:433
  73.4 4.4 %collective-permute-start.14 = (bf16[320,128]{1,0:T(8,128)(2,1)S(1)}, bf16[320,128]{1,0:T(8,128)(2,1)S(1)}, u32[]{:S(2)}, u32[]{:S(2)}) collective-permute-start(bf16[320,128]{1,0:T(8,128)(2,1)S(1)} %collective-permute-done.12.refs_4_), channel_id=1, source_target_pairs={{0,7},{1,0},{2,1},{3,2},{4,3},{5,4},{6,5},{7,6},{8,15},{9,8},{10,9... | collective-permute-start | bytes 245768 | tf_op jit(solution)/shard_map/ppermute | solution.py:434

commit v6 on v5

--- a/solution.py
+++ b/solution.py
@@ -266,17 +266,26 @@
 
 def apply_kernel(place, *refs):
     blocks = refs[: len(LATE)]
-    early, inverse, entry, turned, carried, padded = refs[len(LATE) :]
+    early, inverse, entry, leave, turned, send, padded = refs[len(LATE) :]
     value = early[...] + windows(place, blocks, LATE, inverse, padded)
     turned[...] = value.T
     low = value.astype(BF16)
     half = value.shape[1] // 2
-    c = half // carried.shape[0]
-    put(carried, 0, c, dot16(low, entry[0], TN)[:half])
-    put(carried, c, c, dot16(low, entry[1], TN)[half:])
-
-
-def routes_kernel(place, whole, other, before, y1, y2, y3, x1, x2, x3, leave, reach):
+    first = dot16(low, entry[0], TN)[:half]
+    second = dot16(low, entry[1], TN)[half:]
+    n = first.shape[1]
+    values = dot_parts(jnp.concatenate([first, second], axis=1), leave, NT)
+    own, chip = values[:, :n], values[:, n:]
+    c = send.shape[1] // 2
+    groups = half // c
+    for k in range(send.shape[0]):
+        row = (k % groups) * c
+        send[k, :c] = chip[row : row + c]
+        same = place[2] == k // groups
+        send[k, c:] = jnp.where(same, second[row : row + c], own[row : row + c])
+
+
+def routes_kernel(place, whole, other, y1, y2, y3, x1, x2, x3, leave, reach):
     couple0, couple1, _, _ = pieces(whole)
     n = couple0.shape[0]
     rows = lax.broadcasted_iota(jnp.int32, (n, n), 0)
@@ -287,7 +296,7 @@
     out = dot32(lower, couple0, NN)
     chip = jnp.concatenate([lower, out], axis=1)
     top = jnp.concatenate([identity, couple0], axis=1)
-    store_parts(leave, jnp.concatenate([top, chip, dot32(before[:n], chip, NN)], axis=0))
+    store_parts(leave, jnp.concatenate([top, chip], axis=0))
     here = jnp.where(core == 0, other[:n], identity)
     blocks = [identity]
     for e, ref in ((1, y3), (2, y2), (3, y1)):
@@ -301,35 +310,37 @@
     store_parts(reach, jnp.concatenate([stacked, dot32(couple1, stacked, NN)], axis=0))
 
 
-def back_kernel(place, parts, leave, carried, send):
-    c = parts.shape[1] // 2
-    total = parts[0]
-    for k in range(1, parts.shape[0]):
-        total = total + parts[k]
-    carried[...] = total
-    n = total.shape[1]
-    x, y = place[0], place[1]
-    values = dot_parts(jnp.concatenate([total[:c], total[c:]], axis=1), leave, NT)
-    own, chip, group = values[:, :n], values[:, n : 2 * n], values[:, 2 * n :]
+def back_kernel(place, got, before, carried, send):
+    c = carried.shape[0] // 2
+    n = carried.shape[1]
+    groups = got.shape[0] // 2
+    core = place[2]
+
+    def summed(base, rows):
+        total = got[base, rows]
+        for k in range(1, groups):
+            total = total + got[base + k, rows]
+        return total
+
+    upper, lower = slice(0, c), slice(c, 2 * c)
+    chip = summed(0, upper) + summed(groups, upper)
+    carried[:c] = summed((1 - core) * groups, lower)
+    carried[c:] = summed(core * groups, lower)
+    group = dot32(chip, before[:n], NT)
     for k in range(send.shape[0]):
-        same_x = x == k // 8
-        same_y = y == (k // 2) % 4
-        send[k] = jnp.where(same_x, jnp.where(same_y, own, chip), group)
+        send[k] = jnp.where(place[0] == k // 4, chip, group)
 
 
 def behind_kernel(place, got, carried, reach, out):
     n = carried.shape[1]
     c = carried.shape[0] // 2
     x, y, core = place[0], place[1], place[2]
-    terms = [jnp.where(core == 0, got[x * 8 + y * 2 + 1], 0.0)]
+    terms = [jnp.where(core == 0, carried[:c], 0.0)]
     for e in (1, 2, 3):
-        base = x * 8 + lax.rem(y + e, 4) * 2
-        terms.append(jnp.where(y + e <= 3, got[base] + got[base + 1], 0.0))
+        terms.append(jnp.where(y + e <= 3, got[x * 4 + lax.rem(y + e, 4)], 0.0))
     for e in (1, 2, 3):
-        base = lax.rem(x + e, 4) * 8
-        extra = got[base]
-        for k in range(1, 8):
-            extra = extra + got[base + k]
+        base = lax.rem(x + e, 4) * 4
+        extra = (got[base] + got[base + 1]) + (got[base + 2] + got[base + 3])
         terms.append(jnp.where(x + e <= 3, extra, 0.0))
     values = dot_parts(jnp.concatenate(terms, axis=1), reach, NT)
     state = values[:, :n]
@@ -423,8 +434,8 @@
     leave, reach = call(
         routes_kernel,
         place,
-        (whole, other, before, y1, y2, y3, x1, x2, x3),
-        (of((3, 3 * n, 2 * n), BF16), of((3, 2 * n, 7 * n), BF16)),
+        (whole, other, y1, y2, y3, x1, x2, x3),
+        (of((3, 2 * n, 2 * n), BF16), of((3, 2 * n, 7 * n), BF16)),
         cost=1 << 29,
     )
     blocks[2], blocks[4], blocks[6], leave, reach = lax.optimization_barrier(
@@ -442,21 +453,21 @@
         [pltpu.VMEM((len(EARLY), room, 2 * cols), BF16)],
         cost=1 << 29,
     )
-    turned_applied, carried_parts = call(
+    turned_applied, leaving = call(
         apply_kernel,
         place,
-        (*[blocks[d] for d in LATE], early, block_inverse, entry_v),
-        (of((2 * cols, local)), of((z, 2 * c, n))),
+        (*[blocks[d] for d in LATE], early, block_inverse, entry_v, leave),
+        (of((2 * cols, local)), of((2 * z, 2 * c, n))),
         [pltpu.VMEM((len(LATE), room, 2 * cols), BF16)],
     )
     carried, send = call(
         back_kernel,
         place,
-        (exchange(carried_parts, COL), leave),
-        (of((2 * c, n)), of((chain, c, n))),
+        (exchange(leaving, (CORE, COL)), before),
+        (of((2 * c, n)), of((chain // 2, c, n))),
     )
     behind = call(
-        behind_kernel, place, (exchange(send, CHAIN), carried, reach), of((z, 2 * c, n))
+        behind_kernel, place, (exchange(send, (X, Y)), carried, reach), of((z, 2 * c, n))
     )
     return call(
         final_kernel,

time: 122 us -> 122 us (level)
  transfers between devices with their start and end apart: 15 -> 15, of which waited for: 11 -> 11; matrix products, arithmetic and copies ran while one was open for 0% -> 0% of each run, Pallas kernels for 6% -> 5%
where the time goes in v6:
time: 122 us; the launch traced here: 121 us
  blocking collectives  67.5 us (55%)
  starting transfers between devices  20.4 us (17%)
  Pallas kernels  16.6 us (14%)
  waiting for transfers between devices  15.5 us (13%)
    all_to_all x5, blocking collectives, exchange(): return lax.all_to_all(value, axes, split_axis=0, concat_axis=0, tiled=True)  67.5 us
    pallas_call x13, Pallas kernels, call(): pl.pallas_call(kernel, out_shape=outs, in_specs=[smem()] + (specs or [vme...  16.6 us
    ppermute x6, starting transfers between devices, ring(): lax.ppermute(value, axis, [(i, (i + d) % size) for i in range(size)])  8.55 us
    ppermute x6, waiting for transfers between devices, ring(): lax.ppermute(value, axis, [(i, (i + d) % size) for i in range(size)])  6.8 us
    ppermute x1, starting transfers between devices, shards(): lax.ppermute(exit_[:1], CHAIN, [(i, (i - 1) % chain) for i in range(chain)])  4.65 us
    ppermute x1, waiting for transfers between devices, shards(): blocks[7] = lax.ppermute(forward, COL, down)  3.83 us
  transfers between devices with their start and end apart: 15, of which 11 were waited for; matrix products, arithmetic and copies ran while one was open for 0% of the time, Pallas kernels for 5%

profile of v6, /device:TPU:32, one launch (start us, length us, event | category | flops | bytes accessed | tf_op | source)
XLA Modules:
  0.0 121.1 jit_solution(15329346050842777713)
XLA Ops:
  0.0 0.9 slice.3
  0.9 4.6 %collective-permute-start = (bf16[1,320,128]{2,1,0:T(8,128)(2,1)S(1)}, bf16[1,320,128]{2,1,0:T(8,128)(2,1)S(1)}, u32[]{:S(2)}, u32[]{:S(2)}) collective-permute-start(bf16[1,320,128]{2,1,0:T(8,128)(2,1)S(1)} %slice.3), channel_id=1, source_target_pairs={{0,248},{8,0},{16,8},{24,16},{32,24},{40,32},{48,40},{56,48},{64,5... | collective-permute-start | bytes 245768 | tf_op jit(solution)/shard_map/ppermute | solution.py:380
  5.6 1.9 %shard_map.55 = (bf16[2,320,128]{2,1,0:T(8,128)(2,1)S(1)}, bf16[2,320,128]{2,1,0:T(8,128)(2,1)S(1)}, bf16[64,320]{1,0:T(8,128)(2,1)S(1)}, f32[320,128]{1,0:T(8,128)S(1)}, f32[8,24,128]{2,1,0:T(8,128)S(1)}) custom-call(s32[4]{0:T(128)S(1)} %pad_add_fusion.place, bf16[2,320,128]{2,1,0:T(8,128)(2,1)} %entry.1, bf16[2,320,128]{2,1,0:T(8,128)(2,1)} %exit_.1, ...), custom_call_target="tpu_custom_call" | custom-call | flops 268435456 | bytes 2684354 | tf_op jit(solution)/shard_map/pallas_call | solution.py:71
  8.4 16.7 %all_to_all.25.parts = f32[8,48,128]{2,1,0:T(8,128)S(1)} all-to-all(f32[8,48,128]{2,1,0:T(8,128)S(1)} %shard_map.56), channel_id=1, replica_groups=mesh['chain_0'=4,'chain_1'=4,'chain_2'=2,'col'=8] {'col'}, dimensions={0} | all-to-all | bytes 393216 | tf_op jit(solution)/shard_map/all_to_all | solution.py:363
  25.6 12.3 %all_to_all.26.mine.whole = f32[8,48,128]{2,1,0:T(8,128)S(1)} all-to-all(f32[8,48,128]{2,1,0:T(8,128)S(1)} %shard_map.57), channel_id=1, replica_groups=mesh['chain_0'=4,'chain_1'=4,'chain_2'=2,'col'=8] {'col'}, dimensions={0} | all-to-all | bytes 393216 | tf_op jit(solution)/shard_map/all_to_all | solution.py:363
  37.9 1.4 %collective-permute-done.1.other = f32[8,48,128]{2,1,0:T(8,128)S(1)} collective-permute-done((f32[8,48,128]{2,1,0:T(8,128)S(1)}, f32[8,48,128]{2,1,0:T(8,128)S(1)}, u32[]{:S(2)}, u32[]{:S(2)}) %collective-permute-start.1) | collective-permute-done | bytes 196640 | tf_op jit(solution)/shard_map/ppermute | solution.py:405
  39.4 1.2 shard_map.58
  40.7 1.8 %collective-permute-start.3 = (f32[192,128]{1,0:T(8,128)S(1)}, f32[192,128]{1,0:T(8,128)S(1)}, u32[]{:S(2)}, u32[]{:S(2)}) collective-permute-start(f32[192,128]{1,0:T(8,128)S(1)} %get-tuple-element.32.mine), channel_id=1, source_target_pairs={{0,32},{16,48},{32,0},{48,16},{1,33},{17,49},{33,1},{49,17},{2,34}... | collective-permute-start | bytes 294920 | tf_op jit(solution)/shard_map/ppermute | solution.py:369
  42.6 2.5 %collective-permute-start.4 = (f32[192,128]{1,0:T(8,128)S(1)}, f32[192,128]{1,0:T(8,128)S(1)}, u32[]{:S(2)}, u32[]{:S(2)}) collective-permute-start(f32[192,128]{1,0:T(8,128)S(1)} %get-tuple-element.32.mine), channel_id=1, source_target_pairs={{0,48},{16,0},{32,16},{48,32},{1,49},{17,1},{33,17},{49,33},{2,50}... | collective-permute-start | bytes 294920 | tf_op jit(solution)/shard_map/ppermute | solution.py:369
  45.1 3.7 %collective-permute-done.2.one.y1 = f32[192,128]{1,0:T(8,128)S(1)} collective-permute-done((f32[192,128]{1,0:T(8,128)S(1)}, f32[192,128]{1,0:T(8,128)S(1)}, u32[]{:S(2)}, u32[]{:S(2)}) %collective-permute-start.2) | collective-permute-done | bytes 98336 | tf_op jit(solution)/shard_map/ppermute | solution.py:369
  49.4 1.2 shard_map.59
  50.7 2.5 %collective-permute-start.6 = (f32[192,128]{1,0:T(8,128)S(1)}, f32[192,128]{1,0:T(8,128)S(1)}, u32[]{:S(2)}, u32[]{:S(2)}) collective-permute-start(f32[192,128]{1,0:T(8,128)S(1)} %get-tuple-element.36.own), channel_id=1, source_target_pairs={{0,128},{64,192},{128,0},{192,64},{1,129},{65,193},{129,1},{193,65... | collective-permute-start | bytes 294920 | tf_op jit(solution)/shard_map/ppermute | solution.py:369
  53.2 1.4 %collective-permute-start.7 = (f32[192,128]{1,0:T(8,128)S(1)}, f32[192,128]{1,0:T(8,128)S(1)}, u32[]{:S(2)}, u32[]{:S(2)}) collective-permute-start(f32[192,128]{1,0:T(8,128)S(1)} %get-tuple-element.36.own), channel_id=1, source_target_pairs={{0,192},{64,0},{128,64},{192,128},{1,193},{65,1},{129,65},{193,129... | collective-permute-start | bytes 294920 | tf_op jit(solution)/shard_map/ppermute | solution.py:369
  54.6 1.3 %shard_map.60 = (f32[128,256]{1,0:T(8,128)S(1)}, f32[64,256]{1,0:T(8,128)S(1)}, f32[192,128]{1,0:T(8,128)S(1)}) custom-call(s32[4]{0:T(128)S(1)} %pad_add_fusion.place, f32[8,48,128]{2,1,0:T(8,128)S(1)} %all_to_all.26.mine.whole, f32[192,128]{1,0:T(8,128)S(1)} %get-tuple-element.31.other, f32[192,128]{1,0:T(8,128)S(1)} %get-tuple-element.33.low, ...), custom_call_target="tpu_custom_call" | custom-call | flops 134217728 | bytes 1342177 | tf_op jit(solution)/shard_map/pallas_call | solution.py:71
  55.9 2.0 %collective-permute-done.5.one.x1 = f32[192,128]{1,0:T(8,128)S(1)} collective-permute-done((f32[192,128]{1,0:T(8,128)S(1)}, f32[192,128]{1,0:T(8,128)S(1)}, u32[]{:S(2)}, u32[]{:S(2)}) %collective-permute-start.5) | collective-permute-done | bytes 98336 | tf_op jit(solution)/shard_map/ppermute | solution.py:369
  58.4 1.5 %shard_map.61.refs_0_ = bf16[320,128]{1,0:T(8,128)(2,1)S(1)} custom-call(s32[4]{0:T(128)S(1)} %pad_add_fusion.place, f32[128,256]{1,0:T(8,128)S(1)} %get-tuple-element.34.maps, f32[64,256]{1,0:T(8,128)S(1)} %get-tuple-element.35.shifts, f32[192,128]{1,0:T(8,128)S(1)} %get-tuple-element.36.own, f32[192,128]{1,0:T(8,128)S(1)} %collective-permute-done.5.one.x1, ...), custom_call_target="tpu_custom_call" | custom-call | tf_op jit(solution)/shard_map/pallas_call | solution.py:71
  59.9 1.5 %collective-permute-start.11 = (bf16[320,128]{1,0:T(8,128)(2,1)S(1)}, bf16[320,128]{1,0:T(8,128)(2,1)S(1)}, u32[]{:S(2)}, u32[]{:S(2)}) collective-permute-start(bf16[320,128]{1,0:T(8,128)(2,1)S(1)} %shard_map.61.refs_0_), channel_id=1, source_target_pairs={{0,7},{1,0},{2,1},{3,2},{4,3},{5,4},{6,5},{7,6},{8,15},{9,8},{10,9... | collective-permute-start | bytes 245768 | tf_op jit(solution)/shard_map/ppermute | solution.py:430
  62.0 1.0 collective-permute-start.10
  63.1 3.8 %collective-permute-done.11.refs_5_ = bf16[320,128]{1,0:T(8,128)(2,1)S(1)} collective-permute-done((bf16[320,128]{1,0:T(8,128)(2,1)S(1)}, bf16[320,128]{1,0:T(8,128)(2,1)S(1)}, u32[]{:S(2)}, u32[]{:S(2)}) %collective-permute-start.11) | collective-permute-done | bytes 81952 | tf_op jit(solution)/shard_map/ppermute | solution.py:430
  67.5 1.5 %collective-permute-start.9 = (bf16[320,128]{1,0:T(8,128)(2,1)S(1)}, bf16[320,128]{1,0:T(8,128)(2,1)S(1)}, u32[]{:S(2)}, u32[]{:S(2)}) collective-permute-start(bf16[320,128]{1,0:T(8,128)(2,1)S(1)} %collective-permute-done.8.refs_1_), channel_id=1, source_target_pairs={{0,1},{1,2},{2,3},{3,4},{4,5},{5,6},{6,7},{7,0},{8,9},{9,10},{10,1... | collective-permute-start | bytes 245768 | tf_op jit(solution)/shard_map/ppermute | solution.py:432
  68.9 2.0 %shard_map.62 = (bf16[3,256,256]{2,1,0:T(8,128)(2,1)S(1)}, bf16[3,256,896]{2,1,0:T(8,128)(2,1)S(1)}) custom-call(s32[4]{0:T(128)S(1)} %pad_add_fusion.place, f32[8,48,128]{2,1,0:T(8,128)S(1)} %all_to_all.26.mine.whole, f32[192,128]{1,0:T(8,128)S(1)} %get-tuple-element.31.other, f32[192,128]{1,0:T(8,128)S(1)} %collective-permute-done.2.one.y1, ...), custom_call_target="tpu_custom_call" | custom-call | flops 536870912 | bytes 5368709 | tf_op jit(solution)/shard_map/pallas_call | solution.py:71
  70.9 1.3 %collective-permute-done.12.refs_4_ = bf16[320,128]{1,0:T(8,128)(2,1)S(1)} collective-permute-done((bf16[320,128]{1,0:T(8,128)(2,1)S(1)}, bf16[320,128]{1,0:T(8,128)(2,1)S(1)}, u32[]{:S(2)}, u32[]{:S(2)}) %collective-permute-start.12) | collective-permute-done | bytes 81952 | tf_op jit(solution)/shard_map/ppermute | solution.py:433
  72.5 0.9 collective-permute-start.13
  73.4 1.1 collective-permute-start.14
  74.5 1.5 %shard_map.63.refs_2_ = f32[320,128]{1,0:T(8,128)S(1)} custom-call(s32[4]{0:T(128)S(1)} %pad_add_fusion.place, bf16[320,128]{1,0:T(8,128)(2,1)S(1)} %shard_map.61.refs_0_, bf16[320,128]{1,0:T(8,128)(2,1)S(1)} %collective-permute-done.8.refs_1_, bf16[320,128]{1,0:T(8,128)(2,1)S(1)} %collective-permute-done.9.refs_2_, ...), custom_call_target="tpu_custom_call" | custom-call | flops 536870912 | bytes 5368709 | tf_op jit(solution)/shard_map/pallas_call | solution.py:71
  76.9 0.9 collective-permute-done.14.refs_1_
  77.8 1.5 %shard_map.64 = (f32[128,320]{1,0:T(8,128)S(1)}, f32[16,16,128]{2,1,0:T(8,128)S(1)}) custom-call(s32[4]{0:T(128)S(1)} %pad_add_fusion.place, bf16[320,128]{1,0:T(8,128)(2,1)S(1)} %collective-permute-done.13.refs_0_, bf16[320,128]{1,0:T(8,128)(2,1)S(1)} %collective-permute-done.14.refs_1_, f32[320,128]{1,0:T(8,128)S(1)} %shard_map.63.refs_2_, ...), custom_call_target="tpu_custom_call" | custom-call | tf_op jit(solution)/shard_map/pallas_call | solution.py:71
  79.4 14.1 %all_to_all.27.got = f32[16,16,128]{2,1,0:T(8,128)S(1)} all-to-all(f32[16,16,128]{2,1,0:T(8,128)S(1)} %get-tuple-element.44), channel_id=1, replica_groups=mesh['chain_0'=4,'chain_1'=4,'chain_2'=2,'col'=8] {'chain_2','col'}, dimensions={0} | all-to-all | bytes 262144 | tf_op jit(solution)/shard_map/all_to_all | solution.py:363
  94.1 14.2 %all_to_all.28.got = f32[16,8,128]{2,1,0:T(8,128)S(1)} all-to-all(f32[16,8,128]{2,1,0:T(8,128)S(1)} %get-tuple-element.46), channel_id=1, replica_groups=mesh['chain_0'=4,'chain_1'=4,'chain_2'=2,'col'=8] {'chain_0','chain_1'}, dimensions={0} | all-to-all | bytes 131072 | tf_op jit(solution)/shard_map/all_to_all | solution.py:363
  108.3 1.0 shard_map.66
  109.3 10.3 %all_to_all.29.got = f32[8,16,128]{2,1,0:T(8,128)S(1)} all-to-all(f32[8,16,128]{2,1,0:T(8,128)S(1)} %shard_map.66), channel_id=1, replica_groups=mesh['chain_0'=4,'chain_1'=4,'chain_2'=2,'col'=8] {'col'}, dimensions={0} | all-to-all | bytes 131072 | tf_op jit(solution)/shard_map/all_to_all | solution.py:363
  119.6 1.5 %shard_map.67 = f32[2,64,320]{2,1,0:T(8,128)} custom-call(s32[4]{0:T(128)S(1)} %pad_add_fusion.place, f32[8,16,128]{2,1,0:T(8,128)S(1)} %all_to_all.29.got, f32[128,320]{1,0:T(8,128)S(1)} %get-tuple-element.49.turned, bf16[2,320,128]{2,1,0:T(8,128)(2,1)S(1)} %get-tuple-element.50.exit_, bf16[1,320,128]{2,1,0:T(8,128)(2,1)S(1)} %collective-permute-done.arriving), custom_call_target="tpu_custom_call" | custom-call | tf_op jit(solution)/shard_map/pallas_call | solution.py:71
  (20 shorter events, 5.8 us)
Async XLA Ops:
  0.9 6.7 %collective-permute-start = (bf16[1,320,128]{2,1,0:T(8,128)(2,1)S(1)}, bf16[1,320,128]{2,1,0:T(8,128)(2,1)S(1)}, u32[]{:S(2)}, u32[]{:S(2)}) collective-permute-start(bf16[1,320,128]{2,1,0:T(8,128)(2,1)S(1)} %slice.3), channel_id=1, source_target_pairs={{0,248},{8,0},{16,8},{24,16},{32,24},{40,32},{48,40},{56,48},{64,5... | collective-permute-start | bytes 245768 | tf_op jit(solution)/shard_map/ppermute | solution.py:380
  7.5 67.0 %copy-start = (bf16[2,320,2560]{2,1,0:T(8,128)(2,1)S(1)}, bf16[2,320,2560]{2,1,0:T(8,128)(2,1)}, u32[]{:S(2)}) copy-start(bf16[2,320,2560]{2,1,0:T(8,128)(2,1)} %refs_3_.1) | copy-start | bytes 9830404
  37.9 1.4 %collective-permute-start.1 = (f32[8,48,128]{2,1,0:T(8,128)S(1)}, f32[8,48,128]{2,1,0:T(8,128)S(1)}, u32[]{:S(2)}, u32[]{:S(2)}) collective-permute-start(f32[8,48,128]{2,1,0:T(8,128)S(1)} %all_to_all.26.mine.whole), channel_id=1, source_target_pairs={{0,8},{8,0},{1,9},{9,1},{2,10},{10,2},{3,11},{11,3},{4,12},{12,4},... | collective-permute-start | bytes 589832 | tf_op jit(solution)/shard_map/ppermute | solution.py:405
  40.6 8.2 %collective-permute-start.2 = (f32[192,128]{1,0:T(8,128)S(1)}, f32[192,128]{1,0:T(8,128)S(1)}, u32[]{:S(2)}, u32[]{:S(2)}) collective-permute-start(f32[192,128]{1,0:T(8,128)S(1)} %get-tuple-element.32.mine), channel_id=1, source_target_pairs={{0,16},{16,32},{32,48},{48,0},{1,17},{17,33},{33,49},{49,1},{2,18}... | collective-permute-start | bytes 294920 | tf_op jit(solution)/shard_map/ppermute | solution.py:369
  40.7 8.1 %collective-permute-start.3 = (f32[192,128]{1,0:T(8,128)S(1)}, f32[192,128]{1,0:T(8,128)S(1)}, u32[]{:S(2)}, u32[]{:S(2)}) collective-permute-start(f32[192,128]{1,0:T(8,128)S(1)} %get-tuple-element.32.mine), channel_id=1, source_target_pairs={{0,32},{16,48},{32,0},{48,16},{1,33},{17,49},{33,1},{49,17},{2,34}... | collective-permute-start | bytes 294920 | tf_op jit(solution)/shard_map/ppermute | solution.py:369
  42.6 6.8 %collective-permute-start.4 = (f32[192,128]{1,0:T(8,128)S(1)}, f32[192,128]{1,0:T(8,128)S(1)}, u32[]{:S(2)}, u32[]{:S(2)}) collective-permute-start(f32[192,128]{1,0:T(8,128)S(1)} %get-tuple-element.32.mine), channel_id=1, source_target_pairs={{0,48},{16,0},{32,16},{48,32},{1,49},{17,1},{33,17},{49,33},{2,50}... | collective-permute-start | bytes 294920 | tf_op jit(solution)/shard_map/ppermute | solution.py:369
  50.6 7.3 %collective-permute-start.5 = (f32[192,128]{1,0:T(8,128)S(1)}, f32[192,128]{1,0:T(8,128)S(1)}, u32[]{:S(2)}, u32[]{:S(2)}) collective-permute-start(f32[192,128]{1,0:T(8,128)S(1)} %get-tuple-element.36.own), channel_id=1, source_target_pairs={{0,64},{64,128},{128,192},{192,0},{1,65},{65,129},{129,193},{193,1... | collective-permute-start | bytes 294920 | tf_op jit(solution)/shard_map/ppermute | solution.py:369
  50.7 7.2 %collective-permute-start.6 = (f32[192,128]{1,0:T(8,128)S(1)}, f32[192,128]{1,0:T(8,128)S(1)}, u32[]{:S(2)}, u32[]{:S(2)}) collective-permute-start(f32[192,128]{1,0:T(8,128)S(1)} %get-tuple-element.36.own), channel_id=1, source_target_pairs={{0,128},{64,192},{128,0},{192,64},{1,129},{65,193},{129,1},{193,65... | collective-permute-start | bytes 294920 | tf_op jit(solution)/shard_map/ppermute | solution.py:369
  53.2 5.2 %collective-permute-start.7 = (f32[192,128]{1,0:T(8,128)S(1)}, f32[192,128]{1,0:T(8,128)S(1)}, u32[]{:S(2)}, u32[]{:S(2)}) collective-permute-start(f32[192,128]{1,0:T(8,128)S(1)} %get-tuple-element.36.own), channel_id=1, source_target_pairs={{0,192},{64,0},{128,64},{192,128},{1,193},{65,1},{129,65},{193,129... | collective-permute-start | bytes 294920 | tf_op jit(solution)/shard_map/ppermute | solution.py:369
  59.9 7.0 %collective-permute-start.11 = (bf16[320,128]{1,0:T(8,128)(2,1)S(1)}, bf16[320,128]{1,0:T(8,128)(2,1)S(1)}, u32[]{:S(2)}, u32[]{:S(2)}) collective-permute-start(bf16[320,128]{1,0:T(8,128)(2,1)S(1)} %shard_map.61.refs_0_), channel_id=1, source_target_pairs={{0,7},{1,0},{2,1},{3,2},{4,3},{5,4},{6,5},{7,6},{8,15},{9,8},{10,9... | collective-permute-start | bytes 245768 | tf_op jit(solution)/shard_map/ppermute | solution.py:430
  61.4 6.0 %collective-permute-start.8 = (bf16[320,128]{1,0:T(8,128)(2,1)S(1)}, bf16[320,128]{1,0:T(8,128)(2,1)S(1)}, u32[]{:S(2)}, u32[]{:S(2)}) collective-permute-start(bf16[320,128]{1,0:T(8,128)(2,1)S(1)} %shard_map.61.refs_0_), channel_id=1, source_target_pairs={{0,1},{1,2},{2,3},{3,4},{4,5},{5,6},{6,7},{7,0},{8,9},{9,10},{10,1... | collective-permute-start | bytes 245768 | tf_op jit(solution)/shard_map/ppermute | solution.py:429
  62.0 8.9 %collective-permute-start.10 = (bf16[320,128]{1,0:T(8,128)(2,1)S(1)}, bf16[320,128]{1,0:T(8,128)(2,1)S(1)}, u32[]{:S(2)}, u32[]{:S(2)}) collective-permute-start(bf16[320,128]{1,0:T(8,128)(2,1)S(1)} %shard_map.61.refs_0_), channel_id=1, source_target_pairs={{0,4},{1,5},{2,6},{3,7},{4,0},{5,1},{6,2},{7,3},{8,12},{9,13},{10,... | collective-permute-start | bytes 245768 | tf_op jit(solution)/shard_map/ppermute | solution.py:431
  66.9 5.3 %collective-permute-start.12 = (bf16[320,128]{1,0:T(8,128)(2,1)S(1)}, bf16[320,128]{1,0:T(8,128)(2,1)S(1)}, u32[]{:S(2)}, u32[]{:S(2)}) collective-permute-start(bf16[320,128]{1,0:T(8,128)(2,1)S(1)} %collective-permute-done.11.refs_5_), channel_id=1, source_target_pairs={{0,7},{1,0},{2,1},{3,2},{4,3},{5,4},{6,5},{7,6},{8,15},{9,8},{10,9... | collective-permute-start | bytes 245768 | tf_op jit(solution)/shard_map/ppermute | solution.py:433
  67.5 5.0 %collective-permute-start.9 = (bf16[320,128]{1,0:T(8,128)(2,1)S(1)}, bf16[320,128]{1,0:T(8,128)(2,1)S(1)}, u32[]{:S(2)}, u32[]{:S(2)}) collective-permute-start(bf16[320,128]{1,0:T(8,128)(2,1)S(1)} %collective-permute-done.8.refs_1_), channel_id=1, source_target_pairs={{0,1},{1,2},{2,3},{3,4},{4,5},{5,6},{6,7},{7,0},{8,9},{9,10},{10,1... | collective-permute-start | bytes 245768 | tf_op jit(solution)/shard_map/ppermute | solution.py:432
  72.5 4.4 %collective-permute-start.13 = (bf16[320,128]{1,0:T(8,128)(2,1)S(1)}, bf16[320,128]{1,0:T(8,128)(2,1)S(1)}, u32[]{:S(2)}, u32[]{:S(2)}) collective-permute-start(bf16[320,128]{1,0:T(8,128)(2,1)S(1)} %collective-permute-done.9.refs_2_), channel_id=1, source_target_pairs={{0,1},{1,2},{2,3},{3,4},{4,5},{5,6},{6,7},{7,0},{8,9},{9,10},{10,1... | collective-permute-start | bytes 245768 | tf_op jit(solution)/shard_map/ppermute | solution.py:444
  73.4 4.4 %collective-permute-start.14 = (bf16[320,128]{1,0:T(8,128)(2,1)S(1)}, bf16[320,128]{1,0:T(8,128)(2,1)S(1)}, u32[]{:S(2)}, u32[]{:S(2)}) collective-permute-start(bf16[320,128]{1,0:T(8,128)(2,1)S(1)} %collective-permute-done.12.refs_4_), channel_id=1, source_target_pairs={{0,7},{1,0},{2,1},{3,2},{4,3},{5,4},{6,5},{7,6},{8,15},{9,8},{10,9... | collective-permute-start | bytes 245768 | tf_op jit(solution)/shard_map/ppermute | solution.py:445

commit v7 on v5

--- a/solution.py
+++ b/solution.py
@@ -209,9 +209,10 @@
     n = one.shape[1]
     x = place[0]
     state = jnp.where(x == 3, own[n:], 0.0)
-    for d, ref in ((3, three), (2, two), (1, one)):
+    for d, ref in ((3, three), (2, two)):
         state = jnp.where(d <= x + 1, dot32(state, ref[:n], NN) + ref[n:], state)
-    both = dot32(state, maps[...], NN) + shifts[...]
+    onward = dot32(one[...], maps[...], NN)
+    both = dot32(state, onward[:n], NN) + (onward[n:] + shifts[...])
     states = jnp.concatenate([both[:, :n], both[:, n:]], axis=0)
     high, middle, low = (part.astype(BF16) for part in three_parts(states))
     factor = jnp.concatenate(

time: 122 us -> 122 us (level)
  no operation moved by 1% of the time
where the time goes in v7:
time: 122 us; the launch traced here: 121 us
  blocking collectives  67.2 us (55%)
  starting transfers between devices  20.4 us (17%)
  Pallas kernels  16.5 us (14%)
  waiting for transfers between devices  15.4 us (13%)
    all_to_all x5, blocking collectives, exchange(): return lax.all_to_all(value, axes, split_axis=0, concat_axis=0, tiled=True)  67.2 us
    pallas_call x13, Pallas kernels, call(): pl.pallas_call(kernel, out_shape=outs, in_specs=[smem()] + (specs or [vme...  16.5 us
    ppermute x6, starting transfers between devices, ring(): lax.ppermute(value, axis, [(i, (i + d) % size) for i in range(size)])  8.55 us
    ppermute x6, waiting for transfers between devices, ring(): lax.ppermute(value, axis, [(i, (i + d) % size) for i in range(size)])  6.8 us
    ppermute x1, starting transfers between devices, shards(): lax.ppermute(exit_[:1], CHAIN, [(i, (i - 1) % chain) for i in range(chain)])  4.65 us
    ppermute x1, waiting for transfers between devices, shards(): blocks[7] = lax.ppermute(forward, COL, down)  3.83 us
  transfers between devices with their start and end apart: 15, of which 11 were waited for; matrix products, arithmetic and copies ran while one was open for 0% of the time, Pallas kernels for 6%

profile of v7, /device:TPU:32, one launch (start us, length us, event | category | flops | bytes accessed | tf_op | source)
XLA Modules:
  0.0 120.6 jit_solution(10418342820466577026)
XLA Ops:
  0.0 0.9 slice.3
  0.9 4.6 %collective-permute-start = (bf16[1,320,128]{2,1,0:T(8,128)(2,1)S(1)}, bf16[1,320,128]{2,1,0:T(8,128)(2,1)S(1)}, u32[]{:S(2)}, u32[]{:S(2)}) collective-permute-start(bf16[1,320,128]{2,1,0:T(8,128)(2,1)S(1)} %slice.3), channel_id=1, source_target_pairs={{0,248},{8,0},{16,8},{24,16},{32,24},{40,32},{48,40},{56,48},{64,5... | collective-permute-start | bytes 245768 | tf_op jit(solution)/shard_map/ppermute | solution.py:370
  5.6 1.9 %shard_map.55 = (bf16[2,320,128]{2,1,0:T(8,128)(2,1)S(1)}, bf16[2,320,128]{2,1,0:T(8,128)(2,1)S(1)}, bf16[64,320]{1,0:T(8,128)(2,1)S(1)}, f32[320,128]{1,0:T(8,128)S(1)}, f32[8,24,128]{2,1,0:T(8,128)S(1)}) custom-call(s32[4]{0:T(128)S(1)} %pad_add_fusion.place, bf16[2,320,128]{2,1,0:T(8,128)(2,1)} %entry.1, bf16[2,320,128]{2,1,0:T(8,128)(2,1)} %exit_.1, ...), custom_call_target="tpu_custom_call" | custom-call | flops 268435456 | bytes 2684354 | tf_op jit(solution)/shard_map/pallas_call | solution.py:71
  8.4 16.7 %all_to_all.25.parts = f32[8,48,128]{2,1,0:T(8,128)S(1)} all-to-all(f32[8,48,128]{2,1,0:T(8,128)S(1)} %shard_map.56), channel_id=1, replica_groups=mesh['chain_0'=4,'chain_1'=4,'chain_2'=2,'col'=8] {'col'}, dimensions={0} | all-to-all | bytes 393216 | tf_op jit(solution)/shard_map/all_to_all | solution.py:353
  25.6 12.3 %all_to_all.26.mine.whole = f32[8,48,128]{2,1,0:T(8,128)S(1)} all-to-all(f32[8,48,128]{2,1,0:T(8,128)S(1)} %shard_map.57), channel_id=1, replica_groups=mesh['chain_0'=4,'chain_1'=4,'chain_2'=2,'col'=8] {'col'}, dimensions={0} | all-to-all | bytes 393216 | tf_op jit(solution)/shard_map/all_to_all | solution.py:353
  37.9 1.4 %collective-permute-done.1.other = f32[8,48,128]{2,1,0:T(8,128)S(1)} collective-permute-done((f32[8,48,128]{2,1,0:T(8,128)S(1)}, f32[8,48,128]{2,1,0:T(8,128)S(1)}, u32[]{:S(2)}, u32[]{:S(2)}) %collective-permute-start.1) | collective-permute-done | bytes 196640 | tf_op jit(solution)/shard_map/ppermute | solution.py:395
  39.4 1.2 shard_map.58
  40.7 1.8 %collective-permute-start.3 = (f32[192,128]{1,0:T(8,128)S(1)}, f32[192,128]{1,0:T(8,128)S(1)}, u32[]{:S(2)}, u32[]{:S(2)}) collective-permute-start(f32[192,128]{1,0:T(8,128)S(1)} %get-tuple-element.32.mine), channel_id=1, source_target_pairs={{0,32},{16,48},{32,0},{48,16},{1,33},{17,49},{33,1},{49,17},{2,34}... | collective-permute-start | bytes 294920 | tf_op jit(solution)/shard_map/ppermute | solution.py:359
  42.6 2.5 %collective-permute-start.4 = (f32[192,128]{1,0:T(8,128)S(1)}, f32[192,128]{1,0:T(8,128)S(1)}, u32[]{:S(2)}, u32[]{:S(2)}) collective-permute-start(f32[192,128]{1,0:T(8,128)S(1)} %get-tuple-element.32.mine), channel_id=1, source_target_pairs={{0,48},{16,0},{32,16},{48,32},{1,49},{17,1},{33,17},{49,33},{2,50}... | collective-permute-start | bytes 294920 | tf_op jit(solution)/shard_map/ppermute | solution.py:359
  45.1 3.7 %collective-permute-done.2.one.y1 = f32[192,128]{1,0:T(8,128)S(1)} collective-permute-done((f32[192,128]{1,0:T(8,128)S(1)}, f32[192,128]{1,0:T(8,128)S(1)}, u32[]{:S(2)}, u32[]{:S(2)}) %collective-permute-start.2) | collective-permute-done | bytes 98336 | tf_op jit(solution)/shard_map/ppermute | solution.py:359
  49.4 1.2 shard_map.59
  50.7 2.5 %collective-permute-start.6 = (f32[192,128]{1,0:T(8,128)S(1)}, f32[192,128]{1,0:T(8,128)S(1)}, u32[]{:S(2)}, u32[]{:S(2)}) collective-permute-start(f32[192,128]{1,0:T(8,128)S(1)} %get-tuple-element.36.own), channel_id=1, source_target_pairs={{0,128},{64,192},{128,0},{192,64},{1,129},{65,193},{129,1},{193,65... | collective-permute-start | bytes 294920 | tf_op jit(solution)/shard_map/ppermute | solution.py:359
  53.2 1.4 %collective-permute-start.7 = (f32[192,128]{1,0:T(8,128)S(1)}, f32[192,128]{1,0:T(8,128)S(1)}, u32[]{:S(2)}, u32[]{:S(2)}) collective-permute-start(f32[192,128]{1,0:T(8,128)S(1)} %get-tuple-element.36.own), channel_id=1, source_target_pairs={{0,192},{64,0},{128,64},{192,128},{1,193},{65,1},{129,65},{193,129... | collective-permute-start | bytes 294920 | tf_op jit(solution)/shard_map/ppermute | solution.py:359
  54.6 1.3 %shard_map.60 = (f32[128,256]{1,0:T(8,128)S(1)}, f32[64,256]{1,0:T(8,128)S(1)}, f32[192,128]{1,0:T(8,128)S(1)}) custom-call(s32[4]{0:T(128)S(1)} %pad_add_fusion.place, f32[8,48,128]{2,1,0:T(8,128)S(1)} %all_to_all.26.mine.whole, f32[192,128]{1,0:T(8,128)S(1)} %get-tuple-element.31.other, f32[192,128]{1,0:T(8,128)S(1)} %get-tuple-element.33.low, ...), custom_call_target="tpu_custom_call" | custom-call | flops 134217728 | bytes 1342177 | tf_op jit(solution)/shard_map/pallas_call | solution.py:71
  55.9 2.0 %collective-permute-done.5.one.x1 = f32[192,128]{1,0:T(8,128)S(1)} collective-permute-done((f32[192,128]{1,0:T(8,128)S(1)}, f32[192,128]{1,0:T(8,128)S(1)}, u32[]{:S(2)}, u32[]{:S(2)}) %collective-permute-start.5) | collective-permute-done | bytes 98336 | tf_op jit(solution)/shard_map/ppermute | solution.py:359
  58.4 1.6 %shard_map.61.refs_0_ = bf16[320,128]{1,0:T(8,128)(2,1)S(1)} custom-call(s32[4]{0:T(128)S(1)} %pad_add_fusion.place, f32[128,256]{1,0:T(8,128)S(1)} %get-tuple-element.34.maps, f32[64,256]{1,0:T(8,128)S(1)} %get-tuple-element.35.shifts, f32[192,128]{1,0:T(8,128)S(1)} %get-tuple-element.36.own, f32[192,128]{1,0:T(8,128)S(1)} %collective-permute-done.5.one.x1, ...), custom_call_target="tpu_custom_call" | custom-call | tf_op jit(solution)/shard_map/pallas_call | solution.py:71
  60.0 1.5 %collective-permute-start.11 = (bf16[320,128]{1,0:T(8,128)(2,1)S(1)}, bf16[320,128]{1,0:T(8,128)(2,1)S(1)}, u32[]{:S(2)}, u32[]{:S(2)}) collective-permute-start(bf16[320,128]{1,0:T(8,128)(2,1)S(1)} %shard_map.61.refs_0_), channel_id=1, source_target_pairs={{0,7},{1,0},{2,1},{3,2},{4,3},{5,4},{6,5},{7,6},{8,15},{9,8},{10,9... | collective-permute-start | bytes 245768 | tf_op jit(solution)/shard_map/ppermute | solution.py:420
  62.1 1.0 collective-permute-start.10
  63.1 3.8 %collective-permute-done.11.refs_5_ = bf16[320,128]{1,0:T(8,128)(2,1)S(1)} collective-permute-done((bf16[320,128]{1,0:T(8,128)(2,1)S(1)}, bf16[320,128]{1,0:T(8,128)(2,1)S(1)}, u32[]{:S(2)}, u32[]{:S(2)}) %collective-permute-start.11) | collective-permute-done | bytes 81952 | tf_op jit(solution)/shard_map/ppermute | solution.py:420
  67.5 1.4 %collective-permute-start.9 = (bf16[320,128]{1,0:T(8,128)(2,1)S(1)}, bf16[320,128]{1,0:T(8,128)(2,1)S(1)}, u32[]{:S(2)}, u32[]{:S(2)}) collective-permute-start(bf16[320,128]{1,0:T(8,128)(2,1)S(1)} %collective-permute-done.8.refs_1_), channel_id=1, source_target_pairs={{0,1},{1,2},{2,3},{3,4},{4,5},{5,6},{6,7},{7,0},{8,9},{9,10},{10,1... | collective-permute-start | bytes 245768 | tf_op jit(solution)/shard_map/ppermute | solution.py:422
  69.0 2.0 %shard_map.62 = (bf16[3,384,256]{2,1,0:T(8,128)(2,1)S(1)}, bf16[3,256,896]{2,1,0:T(8,128)(2,1)S(1)}) custom-call(s32[4]{0:T(128)S(1)} %pad_add_fusion.place, f32[8,48,128]{2,1,0:T(8,128)S(1)} %all_to_all.26.mine.whole, f32[192,128]{1,0:T(8,128)S(1)} %get-tuple-element.31.other, f32[192,128]{1,0:T(8,128)S(1)} %get-tuple-element.38.before, ...), custom_call_target="tpu_custom_call" | custom-call | flops 536870912 | bytes 5368709 | tf_op jit(solution)/shard_map/pallas_call | solution.py:71
  71.0 1.3 %collective-permute-done.12.refs_4_ = bf16[320,128]{1,0:T(8,128)(2,1)S(1)} collective-permute-done((bf16[320,128]{1,0:T(8,128)(2,1)S(1)}, bf16[320,128]{1,0:T(8,128)(2,1)S(1)}, u32[]{:S(2)}, u32[]{:S(2)}) %collective-permute-start.12) | collective-permute-done | bytes 81952 | tf_op jit(solution)/shard_map/ppermute | solution.py:423
  73.4 1.2 collective-permute-start.14
  74.6 1.5 %shard_map.63.refs_2_ = f32[320,128]{1,0:T(8,128)S(1)} custom-call(s32[4]{0:T(128)S(1)} %pad_add_fusion.place, bf16[320,128]{1,0:T(8,128)(2,1)S(1)} %shard_map.61.refs_0_, bf16[320,128]{1,0:T(8,128)(2,1)S(1)} %collective-permute-done.8.refs_1_, bf16[320,128]{1,0:T(8,128)(2,1)S(1)} %collective-permute-done.9.refs_2_, ...), custom_call_target="tpu_custom_call" | custom-call | flops 536870912 | bytes 5368709 | tf_op jit(solution)/shard_map/pallas_call | solution.py:71
  76.2 0.9 collective-permute-done.13.refs_0_
  77.9 1.2 %shard_map.64 = (f32[128,320]{1,0:T(8,128)S(1)}, f32[8,16,128]{2,1,0:T(8,128)S(1)}) custom-call(s32[4]{0:T(128)S(1)} %pad_add_fusion.place, bf16[320,128]{1,0:T(8,128)(2,1)S(1)} %collective-permute-done.13.refs_0_, bf16[320,128]{1,0:T(8,128)(2,1)S(1)} %collective-permute-done.14.refs_1_, f32[320,128]{1,0:T(8,128)S(1)} %shard_map.63.refs_2_, ...), custom_call_target="tpu_custom_call" | custom-call | tf_op jit(solution)/shard_map/pallas_call | solution.py:71
  79.1 12.8 %all_to_all.27.parts = f32[8,16,128]{2,1,0:T(8,128)S(1)} all-to-all(f32[8,16,128]{2,1,0:T(8,128)S(1)} %get-tuple-element.44), channel_id=1, replica_groups=mesh['chain_0'=4,'chain_1'=4,'chain_2'=2,'col'=8] {'col'}, dimensions={0} | all-to-all | bytes 131072 | tf_op jit(solution)/shard_map/all_to_all | solution.py:353
  91.9 0.8 shard_map.65
  92.7 14.6 %all_to_all.28.got = f32[32,8,128]{2,1,0:T(8,128)S(1)} all-to-all(f32[32,8,128]{2,1,0:T(8,128)S(1)} %get-tuple-element.46), channel_id=1, replica_groups=mesh['chain_0'=4,'chain_1'=4,'chain_2'=2,'col'=8] {'chain_0','chain_1','..., dimensions={0} | all-to-all | bytes 262144 | tf_op jit(solution)/shard_map/all_to_all | solution.py:353
  107.4 1.0 shard_map.66
  108.4 10.8 %all_to_all.29.got = f32[8,16,128]{2,1,0:T(8,128)S(1)} all-to-all(f32[8,16,128]{2,1,0:T(8,128)S(1)} %shard_map.66), channel_id=1, replica_groups=mesh['chain_0'=4,'chain_1'=4,'chain_2'=2,'col'=8] {'col'}, dimensions={0} | all-to-all | bytes 131072 | tf_op jit(solution)/shard_map/all_to_all | solution.py:353
  119.1 1.5 %shard_map.67 = f32[2,64,320]{2,1,0:T(8,128)} custom-call(s32[4]{0:T(128)S(1)} %pad_add_fusion.place, f32[8,16,128]{2,1,0:T(8,128)S(1)} %all_to_all.29.got, f32[128,320]{1,0:T(8,128)S(1)} %get-tuple-element.49.turned, bf16[2,320,128]{2,1,0:T(8,128)(2,1)S(1)} %get-tuple-element.50.exit_, bf16[1,320,128]{2,1,0:T(8,128)(2,1)S(1)} %collective-permute-done.arriving), custom_call_target="tpu_custom_call" | custom-call | tf_op jit(solution)/shard_map/pallas_call | solution.py:71
  (20 shorter events, 5.9 us)
Async XLA Ops:
  0.9 6.7 %collective-permute-start = (bf16[1,320,128]{2,1,0:T(8,128)(2,1)S(1)}, bf16[1,320,128]{2,1,0:T(8,128)(2,1)S(1)}, u32[]{:S(2)}, u32[]{:S(2)}) collective-permute-start(bf16[1,320,128]{2,1,0:T(8,128)(2,1)S(1)} %slice.3), channel_id=1, source_target_pairs={{0,248},{8,0},{16,8},{24,16},{32,24},{40,32},{48,40},{56,48},{64,5... | collective-permute-start | bytes 245768 | tf_op jit(solution)/shard_map/ppermute | solution.py:370
  7.5 67.1 %copy-start = (bf16[2,320,2560]{2,1,0:T(8,128)(2,1)S(1)}, bf16[2,320,2560]{2,1,0:T(8,128)(2,1)}, u32[]{:S(2)}) copy-start(bf16[2,320,2560]{2,1,0:T(8,128)(2,1)} %refs_3_.1) | copy-start | bytes 9830404
  37.9 1.4 %collective-permute-start.1 = (f32[8,48,128]{2,1,0:T(8,128)S(1)}, f32[8,48,128]{2,1,0:T(8,128)S(1)}, u32[]{:S(2)}, u32[]{:S(2)}) collective-permute-start(f32[8,48,128]{2,1,0:T(8,128)S(1)} %all_to_all.26.mine.whole), channel_id=1, source_target_pairs={{0,8},{8,0},{1,9},{9,1},{2,10},{10,2},{3,11},{11,3},{4,12},{12,4},... | collective-permute-start | bytes 589832 | tf_op jit(solution)/shard_map/ppermute | solution.py:395
  40.6 8.2 %collective-permute-start.2 = (f32[192,128]{1,0:T(8,128)S(1)}, f32[192,128]{1,0:T(8,128)S(1)}, u32[]{:S(2)}, u32[]{:S(2)}) collective-permute-start(f32[192,128]{1,0:T(8,128)S(1)} %get-tuple-element.32.mine), channel_id=1, source_target_pairs={{0,16},{16,32},{32,48},{48,0},{1,17},{17,33},{33,49},{49,1},{2,18}... | collective-permute-start | bytes 294920 | tf_op jit(solution)/shard_map/ppermute | solution.py:359
  40.7 8.1 %collective-permute-start.3 = (f32[192,128]{1,0:T(8,128)S(1)}, f32[192,128]{1,0:T(8,128)S(1)}, u32[]{:S(2)}, u32[]{:S(2)}) collective-permute-start(f32[192,128]{1,0:T(8,128)S(1)} %get-tuple-element.32.mine), channel_id=1, source_target_pairs={{0,32},{16,48},{32,0},{48,16},{1,33},{17,49},{33,1},{49,17},{2,34}... | collective-permute-start | bytes 294920 | tf_op jit(solution)/shard_map/ppermute | solution.py:359
  42.6 6.8 %collective-permute-start.4 = (f32[192,128]{1,0:T(8,128)S(1)}, f32[192,128]{1,0:T(8,128)S(1)}, u32[]{:S(2)}, u32[]{:S(2)}) collective-permute-start(f32[192,128]{1,0:T(8,128)S(1)} %get-tuple-element.32.mine), channel_id=1, source_target_pairs={{0,48},{16,0},{32,16},{48,32},{1,49},{17,1},{33,17},{49,33},{2,50}... | collective-permute-start | bytes 294920 | tf_op jit(solution)/shard_map/ppermute | solution.py:359
  50.6 7.3 %collective-permute-start.5 = (f32[192,128]{1,0:T(8,128)S(1)}, f32[192,128]{1,0:T(8,128)S(1)}, u32[]{:S(2)}, u32[]{:S(2)}) collective-permute-start(f32[192,128]{1,0:T(8,128)S(1)} %get-tuple-element.36.own), channel_id=1, source_target_pairs={{0,64},{64,128},{128,192},{192,0},{1,65},{65,129},{129,193},{193,1... | collective-permute-start | bytes 294920 | tf_op jit(solution)/shard_map/ppermute | solution.py:359
  50.7 7.2 %collective-permute-start.6 = (f32[192,128]{1,0:T(8,128)S(1)}, f32[192,128]{1,0:T(8,128)S(1)}, u32[]{:S(2)}, u32[]{:S(2)}) collective-permute-start(f32[192,128]{1,0:T(8,128)S(1)} %get-tuple-element.36.own), channel_id=1, source_target_pairs={{0,128},{64,192},{128,0},{192,64},{1,129},{65,193},{129,1},{193,65... | collective-permute-start | bytes 294920 | tf_op jit(solution)/shard_map/ppermute | solution.py:359
  53.2 5.2 %collective-permute-start.7 = (f32[192,128]{1,0:T(8,128)S(1)}, f32[192,128]{1,0:T(8,128)S(1)}, u32[]{:S(2)}, u32[]{:S(2)}) collective-permute-start(f32[192,128]{1,0:T(8,128)S(1)} %get-tuple-element.36.own), channel_id=1, source_target_pairs={{0,192},{64,0},{128,64},{192,128},{1,193},{65,1},{129,65},{193,129... | collective-permute-start | bytes 294920 | tf_op jit(solution)/shard_map/ppermute | solution.py:359
  60.0 7.0 %collective-permute-start.11 = (bf16[320,128]{1,0:T(8,128)(2,1)S(1)}, bf16[320,128]{1,0:T(8,128)(2,1)S(1)}, u32[]{:S(2)}, u32[]{:S(2)}) collective-permute-start(bf16[320,128]{1,0:T(8,128)(2,1)S(1)} %shard_map.61.refs_0_), channel_id=1, source_target_pairs={{0,7},{1,0},{2,1},{3,2},{4,3},{5,4},{6,5},{7,6},{8,15},{9,8},{10,9... | collective-permute-start | bytes 245768 | tf_op jit(solution)/shard_map/ppermute | solution.py:420
  61.5 6.0 %collective-permute-start.8 = (bf16[320,128]{1,0:T(8,128)(2,1)S(1)}, bf16[320,128]{1,0:T(8,128)(2,1)S(1)}, u32[]{:S(2)}, u32[]{:S(2)}) collective-permute-start(bf16[320,128]{1,0:T(8,128)(2,1)S(1)} %shard_map.61.refs_0_), channel_id=1, source_target_pairs={{0,1},{1,2},{2,3},{3,4},{4,5},{5,6},{6,7},{7,0},{8,9},{9,10},{10,1... | collective-permute-start | bytes 245768 | tf_op jit(solution)/shard_map/ppermute | solution.py:419
  62.1 8.9 %collective-permute-start.10 = (bf16[320,128]{1,0:T(8,128)(2,1)S(1)}, bf16[320,128]{1,0:T(8,128)(2,1)S(1)}, u32[]{:S(2)}, u32[]{:S(2)}) collective-permute-start(bf16[320,128]{1,0:T(8,128)(2,1)S(1)} %shard_map.61.refs_0_), channel_id=1, source_target_pairs={{0,4},{1,5},{2,6},{3,7},{4,0},{5,1},{6,2},{7,3},{8,12},{9,13},{10,... | collective-permute-start | bytes 245768 | tf_op jit(solution)/shard_map/ppermute | solution.py:421
  67.0 5.3 %collective-permute-start.12 = (bf16[320,128]{1,0:T(8,128)(2,1)S(1)}, bf16[320,128]{1,0:T(8,128)(2,1)S(1)}, u32[]{:S(2)}, u32[]{:S(2)}) collective-permute-start(bf16[320,128]{1,0:T(8,128)(2,1)S(1)} %collective-permute-done.11.refs_5_), channel_id=1, source_target_pairs={{0,7},{1,0},{2,1},{3,2},{4,3},{5,4},{6,5},{7,6},{8,15},{9,8},{10,9... | collective-permute-start | bytes 245768 | tf_op jit(solution)/shard_map/ppermute | solution.py:423
  67.5 5.1 %collective-permute-start.9 = (bf16[320,128]{1,0:T(8,128)(2,1)S(1)}, bf16[320,128]{1,0:T(8,128)(2,1)S(1)}, u32[]{:S(2)}, u32[]{:S(2)}) collective-permute-start(bf16[320,128]{1,0:T(8,128)(2,1)S(1)} %collective-permute-done.8.refs_1_), channel_id=1, source_target_pairs={{0,1},{1,2},{2,3},{3,4},{4,5},{5,6},{6,7},{7,0},{8,9},{9,10},{10,1... | collective-permute-start | bytes 245768 | tf_op jit(solution)/shard_map/ppermute | solution.py:422
  72.6 4.4 %collective-permute-start.13 = (bf16[320,128]{1,0:T(8,128)(2,1)S(1)}, bf16[320,128]{1,0:T(8,128)(2,1)S(1)}, u32[]{:S(2)}, u32[]{:S(2)}) collective-permute-start(bf16[320,128]{1,0:T(8,128)(2,1)S(1)} %collective-permute-done.9.refs_2_), channel_id=1, source_target_pairs={{0,1},{1,2},{2,3},{3,4},{4,5},{5,6},{6,7},{7,0},{8,9},{9,10},{10,1... | collective-permute-start | bytes 245768 | tf_op jit(solution)/shard_map/ppermute | solution.py:434
  73.4 4.4 %collective-permute-start.14 = (bf16[320,128]{1,0:T(8,128)(2,1)S(1)}, bf16[320,128]{1,0:T(8,128)(2,1)S(1)}, u32[]{:S(2)}, u32[]{:S(2)}) collective-permute-start(bf16[320,128]{1,0:T(8,128)(2,1)S(1)} %collective-permute-done.12.refs_4_), channel_id=1, source_target_pairs={{0,7},{1,0},{2,1},{3,2},{4,3},{5,4},{6,5},{7,6},{8,15},{9,8},{10,9... | collective-permute-start | bytes 245768 | tf_op jit(solution)/shard_map/ppermute | solution.py:435
